TPU v7x, 512 devices: a whole 4x8x8 slice. The times are simulated.
512 devices in a mesh: mem: 32 (over y, x), tile: 16 (over z, core).
Axes of the slice: x: 4, y: 8, z: 8, core: 2. Of those that a mesh axis runs over, the one named last changes fastest.
Arguments:
- latents: bfloat16 [64, 64, 8192], P('mem', 'tile'), may hold values from -3 to 3
- in_weight: bfloat16 [2, 576, 256], replicated, may hold values from -0.25 to 0.25
- out_weight: bfloat16 [2, 2304, 64], replicated, may hold values from -0.125 to 0.125
- observe_weight: bfloat16 [576, 8], replicated, may hold values from -0.25 to 0.25
- obs_cells: int32 [64, 32], P('tile'), may hold values from 0 to 127, all different within a row
- obs_values: float32 [64, 256], P('tile'), may hold values from -6 to 6
- obs_precision: float32 [64, 256], P('tile'), may hold values from 0.3 to 3
Outputs:
- analysis: float32 [64, 64, 8192], P('mem', 'tile')
- covariance: float32 [64, 64], replicated
Inputs may be any that keep to these rules, and one draw needn't show every extreme that they name: `obs_cells`: each row lists 32 different columns of the slab.
All inputs are finite; a program needn't handle non-finite values.
Results may differ from a plain program's by a relative error of at most 0.009.
Values may be sent and summed in bfloat16 or wider, within the bound.
No kernel may reach another device: no remote copies, remote signals or barrier semaphores. Data moves between devices by JAX's collectives and lax.ppermute only.
A program may use at most 64 MiB of HBM per device.

v0:
```python
import jax
import jax.numpy as jnp
from jax import lax
from jax.sharding import Mesh
from jax.sharding import PartitionSpec as P

COLS = 128
CH = 64
MEM = ("mem_0", "mem_1")


eps = 1e-06
guide_step = 0.5


def padded_2(x, sides, width):
    for axis, dim in sides:
        peers, length = (lax.axis_size(axis), x.shape[dim])
        up = [(i, (i + 1) % peers) for i in range(peers - 1)]
        down = [(j, i) for i, j in up]
        last = lax.slice_in_dim(x, length - width, length, axis=dim)
        initial = lax.slice_in_dim(x, 0, width, axis=dim)
        before = lax.ppermute(last, axis, up)
        after = lax.ppermute(initial, axis, down)
        x = jnp.concatenate([before, x, after], axis=dim)
    return x


def in_order(pieces, dim):
    shape = list(pieces.shape[1:])
    shape[dim] *= pieces.shape[0]
    return jnp.moveaxis(pieces, 0, dim).reshape(shape)


def sent_to_all(x, axis):
    peers = lax.axis_size(axis)
    return lax.all_to_all(jnp.broadcast_to(x[None], (peers, *x.shape)), axis, 0, 0, tiled=True)


def gathered_copies(x, axis, dim):
    return in_order(sent_to_all(x, axis), dim)


def over_copies(x, axis):
    return sent_to_all(x, axis).sum(axis=0)


def in_blocks(x, dim, peers):
    shape = x.shape
    pieces = x.reshape(*shape[:dim], peers, shape[dim] // peers, *shape[dim + 1 :])
    return jnp.moveaxis(pieces, dim, 0)


def exchange_in_order(pieces, axes, sequence):
    inside = pieces.shape[1:]
    result = pieces.reshape(*(lax.axis_size(a) for a in axes), *inside)
    for k in sequence:
        result = lax.all_to_all(result, axes[k], k, k, tiled=True)
    return result.reshape(-1, *inside)


def stepwise_exchange(x, axes, sequence, split_dim, concat_dim):
    pieces = in_blocks(x, split_dim, lax.axis_size(axes))
    return in_order(exchange_in_order(pieces, axes, sequence), concat_dim)


def rms_norm(values):
    return values * lax.rsqrt(jnp.mean(values * values, axis=-1, keepdims=True) + eps)


def pad_cols(values):
    return jnp.pad(values, ((0, 0), (0, 0), (1, 1), (0, 0)))


def conv_rows(padded, weight):
    row_count = padded.shape[1] - 2
    col_count = padded.shape[2] - 2
    in_ch = padded.shape[3]
    summed = None
    for row_tap in range(3):
        row_band = padded[:, row_tap : row_tap + row_count]
        col_patch = jnp.concatenate(
            [row_band[:, :, col_tap : col_tap + col_count] for col_tap in range(3)], axis=-1
        )
        part_sum = jnp.dot(
            col_patch,
            weight[row_tap * 3 * in_ch : (row_tap + 1) * 3 * in_ch],
            preferred_element_type=jnp.float32,
        )
        summed = part_sum if summed is None else summed + part_sum
    return summed


def res_block(current, first_weight, second_weight):
    member_count, row_count, flat_count = current.shape
    framed = padded_2(current, (("tile", 1),), 2).reshape(member_count, row_count + 4, COLS, CH)
    normed = rms_norm(framed.astype(jnp.float32)).astype(jnp.bfloat16)
    hidden = jax.nn.silu(conv_rows(pad_cols(normed), first_weight))
    row_ids = lax.broadcasted_iota(jnp.int32, (1, row_count + 2, 1, 1), 1)
    tile_pos = lax.axis_index("tile")
    last_tile = lax.axis_size("tile") - 1
    outside = (row_ids == 0) & (tile_pos == 0) | (row_ids == row_count + 1) & (
        tile_pos == last_tile
    )
    hidden = jnp.where(outside, 0.0, hidden).astype(jnp.bfloat16)
    update = conv_rows(pad_cols(hidden), second_weight)
    return (
        current.astype(jnp.float32) + update.reshape(member_count, row_count, flat_count)
    ).astype(jnp.bfloat16)


def observe_padded(padded, obs_cells, observe_weight):
    row_count = padded.shape[1] - 2
    patches = []
    for row_tap in range(3):
        row_band = padded[:, row_tap : row_tap + row_count]
        for col_tap in range(3):
            col_index = (obs_cells + col_tap)[None, :, :, None]
            patches.append(jnp.take_along_axis(row_band, col_index, axis=2))
    stacked = jnp.concatenate(patches, axis=-1)
    predicted = jnp.dot(stacked, observe_weight, preferred_element_type=jnp.float32)
    return predicted.reshape(predicted.shape[0], predicted.shape[1], -1)


def member_gram(members, values_here, precision_here):
    anomaly = members - jnp.mean(members, axis=0)
    innovation = values_here - members
    return jnp.einsum(
        "jrc,mrc->jm", anomaly * precision_here, innovation, precision=lax.Precision.HIGHEST
    )


def per_device(
    latents, in_weight, out_weight, observe_weight, obs_cells, obs_values, obs_precision
):
    member_count, row_count, flat_count = latents.shape
    current = latents
    for layer_idx in range(2):
        current = res_block(current, in_weight[layer_idx], out_weight[layer_idx])
    framed = padded_2(current, (("tile", 1),), 1).reshape(member_count, row_count + 2, COLS, CH)
    predicted = observe_padded(pad_cols(framed), obs_cells, observe_weight)
    total_count = row_count * lax.axis_size("tile") * predicted.shape[2]
    members = gathered_copies(predicted, MEM, 0)
    covariance = over_copies(member_gram(members, obs_values, obs_precision), "tile")
    covariance = covariance / total_count
    cov_high = covariance.astype(jnp.bfloat16)
    cov_low = (covariance - cov_high.astype(jnp.float32)).astype(jnp.bfloat16)
    col_totals = jnp.sum(covariance, axis=0)
    col_block = stepwise_exchange(current, MEM, (0, 1), 2, 0)
    moved = jnp.einsum("jrc,jm->mrc", col_block, cov_high, preferred_element_type=jnp.float32)
    moved = moved + jnp.einsum(
        "jrc,jm->mrc", col_block, cov_low, preferred_element_type=jnp.float32
    )
    center = jnp.mean(col_block.astype(jnp.float32), axis=0)
    moved = moved - col_totals[:, None, None] * center[None]
    fresh = col_block.astype(jnp.float32) + guide_step * moved
    analysis = lax.all_to_all(
        fresh.astype(jnp.bfloat16), MEM, split_axis=0, concat_axis=2, tiled=True
    ).astype(fresh.dtype)
    return (analysis, covariance)


def solution(mesh):
    split = Mesh(mesh.devices.reshape(8, 4, mesh.shape["tile"]), ("mem_0", "mem_1", "tile"))
    return jax.shard_map(
        per_device,
        mesh=split,
        in_specs=(
            P(MEM, "tile", None),
            P(),
            P(),
            P(),
            P("tile", None),
            P("tile", None),
            P("tile", None),
        ),
        out_specs=(P(MEM, "tile", None), P()),
        check_vma=False,
    )
```

profile of v0, /device:TPU:1, one launch (start us, length us, event | category | flops | bytes accessed | tf_op | source)
XLA Modules:
  0.0 131.7 jit_solution(9661298611138935118)
XLA Ops:
  0.6 1.1 fusion.136
  1.7 5.4 %collective-permute-start = (bf16[2,2,8192]{2,1,0:T(2,128)(2,1)S(1)}, bf16[2,2,8192]{2,1,0:T(2,128)(2,1)S(1)}, u32[]{:S(2)}, u32[]{:S(2)}) collective-permute-start(bf16[2,2,8192]{2,1,0:T(2,128)(2,1)S(1)} %get-tuple-element.50), channel_id=1, source_target_pairs={{0,1},{1,2},{2,3},{3,4},{4,5},{5,6},{6,7},{7,8},{8,9},{9,10},{10,1... | collective-permute-start | bytes 196616 | tf_op jit(solution)/shard_map/ppermute | solution.py:23
  7.1 4.7 %collective-permute-start.1 = (bf16[2,2,8192]{2,1,0:T(2,128)(2,1)S(1)}, bf16[2,2,8192]{2,1,0:T(2,128)(2,1)S(1)}, u32[]{:S(2)}, u32[]{:S(2)}) collective-permute-start(bf16[2,2,8192]{2,1,0:T(2,128)(2,1)S(1)} %get-tuple-element.51), channel_id=1, source_target_pairs={{1,0},{2,1},{3,2},{4,3},{5,4},{6,5},{7,6},{8,7},{9,8},{10,9},{11,1... | collective-permute-start | bytes 196616 | tf_op jit(solution)/shard_map/ppermute | solution.py:24
  11.8 0.9 collective-permute-done.1
  12.7 1.1 maximum_convert_fusion
  15.0 0.5 pad_slice_fusion.7
  15.5 0.5 copy-done.3
  16.9 0.7 select_convert_fusion.1
  17.6 0.8 pad_slice_fusion.19
  18.6 0.6 fusion
  19.2 0.6 fusion.48
  19.8 0.6 fusion.45
  21.5 1.9 %collective-permute-start.2 = (bf16[2,2,8192]{2,1,0:T(2,128)(2,1)S(1)}, bf16[2,2,8192]{2,1,0:T(2,128)(2,1)S(1)}, u32[]{:S(2)}, u32[]{:S(2)}) collective-permute-start(bf16[2,2,8192]{2,1,0:T(2,128)(2,1)S(1)} %get-tuple-element.48), channel_id=1, source_target_pairs={{0,1},{1,2},{2,3},{3,4},{4,5},{5,6},{6,7},{7,8},{8,9},{9,10},{10,1... | collective-permute-start | bytes 196616 | tf_op jit(solution)/shard_map/ppermute | solution.py:23
  23.5 2.4 %collective-permute-start.3 = (bf16[2,2,8192]{2,1,0:T(2,128)(2,1)S(1)}, bf16[2,2,8192]{2,1,0:T(2,128)(2,1)S(1)}, u32[]{:S(2)}, u32[]{:S(2)}) collective-permute-start(bf16[2,2,8192]{2,1,0:T(2,128)(2,1)S(1)} %get-tuple-element.49), channel_id=1, source_target_pairs={{1,0},{2,1},{3,2},{4,3},{5,4},{6,5},{7,6},{8,7},{9,8},{10,9},{11,1... | collective-permute-start | bytes 196616 | tf_op jit(solution)/shard_map/ppermute | solution.py:24
  25.9 3.9 %collective-permute-done.3 = bf16[2,2,8192]{2,1,0:T(2,128)(2,1)S(1)} collective-permute-done((bf16[2,2,8192]{2,1,0:T(2,128)(2,1)S(1)}, bf16[2,2,8192]{2,1,0:T(2,128)(2,1)S(1)}, u32[]{:S(2)}, u32[]{:S(2)}) %collective-permute-start.3) | collective-permute-done | bytes 65568 | tf_op jit(solution)/shard_map/ppermute | solution.py:24
  31.2 0.5 pad_slice_fusion.1
  32.5 0.7 select_convert_fusion
  33.2 0.8 pad_slice_fusion.13
  34.0 0.6 fusion.18
  34.6 0.6 fusion.42
  35.2 0.6 fusion.39
  36.4 1.9 %collective-permute-start.4 = (bf16[2,1,8192]{2,1,0:T(2,128)(2,1)S(1)}, bf16[2,1,8192]{2,1,0:T(2,128)(2,1)S(1)}, u32[]{:S(2)}, u32[]{:S(2)}) collective-permute-start(bf16[2,1,8192]{2,1,0:T(2,128)(2,1)S(1)} %get-tuple-element.46), channel_id=1, source_target_pairs={{0,1},{1,2},{2,3},{3,4},{4,5},{5,6},{6,7},{7,8},{8,9},{9,10},{10,1... | collective-permute-start | bytes 98312 | tf_op jit(solution)/shard_map/ppermute | solution.py:23
  38.4 2.4 %collective-permute-start.5 = (bf16[2,1,8192]{2,1,0:T(2,128)(2,1)S(1)}, bf16[2,1,8192]{2,1,0:T(2,128)(2,1)S(1)}, u32[]{:S(2)}, u32[]{:S(2)}) collective-permute-start(bf16[2,1,8192]{2,1,0:T(2,128)(2,1)S(1)} %get-tuple-element.47), channel_id=1, source_target_pairs={{1,0},{2,1},{3,2},{4,3},{5,4},{6,5},{7,6},{8,7},{9,8},{10,9},{11,1... | collective-permute-start | bytes 98312 | tf_op jit(solution)/shard_map/ppermute | solution.py:24
  41.1 0.8 copy.90
  41.9 6.8 %all-to-all-start = ((bf16[8,4,2,4,256]{4,2,1,3,0:T(2,128)(2,1)}), bf16[8,4,2,4,256]{4,2,1,3,0:T(2,128)(2,1)S(1)}, u32[]{:S(2)}, u32[]{:S(2)}) async-start(bf16[8,4,2,4,256]{4,2,1,3,0:T(2,128)(2,1)} %copy.90), calls=%async_computation | async-start | bytes 262144 | tf_op jit(solution)/shard_map/all_to_all | solution.py:58
  49.7 0.6 pad_slice_fusion.24
  50.3 0.9 gather_fusion.1
  51.2 0.9 gather_fusion.2
  52.1 0.9 gather_fusion.4
  52.9 0.9 gather_fusion.5
  53.8 0.9 gather_fusion.7
  54.7 0.9 gather_fusion.8
  55.6 0.9 gather_fusion
  56.5 0.9 gather_fusion.3
  57.3 0.9 gather_fusion.6
  59.2 0.8 broadcast_in_dim.63
  60.0 9.5 %all-to-all-start.2 = ((f32[32,2,4,256]{3,1,2,0:T(2,128)}), f32[32,2,4,256]{3,1,2,0:T(2,128)S(1)}, u32[]{:S(2)}, u32[]{:S(2)}) async-start(f32[32,2,4,256]{3,1,2,0:T(2,128)} %broadcast_in_dim.63), calls=%async_computation.2 | async-start | bytes 524288 | tf_op jit(solution)/shard_map/all_to_all | solution.py:37
  69.5 0.8 copy.91
  70.3 11.4 %all-to-all-done.2 = f32[32,2,4,256]{3,1,2,0:T(2,128)S(1)} async-done(((f32[32,2,4,256]{3,1,2,0:T(2,128)}), f32[32,2,4,256]{3,1,2,0:T(2,128)S(1)}, u32[]{:S(2)}, u32[]{:S(2)}) %all-to-all-start.2) | async-done | bytes 262176 | tf_op jit(solution)/shard_map/all_to_all | solution.py:37
  81.6 3.3 %all-to-all-start.1 = ((bf16[8,4,2,4,256]{4,2,0,3,1:T(2,128)(2,1)}), bf16[8,4,2,4,256]{4,2,0,3,1:T(2,128)(2,1)S(1)}, u32[]{:S(2)}, u32[]{:S(2)}) async-start(bf16[8,4,2,4,256]{4,2,0,3,1:T(2,128)(2,1)} %copy.91), calls=%async_computation.1 | async-start | bytes 262144 | tf_op jit(solution)/shard_map/all_to_all | solution.py:58
  85.7 1.0 reshape.283
  86.7 3.0 %all-to-all-done.1 = bf16[8,4,2,4,256]{4,2,0,3,1:T(2,128)(2,1)S(1)} async-done(((bf16[8,4,2,4,256]{4,2,0,3,1:T(2,128)(2,1)}), bf16[8,4,2,4,256]{4,2,0,3,1:T(2,128)(2,1)S(1)}, u32[]{:S(2)}, u32[]{:S(2)}) %all-to-all-start.1) | async-done | bytes 131104 | tf_op jit(solution)/shard_map/all_to_all | solution.py:58
  89.7 13.8 %all-to-all-start.3 = ((f32[16,1,4096]{2,1,0:T(1,128)}), f32[16,1,4096]{2,1,0:T(1,128)S(1)}, u32[]{:S(2)}, u32[]{:S(2)}) async-start(f32[16,1,4096]{2,1,0:T(1,128)} %reshape.283), calls=%async_computation.3 | async-start | bytes 524288 | tf_op jit(solution)/shard_map/all_to_all | solution.py:37
  103.8 11.3 %all-to-all-done.3 = f32[16,1,4096]{2,1,0:T(1,128)S(1)} async-done(((f32[16,1,4096]{2,1,0:T(1,128)}), f32[16,1,4096]{2,1,0:T(1,128)S(1)}, u32[]{:S(2)}, u32[]{:S(2)}) %all-to-all-start.3) | async-done | bytes 262176 | tf_op jit(solution)/shard_map/all_to_all | solution.py:37
  115.1 0.5 broadcast.426
  115.6 1.3 reduce.2
  117.8 13.1 %all_to_all.29 = bf16[64,4,256]{2,1,0:T(4,128)(2,1)S(1)} all-to-all(bf16[64,4,256]{2,1,0:T(4,128)(2,1)S(1)} %copy.111), channel_id=1, replica_groups=mesh['mem_0'=8,'mem_1'=4,'tile'=16] {'mem_0','mem_1'}, dimensions={0} | all-to-all | bytes 262144 | tf_op jit(solution)/shard_map/all_to_all | solution.py:157
  130.9 0.7 copy.134
  (85 shorter events, 10.1 us)
Async XLA Ops:
  0.6 58.2 %copy-start = (bf16[576,8]{0,1:T(8,128)(2,1)S(1)}, bf16[576,8]{0,1:T(8,128)(2,1)}, u32[]{:S(2)}) copy-start(bf16[576,8]{0,1:T(8,128)(2,1)} %param.12) | copy-start | bytes 27652
  1.7 10.1 %collective-permute-start = (bf16[2,2,8192]{2,1,0:T(2,128)(2,1)S(1)}, bf16[2,2,8192]{2,1,0:T(2,128)(2,1)S(1)}, u32[]{:S(2)}, u32[]{:S(2)}) collective-permute-start(bf16[2,2,8192]{2,1,0:T(2,128)(2,1)S(1)} %get-tuple-element.50), channel_id=1, source_target_pairs={{0,1},{1,2},{2,3},{3,4},{4,5},{5,6},{6,7},{7,8},{8,9},{9,10},{10,1... | collective-permute-start | bytes 196616 | tf_op jit(solution)/shard_map/ppermute | solution.py:23
  7.1 5.6 %collective-permute-start.1 = (bf16[2,2,8192]{2,1,0:T(2,128)(2,1)S(1)}, bf16[2,2,8192]{2,1,0:T(2,128)(2,1)S(1)}, u32[]{:S(2)}, u32[]{:S(2)}) collective-permute-start(bf16[2,2,8192]{2,1,0:T(2,128)(2,1)S(1)} %get-tuple-element.51), channel_id=1, source_target_pairs={{1,0},{2,1},{3,2},{4,3},{5,4},{6,5},{7,6},{8,7},{9,8},{10,9},{11,1... | collective-permute-start | bytes 196616 | tf_op jit(solution)/shard_map/ppermute | solution.py:24
  14.9 1.1 copy-start.3
  17.6 1.1 copy-start.7
  20.4 0.9 copy-start.1
  20.5 5.4 %copy-start.4 = (s32[4,32]{1,0:T(4,128)S(1)}, s32[4,32]{1,0:T(4,128)}, u32[]{:S(2)}) copy-start(s32[4,32]{1,0:T(4,128)} %param.13) | copy-start | bytes 1540
  21.5 4.4 %collective-permute-start.2 = (bf16[2,2,8192]{2,1,0:T(2,128)(2,1)S(1)}, bf16[2,2,8192]{2,1,0:T(2,128)(2,1)S(1)}, u32[]{:S(2)}, u32[]{:S(2)}) collective-permute-start(bf16[2,2,8192]{2,1,0:T(2,128)(2,1)S(1)} %get-tuple-element.48), channel_id=1, source_target_pairs={{0,1},{1,2},{2,3},{3,4},{4,5},{5,6},{6,7},{7,8},{8,9},{9,10},{10,1... | collective-permute-start | bytes 196616 | tf_op jit(solution)/shard_map/ppermute | solution.py:23
  23.5 6.3 %collective-permute-start.3 = (bf16[2,2,8192]{2,1,0:T(2,128)(2,1)S(1)}, bf16[2,2,8192]{2,1,0:T(2,128)(2,1)S(1)}, u32[]{:S(2)}, u32[]{:S(2)}) collective-permute-start(bf16[2,2,8192]{2,1,0:T(2,128)(2,1)S(1)} %get-tuple-element.49), channel_id=1, source_target_pairs={{1,0},{2,1},{3,2},{4,3},{5,4},{6,5},{7,6},{8,7},{9,8},{10,9},{11,1... | collective-permute-start | bytes 196616 | tf_op jit(solution)/shard_map/ppermute | solution.py:24
  36.4 12.2 %collective-permute-start.4 = (bf16[2,1,8192]{2,1,0:T(2,128)(2,1)S(1)}, bf16[2,1,8192]{2,1,0:T(2,128)(2,1)S(1)}, u32[]{:S(2)}, u32[]{:S(2)}) collective-permute-start(bf16[2,1,8192]{2,1,0:T(2,128)(2,1)S(1)} %get-tuple-element.46), channel_id=1, source_target_pairs={{0,1},{1,2},{2,3},{3,4},{4,5},{5,6},{6,7},{7,8},{8,9},{9,10},{10,1... | collective-permute-start | bytes 98312 | tf_op jit(solution)/shard_map/ppermute | solution.py:23
  38.4 10.3 %collective-permute-start.5 = (bf16[2,1,8192]{2,1,0:T(2,128)(2,1)S(1)}, bf16[2,1,8192]{2,1,0:T(2,128)(2,1)S(1)}, u32[]{:S(2)}, u32[]{:S(2)}) collective-permute-start(bf16[2,1,8192]{2,1,0:T(2,128)(2,1)S(1)} %get-tuple-element.47), channel_id=1, source_target_pairs={{1,0},{2,1},{3,2},{4,3},{5,4},{6,5},{7,6},{8,7},{9,8},{10,9},{11,1... | collective-permute-start | bytes 98312 | tf_op jit(solution)/shard_map/ppermute | solution.py:24
  41.9 17.4 %all-to-all-start = ((bf16[8,4,2,4,256]{4,2,1,3,0:T(2,128)(2,1)}), bf16[8,4,2,4,256]{4,2,1,3,0:T(2,128)(2,1)S(1)}, u32[]{:S(2)}, u32[]{:S(2)}) async-start(bf16[8,4,2,4,256]{4,2,1,3,0:T(2,128)(2,1)} %copy.90), calls=%async_computation | async-start | bytes 262144 | tf_op jit(solution)/shard_map/all_to_all | solution.py:58
  58.9 26.3 %copy-start.5 = (f32[4,256]{1,0:T(4,128)S(1)}, f32[4,256]{1,0:T(4,128)}, u32[]{:S(2)}) copy-start(f32[4,256]{1,0:T(4,128)} %param.15) | copy-start | bytes 12292
  58.9 26.3 %copy-start.6 = (f32[4,256]{1,0:T(4,128)S(1)}, f32[4,256]{1,0:T(4,128)}, u32[]{:S(2)}) copy-start(f32[4,256]{1,0:T(4,128)} %param.14) | copy-start | bytes 12292
  60.0 21.6 %all-to-all-start.2 = ((f32[32,2,4,256]{3,1,2,0:T(2,128)}), f32[32,2,4,256]{3,1,2,0:T(2,128)S(1)}, u32[]{:S(2)}, u32[]{:S(2)}) async-start(f32[32,2,4,256]{3,1,2,0:T(2,128)} %broadcast_in_dim.63), calls=%async_computation.2 | async-start | bytes 524288 | tf_op jit(solution)/shard_map/all_to_all | solution.py:37
  81.6 8.1 %all-to-all-start.1 = ((bf16[8,4,2,4,256]{4,2,0,3,1:T(2,128)(2,1)}), bf16[8,4,2,4,256]{4,2,0,3,1:T(2,128)(2,1)S(1)}, u32[]{:S(2)}, u32[]{:S(2)}) async-start(bf16[8,4,2,4,256]{4,2,0,3,1:T(2,128)(2,1)} %copy.91), calls=%async_computation.1 | async-start | bytes 262144 | tf_op jit(solution)/shard_map/all_to_all | solution.py:58
  89.7 25.4 %all-to-all-start.3 = ((f32[16,1,4096]{2,1,0:T(1,128)}), f32[16,1,4096]{2,1,0:T(1,128)S(1)}, u32[]{:S(2)}, u32[]{:S(2)}) async-start(f32[16,1,4096]{2,1,0:T(1,128)} %reshape.283), calls=%async_computation.3 | async-start | bytes 524288 | tf_op jit(solution)/shard_map/all_to_all | solution.py:37
  117.2 14.4 %copy-start.2 = (f32[64,64]{1,0:T(8,128)}, f32[64,64]{1,0:T(8,128)S(1)}, u32[]{:S(2)}) copy-start(f32[64,64]{1,0:T(8,128)S(1)} %get-tuple-element.4) | copy-start | bytes 49156
where the time goes:
time: 132 us
  starting transfers between devices  52.1 us (39%)
  waiting for transfers between devices  30.4 us (23%)
  local copies, waits for them, and re-layouts  22.5 us (17%)
  blocking collectives  13.1 us (10%)
  matrix products  7.74 us (6%)
  other arithmetic  4.42 us (3%)
    all_to_all x2, starting transfers between devices, sent_to_all(): lax.all_to_all(jnp.broadcast_to(x[None], (peers, *x.shape)), axis, 0, 0,...  23.3 us
    all_to_all x2, waiting for transfers between devices, sent_to_all(): lax.all_to_all(jnp.broadcast_to(x[None], (peers, *x.shape)), axis, 0, 0,...  22.6 us
    all_to_all x1, blocking collectives, per_device(): lax.all_to_all(fresh.astype(jnp.bfloat16), MEM, split_axis=0, concat_axis...  13.1 us
    all_to_all x2, starting transfers between devices, exchange_in_order(): result = lax.all_to_all(result, axes[k], k, k, tiled=True)  10.1 us
    ppermute x3, starting transfers between devices, padded_2(): after = lax.ppermute(initial, axis, down)  9.47 us
    ppermute x3, starting transfers between devices, padded_2(): before = lax.ppermute(last, axis, up)  9.22 us
    gather x21, local copies, waits for them, and re-layouts, observe_padded(): patches.append(jnp.take_along_axis(row_band, col_index, axis=2))  8.26 us
    dot_general x12, matrix products, conv_rows(): jnp.dot(col_patch, weight[row_tap * 3 * in_ch:(row_tap + 1) * 3 * in_ch],...  6.7 us
  transfers between devices with their start and end apart: 10, of which 5 were waited for; matrix products, arithmetic and copies ran while one was open for 11% of the time, Pallas kernels for 0%

commit v1 on v0

v1 whole, which is shorter than its diff:
```python
import functools

import jax
import jax.numpy as jnp
from jax import lax
from jax.experimental import pallas as pl
from jax.experimental.pallas import tpu as pltpu
from jax.sharding import Mesh
from jax.sharding import PartitionSpec as P

MEM = ("y", "x")
TILE = ("z", "c")
PAIRS = 64
HID = 256
PEERS = 32
EPS = 1e-06
STEP = 0.5
F32 = jnp.float32
BF16 = jnp.bfloat16
LIMIT = 24 * 1024 * 1024
NT = (((1,), (1,)), ((), ()))
TN = (((0,), (0,)), ((), ()))
BLOCKS = (0, 1, 2, -1)


def kernel_call(body, outs, scratch=(), flops=0, moved=0, limit=LIMIT):
    return pl.pallas_call(
        body,
        out_shape=outs,
        scratch_shapes=scratch,
        cost_estimate=pl.CostEstimate(flops=flops, bytes_accessed=moved, transcendentals=0),
        compiler_params=pltpu.CompilerParams(vmem_limit_bytes=limit),
    )


def shaped(shape, dtype=BF16):
    return jax.ShapeDtypeStruct(shape, dtype)


def rows_kernel(x_ref, rows_ref, inner_ref, outer_ref, flat):
    upper = lax.axis_index("c") == 1
    for m in range(2):
        for t in range(PAIRS):
            flat[256 * m + 4 * t : 256 * m + 4 * t + 4, :] = x_ref[m, :, 128 * t : 128 * t + 128].astype(F32)
    for m in range(2):
        rows = [flat[pl.ds(256 * m + r, PAIRS, stride=4), :] for r in range(4)]
        for r in range(4):
            rows_ref[m, r] = rows[r].astype(BF16)
        inner_ref[m] = jnp.where(upper, rows[3], rows[0]).astype(BF16)
        outer_ref[m] = jnp.where(upper, rows[0], rows[3]).astype(BF16)


def weights_kernel(in_ref, out_ref, first_ref, second_ref):
    first_ref[...] = jnp.zeros_like(first_ref)
    second_ref[...] = jnp.zeros_like(second_ref)
    for layer in range(2):
        for dr in range(3):
            for b, j in enumerate(BLOCKS):
                for h in range(2):
                    dc = j - h + 1
                    if 0 <= dc <= 2:
                        at = 64 * (3 * dr + dc)
                        first_ref[layer, 256 * dr + 64 * b : 256 * dr + 64 * b + 64, 256 * h : 256 * h + 256] = (
                            in_ref[layer, at : at + 64, :] * jnp.asarray(0.5, BF16)
                        )
                    dc = h - j + 1
                    if 0 <= dc <= 2:
                        at = 256 * (3 * dr + dc)
                        second_ref[layer, 64 * b : 64 * b + 64, 512 * dr + 256 * h : 512 * dr + 256 * h + 256] = (
                            out_ref[layer, :, at : at + 256]
                        )


def beside(values, lower):
    at = lax.broadcasted_iota(jnp.int32, values.shape, 1)
    after = jnp.where(at == PAIRS - 1, 0.0, pltpu.roll(values, PAIRS - 1, 1))
    before = jnp.where(at == 0, 0.0, pltpu.roll(values, 1, 1))
    return jnp.where(lower, after, before), jnp.where(lower, before, after)


def patches(a_ref, m, row, count, values, ones, norm):
    wide = values.astype(F32)
    lower = lax.broadcasted_iota(jnp.int32, wide.shape, 2) < 64
    if norm:
        square = (values * values).reshape(count * PAIRS, 128)
        mean = jnp.dot(square, ones, preferred_element_type=F32).reshape(count, PAIRS, 128)
        wide = wide * lax.rsqrt(mean + EPS)
    a_ref[m, pl.ds(row, count), :, 0:128] = wide.astype(BF16)
    a_ref[m, pl.ds(row, count), :, 128:256] = beside(wide, lower)[0].astype(BF16)


def denoise_kernel(chip_ref, outer_ref, inner_row, outer_row, w1_ref, w2_ref, obs_ref, cells_ref, pay_ref,
                   x_ref, a_ref, h_ref, flat):
    c = lax.axis_index("c")
    tile = 2 * lax.axis_index("z") + c
    ones = jnp.where(
        (lax.broadcasted_iota(jnp.int32, (128, 128), 0) < 64) == (lax.broadcasted_iota(jnp.int32, (128, 128), 1) < 64),
        1.0 / 64, 0.0,
    ).astype(BF16)
    for m in range(2):
        x_ref[m, 13 - 13 * c] = inner_row[m]
        x_ref[m, 13 * c] = outer_row[m]
        x_ref[m, pl.ds(1 + 8 * c, 4)] = outer_ref[m]
        for k in range(2):
            x_ref[m, pl.ds(5 - 4 * c + 4 * k, 4)] = chip_ref[k, m]

    def clear(ref, low, high, size):
        @pl.when(tile == 0)
        def _():
            for m in range(2):
                ref[m, 0:low] = jnp.zeros((low, *ref.shape[2:]), ref.dtype)

        @pl.when(tile == 15)
        def _():
            for m in range(2):
                ref[m, high:size] = jnp.zeros((size - high, *ref.shape[2:]), ref.dtype)

    for layer, (size, step1, step2) in enumerate(((14, 4, 5), (10, 4, 3))):
        half = size // 2
        for m in range(2):
            for row in (0, half):
                patches(a_ref, m, row, half, x_ref[m, row : row + half], ones, True)
        hidden = size - 2
        for m in range(2):
            for row in range(0, hidden, step1):
                left = jnp.concatenate(
                    [a_ref[m, row + dr : row + dr + step1].reshape(step1 * PAIRS, 256) for dr in range(3)], axis=1
                )
                v = jnp.dot(left, w1_ref[layer], preferred_element_type=F32)
                v = v + v * jnp.tanh(v)
                h_ref[m, row : row + step1] = v.astype(BF16).reshape(step1, PAIRS, 512)
        edge = 4 - 2 * layer
        clear(h_ref, edge, hidden - edge, hidden)
        kept = size - 4
        for m in range(2):
            for row in range(0, kept, step2):
                left = jnp.concatenate(
                    [h_ref[m, row + dr : row + dr + step2].reshape(step2 * PAIRS, 512) for dr in range(3)], axis=1
                )
                y = lax.dot_general(left, w2_ref[layer], NT, preferred_element_type=F32)
                own = y[:, 0:128].reshape(step2, PAIRS, 128)
                side = y[:, 128:256].reshape(step2, PAIRS, 128)
                lower = lax.broadcasted_iota(jnp.int32, side.shape, 2) < 64
                total = x_ref[m, row + 2 : row + 2 + step2].astype(F32) + own + beside(side, lower)[1]
                x_ref[m, row : row + step2] = total.astype(BF16)
        clear(x_ref, 3 - 2 * layer, kept - 3 + 2 * layer, kept)

    cell = cells_ref[...]
    pair = lax.shift_right_logical(cell, 1)
    lane_row = lax.broadcasted_iota(jnp.int32, (1, 128), 1) // 32
    index = lax.broadcasted_iota(jnp.int32, (384, 128), 0)
    pick = jnp.concatenate(
        [jnp.where(index == (lane_row + dr) * PAIRS + pair, 1.0, 0.0).astype(BF16) for dr in range(3)], axis=0
    )
    parts = []
    for m in range(2):
        patches(a_ref, m, 0, 6, x_ref[m, 0:6], ones, False)
        y = lax.dot_general(obs_ref[...], a_ref[m, 0:6].reshape(384, 256), NT, preferred_element_type=F32)
        y = jnp.concatenate([y[16 * dr : 16 * dr + 16] for dr in range(3)], axis=1)
        high = y.astype(BF16).astype(F32)
        parts += [high, y - high]
    seen = jnp.dot(jnp.concatenate(parts, axis=0).astype(BF16), pick, preferred_element_type=F32)
    odd = jnp.broadcast_to((cell & 1) == 1, (8, 128))
    got = [jnp.where(odd, seen[16 * i + 8 : 16 * i + 16], seen[16 * i : 16 * i + 8]) for i in range(4)]
    high = jnp.concatenate([got[0], got[2]], axis=0).astype(BF16)
    low = jnp.concatenate([got[1], got[3]], axis=0).astype(BF16)
    for m in range(2):
        for r in range(4):
            flat[pl.ds(256 * m + r, PAIRS, stride=4), :] = x_ref[m, 1 + r].astype(F32)
    for p in range(PEERS):
        both = jnp.concatenate([flat[8 * p : 8 * p + 8], flat[256 + 8 * p : 256 + 8 * p + 8]], axis=0)
        pay_ref[p, 0:16] = both.astype(BF16)
        pay_ref[p, 16:32] = high
        pay_ref[p, 32:48] = low


def gram_kernel(got_ref, values_ref, precision_ref, out_ref, flat):
    for p in range(PEERS):
        flat[16 * p : 16 * p + 16] = got_ref[p, 16:32].astype(F32) + got_ref[p, 32:48].astype(F32)
    shape = (64, 128)
    left, right = [], []
    for o in range(8):
        members = flat[pl.ds(o, 64, stride=8), :]
        mean = jnp.sum(members, axis=0, keepdims=True) * (1.0 / 64)
        left.append((members - mean) * jnp.broadcast_to(precision_ref[o : o + 1], shape))
        right.append(jnp.broadcast_to(values_ref[o : o + 1], shape) - members)
    left = jnp.concatenate(left, axis=1)
    right = jnp.concatenate(right, axis=1)
    none = jnp.zeros_like(right)
    total = lax.dot_general(
        left[0:32], jnp.concatenate([right, none], axis=0), NT, precision=lax.Precision.HIGHEST,
        preferred_element_type=F32,
    ) + lax.dot_general(
        left[32:64], jnp.concatenate([none, right], axis=0), NT, precision=lax.Precision.HIGHEST,
        preferred_element_type=F32,
    )
    for t in range(16):
        out_ref[t] = total


def update_kernel(got_ref, parts_ref, covariance_ref, back_ref, flat):
    total = parts_ref[0]
    for t in range(1, 16):
        total = total + parts_ref[t]
    total = total * (1.0 / 16384)
    covariance = jnp.concatenate([total[:, 0:64], total[:, 64:128]], axis=0)
    covariance_ref[...] = covariance
    center = (covariance - jnp.mean(covariance, axis=0, keepdims=True)) * STEP
    high = center.astype(BF16)
    both = jnp.concatenate([high, (center - high.astype(F32)).astype(BF16)], axis=0)
    for p in range(PEERS):
        flat[16 * p : 16 * p + 16] = got_ref[p, 0:16].astype(F32)
    for s in range(8):
        members = flat[pl.ds(s, 64, stride=8), :]
        narrow = members.astype(BF16)
        moved = lax.dot_general(both, jnp.concatenate([narrow, narrow], axis=0), TN, preferred_element_type=F32)
        flat[pl.ds(s, 64, stride=8), :] = members + moved
    for p in range(PEERS):
        back_ref[p] = flat[16 * p : 16 * p + 16].astype(BF16)


def final_kernel(got_ref, out_ref):
    for p in range(PEERS):
        values = got_ref[p].astype(F32)
        for m in range(2):
            for t in range(2):
                at = 128 * (2 * p + t)
                out_ref[m, :, at : at + 128] = values[8 * m + 4 * t : 8 * m + 4 * t + 4]


def observed_weights(weight):
    taps = jnp.transpose(weight.reshape(3, 3, 64, 8), (0, 1, 3, 2))
    none = jnp.zeros_like(taps[:, 0])
    sides = []
    for h in range(2):
        sides.append(jnp.concatenate([taps[:, j - h + 1] if 0 <= j - h + 1 <= 2 else none for j in BLOCKS], axis=-1))
    return jnp.stack(sides, axis=1).reshape(48, 256)


def exchange_pairs():
    across, inner, outer = [], [], []
    for z in range(7):
        across += [(2 * z + 1, 2 * z + 2), (2 * z + 2, 2 * z + 1)]
        inner += [(2 * z + 1, 2 * z + 3), (2 * z + 2, 2 * z)]
        outer += [(2 * z, 2 * z + 2), (2 * z + 3, 2 * z + 1)]
    return across, inner, outer


def per_device(latents, in_weight, out_weight, observe_weight, obs_cells, obs_values, obs_precision):
    across, inner, outer = exchange_pairs()
    rows, inner_row, outer_row = kernel_call(
        rows_kernel,
        (shaped((2, 4, PAIRS, 128)), shaped((2, PAIRS, 128)), shaped((2, PAIRS, 128))),
        [pltpu.VMEM((512, 128), F32)], moved=300_000,
    )(latents)
    outer_tile = lax.ppermute(rows, TILE, across)
    outer_row = lax.ppermute(outer_row, TILE, outer)
    inner_row = lax.ppermute(inner_row, TILE, inner)
    chip = lax.all_gather(rows, "c")
    first, second = kernel_call(
        weights_kernel, (shaped((2, 768, 512)), shaped((2, 256, 1536))), moved=4_300_000,
    )(in_weight, jnp.transpose(out_weight, (0, 2, 1)))
    pay = kernel_call(
        denoise_kernel,
        shaped((PEERS, 48, 128)),
        [
            pltpu.VMEM((2, 14, PAIRS, 128), BF16),
            pltpu.VMEM((2, 14, PAIRS, 256), BF16),
            pltpu.VMEM((2, 12, PAIRS, 512), BF16),
            pltpu.VMEM((512, 128), F32),
        ],
        flops=4_000_000_000, moved=4_300_000, limit=40 * 1024 * 1024,
    )(chip, outer_tile, inner_row, outer_row, first, second, observed_weights(observe_weight),
      obs_cells.reshape(1, 128))
    got = lax.all_to_all(pay, MEM, 0, 0, tiled=True)

    def by_channel(values):
        return jnp.transpose(values.reshape(4, 32, 8), (2, 0, 1)).reshape(8, 128)

    parts = kernel_call(
        gram_kernel, shaped((16, 32, 128), F32), [pltpu.VMEM((512, 128), F32)], moved=700_000,
    )(got, by_channel(obs_values), by_channel(obs_precision))
    parts = lax.all_to_all(parts, TILE, 0, 0, tiled=True)
    covariance, back = kernel_call(
        update_kernel, (shaped((64, 64), F32), shaped((PEERS, 16, 128))), [pltpu.VMEM((512, 128), F32)],
        moved=700_000,
    )(got, parts)
    back = lax.all_to_all(back, MEM, 0, 0, tiled=True)
    analysis = kernel_call(final_kernel, shaped((2, 4, 8192), F32), moved=400_000)(back)
    return analysis, covariance


def solution(mesh):
    split = Mesh(mesh.devices.reshape(8, 4, 8, 2), ("y", "x", "z", "c"))
    return jax.shard_map(
        per_device,
        mesh=split,
        in_specs=(P(MEM, TILE, None), P(), P(), P(), P(TILE, None), P(TILE, None), P(TILE, None)),
        out_specs=(P(MEM, TILE, None), P()),
        check_vma=False,
    )
```

time: 132 us -> 89.5 us (0.68)
  starting transfers between devices: 52.1 us -> 18 us
  blocking collectives: 13.1 us -> 42 us
  local copies, waits for them, and re-layouts: 22.5 us -> 4.93 us
  waiting for transfers between devices: 30.4 us -> 13.9 us
  Pallas kernels: 0 us -> 9.2 us
  matrix products: 7.74 us -> 0 us
  other arithmetic: 4.42 us -> 0.09 us
    all_to_all x4 -> x1, starting transfers between devices: 33.4 us -> 7.36 us  [per_device(): got = lax.all_to_all(pay, MEM, 0, 0, tiled=True)]
    all_to_all x1 -> x2, blocking collectives: 13.1 us -> 37.7 us  [the longest x1 24 us: per_device(): parts = lax.all_to_all(parts, TILE, 0, 0, tiled=True)]
    all_to_all x4 -> x1, waiting for transfers between devices: 25.7 us -> 13.9 us  [per_device(): got = lax.all_to_all(pay, MEM, 0, 0, tiled=True)]
    pallas_call x0 -> x6, Pallas kernels: none -> 9.2 us  [the longest x1 6.69 us: per_device(): kernel_call(denoise_kernel, shaped((PEERS, 48, 128)), [pltpu.VMEM((2, 14,...]
    gather x21 -> x0, local copies, waits for them, and re-layouts: 8.26 us -> none  [observe_padded(): patches.append(jnp.take_along_axis(row_band, col_index, axis=2))]
    ppermute x6 -> x3, starting transfers between devices: 18.7 us -> 10.7 us  [the longest x1 5.38 us: per_device(): outer_tile = lax.ppermute(rows, TILE, across)]
    dot_general x16 -> x0, matrix products: 7.74 us -> none  [the longest x12 6.7 us: conv_rows(): jnp.dot(col_patch, weight[row_tap * 3 * in_ch:(row_tap + 1) * 3 * in_ch],...]
    ppermute x6 -> x3, waiting for transfers between devices: 4.77 us -> 0.01 us  [the longest x1 0.01 us: per_device(): outer_row = lax.ppermute(outer_row, TILE, outer)]
  transfers between devices with their start and end apart: 10 -> 4, of which waited for: 5 -> 1; matrix products, arithmetic and copies ran while one was open for 11% -> 2% of each run, Pallas kernels for 0% -> 0%
where the time goes in v1:
time: 89.5 us; the launch traced here: 89 us
  blocking collectives  42 us (47%)
  starting transfers between devices  18 us (20%)
  waiting for transfers between devices  13.9 us (16%)
  Pallas kernels  9.2 us (10%)
  local copies, waits for them, and re-layouts  4.93 us (6%)
    all_to_all x1, blocking collectives, per_device(): parts = lax.all_to_all(parts, TILE, 0, 0, tiled=True)  24 us
    all_to_all x1, waiting for transfers between devices, per_device(): got = lax.all_to_all(pay, MEM, 0, 0, tiled=True)  13.9 us
    all_to_all x1, blocking collectives, per_device(): back = lax.all_to_all(back, MEM, 0, 0, tiled=True)  13.7 us
    all_to_all x1, starting transfers between devices, per_device(): got = lax.all_to_all(pay, MEM, 0, 0, tiled=True)  7.36 us
    pallas_call x1, Pallas kernels, per_device(): kernel_call(denoise_kernel, shaped((PEERS, 48, 128)), [pltpu.VMEM((2, 14,...  6.69 us
    ppermute x1, starting transfers between devices, per_device(): outer_tile = lax.ppermute(rows, TILE, across)  5.38 us
    all_gather x1, blocking collectives, per_device(): chip = lax.all_gather(rows, 'c')  4.31 us
    ppermute x1, starting transfers between devices, per_device(): inner_row = lax.ppermute(inner_row, TILE, inner)  4 us
  transfers between devices with their start and end apart: 4, of which 1 were waited for; matrix products, arithmetic and copies ran while one was open for 2% of the time, Pallas kernels for 0%

profile of v1, /device:TPU:1, one launch (start us, length us, event | category | flops | bytes accessed | tf_op | source)
XLA Modules:
  0.0 89.0 jit_solution(5445829497202262936)
XLA Ops:
  0.6 0.0 copy-start.2
  0.6 0.9 %copy-done.2 = bf16[2,4,8192]{2,1,0:T(4,128)(2,1)S(1)} copy-done((bf16[2,4,8192]{2,1,0:T(4,128)(2,1)S(1)}, bf16[2,4,8192]{2,1,0:T(4,128)(2,1)}, u32[]{:S(2)}) %copy-start.2) | copy-done | bytes 131096
  1.6 5.4 %collective-permute-start = (bf16[2,4,64,128]{3,2,1,0:T(8,128)(2,1)S(1)}, bf16[2,4,64,128]{3,2,1,0:T(8,128)(2,1)S(1)}, u32[]{:S(2)}, u32[]{:S(2)}) collective-permute-start(bf16[2,4,64,128]{3,2,1,0:T(8,128)(2,1)S(1)} %get-tuple-element.9), channel_id=1, source_target_pairs={{1,2},{2,1},{3,4},{4,3},{5,6},{6,5},{7,8},{8,7},{9,10},{10,9},{11,... | collective-permute-start | bytes 393224 | tf_op jit(solution)/shard_map/ppermute | solution.py:256
  7.0 4.0 %collective-permute-start.1 = (bf16[2,64,128]{2,1,0:T(8,128)(2,1)S(1)}, bf16[2,64,128]{2,1,0:T(8,128)(2,1)S(1)}, u32[]{:S(2)}, u32[]{:S(2)}) collective-permute-start(bf16[2,64,128]{2,1,0:T(8,128)(2,1)S(1)} %get-tuple-element.10), channel_id=1, source_target_pairs={{1,3},{2,0},{3,5},{4,2},{5,7},{6,4},{7,9},{8,6},{9,11},{10,8},{11,... | collective-permute-start | bytes 98312 | tf_op jit(solution)/shard_map/ppermute | solution.py:258
  11.0 1.3 %collective-permute-start.2 = (bf16[2,64,128]{2,1,0:T(8,128)(2,1)S(1)}, bf16[2,64,128]{2,1,0:T(8,128)(2,1)S(1)}, u32[]{:S(2)}, u32[]{:S(2)}) collective-permute-start(bf16[2,64,128]{2,1,0:T(8,128)(2,1)S(1)} %get-tuple-element.11), channel_id=1, source_target_pairs={{0,2},{3,1},{2,4},{5,3},{4,6},{7,5},{6,8},{9,7},{8,10},{11,9},{10,... | collective-permute-start | bytes 98312 | tf_op jit(solution)/shard_map/ppermute | solution.py:257
  12.3 0.8 reshape.25
  13.1 0.1 maximum_bitcast_fusion
  13.3 4.3 %all-gather = bf16[4,4,64,128]{3,2,1,0:T(8,128)(2,1)S(1)} all-gather(bf16[2,4,64,128]{3,2,1,0:T(8,128)(2,1)S(1)} %get-tuple-element.9), channel_id=2, replica_groups=mesh['y'=8,'x'=4,'z'=8,'c'=2] {'c'}, dimensions={0}, use_global_device_ids=true | all-gather | bytes 393216 | tf_op jit(solution)/shard_map/all_gather | solution.py:259
  17.6 0.8 reshape.27.cells_ref
  18.3 0.0 copy-start
  18.3 1.1 %copy-done = bf16[2,576,256]{2,1,0:T(8,128)(2,1)S(1)} copy-done((bf16[2,576,256]{2,1,0:T(8,128)(2,1)S(1)}, bf16[2,576,256]{2,1,0:T(8,128)(2,1)}, u32[]{:S(2)}) %copy-start) | copy-done | bytes 589848
  19.4 0.0 copy-start.1
  19.4 1.1 %copy-done.1 = bf16[2,2304,64]{1,2,0:T(8,128)(2,1)S(1)} copy-done((bf16[2,2304,64]{1,2,0:T(8,128)(2,1)S(1)}, bf16[2,2304,64]{1,2,0:T(8,128)(2,1)}, u32[]{:S(2)}) %copy-start.1) | copy-done | bytes 589848
  20.5 0.2 shard_map.87
  20.7 0.0 collective-permute-done.1.inner_row
  20.7 0.0 collective-permute-done.2.outer_row
  20.7 0.0 collective-permute-done.outer_ref
  20.7 0.0 copy-start.3
  20.7 0.0 copy-start.4
  20.7 6.7 %shard_map.88 = bf16[32,48,128]{2,1,0:T(8,128)(2,1)} custom-call(bf16[2,2,4,64,128]{4,3,2,1,0:T(8,128)(2,1)S(1)} %bitcast.24, bf16[2,4,64,128]{3,2,1,0:T(8,128)(2,1)S(1)} %collective-permute-done.outer_ref, bf16[2,64,128]{2,1,0:T(8,128)(2,1)S(1)} %collective-permute-done.1.inner_row, bf16[2,64,128]{2,1,0:T(8,128)(2,1)S(1)} %collective-permute-done.2.outer_row, ...), custom_call_target="tpu_custom_call" | custom-call | flops 4000000000 | bytes 4300000 | tf_op jit(solution)/shard_map/pallas_call | solution.py:263
  27.4 7.4 %all-to-all-start = ((bf16[32,48,128]{2,1,0:T(8,128)(2,1)}), bf16[32,48,128]{2,1,0:T(8,128)(2,1)S(1)}, u32[]{:S(2)}, u32[]{:S(2)}) async-start(bf16[32,48,128]{2,1,0:T(8,128)(2,1)} %shard_map.88), calls=%async_computation | async-start | bytes 786432 | tf_op jit(solution)/shard_map/all_to_all | solution.py:275
  34.8 0.0 copy-done.3
  34.8 0.1 reshape.28
  34.9 0.0 copy-done.4
  34.9 0.1 reshape.30
  35.1 13.9 %all-to-all-done.got_ref = bf16[32,48,128]{2,1,0:T(8,128)(2,1)S(1)} async-done(((bf16[32,48,128]{2,1,0:T(8,128)(2,1)}), bf16[32,48,128]{2,1,0:T(8,128)(2,1)S(1)}, u32[]{:S(2)}, u32[]{:S(2)}) %all-to-all-start) | async-done | bytes 393248 | tf_op jit(solution)/shard_map/all_to_all | solution.py:275
  49.0 0.8 shard_map.89
  49.8 24.0 %all_to_all.15.parts_ref = f32[16,32,128]{2,1,0:T(8,128)S(1)} all-to-all(f32[16,32,128]{2,1,0:T(8,128)S(1)} %shard_map.89), channel_id=1, replica_groups=mesh['y'=8,'x'=4,'z'=8,'c'=2] {'z','c'}, dimensions={0} | all-to-all | bytes 524288 | tf_op jit(solution)/shard_map/all_to_all | solution.py:283
  73.9 0.7 shard_map.90
  74.6 13.7 %all_to_all.16.got_ref = bf16[32,16,128]{2,1,0:T(8,128)(2,1)S(1)} all-to-all(bf16[32,16,128]{2,1,0:T(8,128)(2,1)S(1)} %get-tuple-element.14), channel_id=1, replica_groups=mesh['y'=8,'x'=4,'z'=8,'c'=2] {'y','x'}, dimensions={0} | all-to-all | bytes 262144 | tf_op jit(solution)/shard_map/all_to_all | solution.py:288
  88.3 0.7 shard_map.91
  (9 shorter events, 0.2 us)
Async XLA Ops:
  0.6 0.9 %copy-start.2 = (bf16[2,4,8192]{2,1,0:T(4,128)(2,1)S(1)}, bf16[2,4,8192]{2,1,0:T(4,128)(2,1)}, u32[]{:S(2)}) copy-start(bf16[2,4,8192]{2,1,0:T(4,128)(2,1)} %x_ref.1) | copy-start | bytes 393220
  1.6 19.1 %collective-permute-start = (bf16[2,4,64,128]{3,2,1,0:T(8,128)(2,1)S(1)}, bf16[2,4,64,128]{3,2,1,0:T(8,128)(2,1)S(1)}, u32[]{:S(2)}, u32[]{:S(2)}) collective-permute-start(bf16[2,4,64,128]{3,2,1,0:T(8,128)(2,1)S(1)} %get-tuple-element.9), channel_id=1, source_target_pairs={{1,2},{2,1},{3,4},{4,3},{5,6},{6,5},{7,8},{8,7},{9,10},{10,9},{11,... | collective-permute-start | bytes 393224 | tf_op jit(solution)/shard_map/ppermute | solution.py:256
  7.0 13.7 %collective-permute-start.1 = (bf16[2,64,128]{2,1,0:T(8,128)(2,1)S(1)}, bf16[2,64,128]{2,1,0:T(8,128)(2,1)S(1)}, u32[]{:S(2)}, u32[]{:S(2)}) collective-permute-start(bf16[2,64,128]{2,1,0:T(8,128)(2,1)S(1)} %get-tuple-element.10), channel_id=1, source_target_pairs={{1,3},{2,0},{3,5},{4,2},{5,7},{6,4},{7,9},{8,6},{9,11},{10,8},{11,... | collective-permute-start | bytes 98312 | tf_op jit(solution)/shard_map/ppermute | solution.py:258
  11.0 9.7 %collective-permute-start.2 = (bf16[2,64,128]{2,1,0:T(8,128)(2,1)S(1)}, bf16[2,64,128]{2,1,0:T(8,128)(2,1)S(1)}, u32[]{:S(2)}, u32[]{:S(2)}) collective-permute-start(bf16[2,64,128]{2,1,0:T(8,128)(2,1)S(1)} %get-tuple-element.11), channel_id=1, source_target_pairs={{0,2},{3,1},{2,4},{5,3},{4,6},{7,5},{6,8},{9,7},{8,10},{11,9},{10,... | collective-permute-start | bytes 98312 | tf_op jit(solution)/shard_map/ppermute | solution.py:257
  18.3 1.1 %copy-start = (bf16[2,576,256]{2,1,0:T(8,128)(2,1)S(1)}, bf16[2,576,256]{2,1,0:T(8,128)(2,1)}, u32[]{:S(2)}) copy-start(bf16[2,576,256]{2,1,0:T(8,128)(2,1)} %in_ref.1) | copy-start | bytes 1769476
  19.4 1.1 %copy-start.1 = (bf16[2,2304,64]{1,2,0:T(8,128)(2,1)S(1)}, bf16[2,2304,64]{1,2,0:T(8,128)(2,1)}, u32[]{:S(2)}) copy-start(bf16[2,2304,64]{1,2,0:T(8,128)(2,1)} %param.9) | copy-start | bytes 1769476
  20.7 14.1 %copy-start.3 = (f32[4,256]{1,0:T(4,128)S(1)}, f32[4,256]{1,0:T(4,128)}, u32[]{:S(2)}) copy-start(f32[4,256]{1,0:T(4,128)} %param.12) | copy-start | bytes 12292
  20.7 14.2 %copy-start.4 = (f32[4,256]{1,0:T(4,128)S(1)}, f32[4,256]{1,0:T(4,128)}, u32[]{:S(2)}) copy-start(f32[4,256]{1,0:T(4,128)} %param.13) | copy-start | bytes 12292
  27.4 21.6 %all-to-all-start = ((bf16[32,48,128]{2,1,0:T(8,128)(2,1)}), bf16[32,48,128]{2,1,0:T(8,128)(2,1)S(1)}, u32[]{:S(2)}, u32[]{:S(2)}) async-start(bf16[32,48,128]{2,1,0:T(8,128)(2,1)} %shard_map.88), calls=%async_computation | async-start | bytes 786432 | tf_op jit(solution)/shard_map/all_to_all | solution.py:275

commit v2 on v1

--- a/solution.py
+++ b/solution.py
@@ -50,7 +50,7 @@
         outer_ref[m] = jnp.where(upper, rows[0], rows[3]).astype(BF16)
 
 
-def weights_kernel(in_ref, out_ref, first_ref, second_ref):
+def spread_weights(in_ref, out_ref, seen_ref, first_ref, second_ref, obs_ref):
     first_ref[...] = jnp.zeros_like(first_ref)
     second_ref[...] = jnp.zeros_like(second_ref)
     for layer in range(2):
@@ -69,6 +69,15 @@
                         second_ref[layer, 64 * b : 64 * b + 64, 512 * dr + 256 * h : 512 * dr + 256 * h + 256] = (
                             out_ref[layer, :, at : at + 256]
                         )
+    taps = seen_ref[...].astype(F32)
+    none = jnp.zeros((8, 64), F32)
+    for dr in range(3):
+        for h in range(2):
+            blocks = [j - h + 1 for j in BLOCKS]
+            obs_ref[8 * (2 * dr + h) : 8 * (2 * dr + h) + 8, :] = jnp.concatenate(
+                [taps[:, 64 * (3 * dr + dc) : 64 * (3 * dr + dc) + 64] if 0 <= dc <= 2 else none for dc in blocks],
+                axis=1,
+            )
 
 
 def beside(values, lower):
@@ -89,8 +98,31 @@
     a_ref[m, pl.ds(row, count), :, 128:256] = beside(wide, lower)[0].astype(BF16)
 
 
-def denoise_kernel(chip_ref, outer_ref, inner_row, outer_row, w1_ref, w2_ref, obs_ref, cells_ref, pay_ref,
-                   x_ref, a_ref, h_ref, flat):
+def by_channel(values_ref, precision_ref, sides_ref):
+    own = lax.broadcasted_iota(jnp.int32, (8, 256), 1) % 8 == lax.broadcasted_iota(jnp.int32, (8, 256), 0)
+    spread = [
+        jnp.concatenate(
+            [jnp.where(own, jnp.broadcast_to(ref[r : r + 1, :], (8, 256)), 0.0) for r in range(4)], axis=1
+        )
+        for ref in (values_ref, precision_ref)
+    ]
+    whole = jnp.concatenate(spread, axis=0)
+    at = lax.broadcasted_iota(jnp.int32, (1024, 128), 0)
+    place = jnp.where(at // 8 == lax.broadcasted_iota(jnp.int32, (1024, 128), 1), 1.0, 0.0).astype(BF16)
+    high = whole.astype(BF16)
+    rest = whole - high.astype(F32)
+    middle = rest.astype(BF16)
+    low = (rest - middle.astype(F32)).astype(BF16)
+    placed = jnp.dot(jnp.concatenate([high, middle, low], axis=0), place, preferred_element_type=F32)
+    sides_ref[...] = placed[0:16] + placed[16:32] + placed[32:48]
+
+
+def denoise_kernel(chip_ref, outer_ref, inner_row, outer_row, in_hbm, out_hbm, seen_ref, cells_ref, values_ref,
+                   precision_ref, pay_ref, sides_ref,
+                   x_ref, a_ref, h_ref, flat, in_ref, out_ref, w1_ref, w2_ref, obs_ref, sems):
+    fetches = [pltpu.make_async_copy(in_hbm, in_ref, sems.at[0]), pltpu.make_async_copy(out_hbm, out_ref, sems.at[1])]
+    for fetch in fetches:
+        fetch.start()
     c = lax.axis_index("c")
     tile = 2 * lax.axis_index("z") + c
     ones = jnp.where(
@@ -115,12 +147,17 @@
             for m in range(2):
                 ref[m, high:size] = jnp.zeros((size - high, *ref.shape[2:]), ref.dtype)
 
+    by_channel(values_ref, precision_ref, sides_ref)
     for layer, (size, step1, step2) in enumerate(((14, 4, 5), (10, 4, 3))):
         half = size // 2
         for m in range(2):
             for row in (0, half):
                 patches(a_ref, m, row, half, x_ref[m, row : row + half], ones, True)
         hidden = size - 2
+        if layer == 0:
+            for fetch in fetches:
+                fetch.wait()
+            spread_weights(in_ref, out_ref, seen_ref, w1_ref, w2_ref, obs_ref)
         for m in range(2):
             for row in range(0, hidden, step1):
                 left = jnp.concatenate(
@@ -145,7 +182,7 @@
                 x_ref[m, row : row + step2] = total.astype(BF16)
         clear(x_ref, 3 - 2 * layer, kept - 3 + 2 * layer, kept)
 
-    cell = cells_ref[...]
+    cell = jnp.concatenate([cells_ref[r : r + 1, :] for r in range(4)], axis=1)
     pair = lax.shift_right_logical(cell, 1)
     lane_row = lax.broadcasted_iota(jnp.int32, (1, 128), 1) // 32
     index = lax.broadcasted_iota(jnp.int32, (384, 128), 0)
@@ -155,35 +192,39 @@
     parts = []
     for m in range(2):
         patches(a_ref, m, 0, 6, x_ref[m, 0:6], ones, False)
-        y = lax.dot_general(obs_ref[...], a_ref[m, 0:6].reshape(384, 256), NT, preferred_element_type=F32)
-        y = jnp.concatenate([y[16 * dr : 16 * dr + 16] for dr in range(3)], axis=1)
-        high = y.astype(BF16).astype(F32)
-        parts += [high, y - high]
-    seen = jnp.dot(jnp.concatenate(parts, axis=0).astype(BF16), pick, preferred_element_type=F32)
+        y = lax.dot_general(obs_ref[...].astype(BF16), a_ref[m, 0:6].reshape(384, 256), NT, preferred_element_type=F32)
+        parts.append(y)
+    seen = []
+    for y in parts:
+        taps = [y[16 * dr : 16 * dr + 16] for dr in range(3)]
+        whole = jnp.concatenate(taps, axis=1)
+        high = whole.astype(BF16).astype(F32)
+        both = jnp.concatenate([high, whole - high], axis=0).astype(BF16)
+        picked = jnp.dot(both, pick, preferred_element_type=F32)
+        seen.append(picked[0:16] + picked[16:32])
+    seen = jnp.concatenate(seen, axis=0)
     odd = jnp.broadcast_to((cell & 1) == 1, (8, 128))
-    got = [jnp.where(odd, seen[16 * i + 8 : 16 * i + 16], seen[16 * i : 16 * i + 8]) for i in range(4)]
-    high = jnp.concatenate([got[0], got[2]], axis=0).astype(BF16)
-    low = jnp.concatenate([got[1], got[3]], axis=0).astype(BF16)
+    got = [jnp.where(odd, seen[16 * m + 8 : 16 * m + 16], seen[16 * m : 16 * m + 8]) for m in range(2)]
+    got = jnp.concatenate(got, axis=0).astype(BF16)
     for m in range(2):
         for r in range(4):
             flat[pl.ds(256 * m + r, PAIRS, stride=4), :] = x_ref[m, 1 + r].astype(F32)
     for p in range(PEERS):
         both = jnp.concatenate([flat[8 * p : 8 * p + 8], flat[256 + 8 * p : 256 + 8 * p + 8]], axis=0)
         pay_ref[p, 0:16] = both.astype(BF16)
-        pay_ref[p, 16:32] = high
-        pay_ref[p, 32:48] = low
-
-
-def gram_kernel(got_ref, values_ref, precision_ref, out_ref, flat):
-    for p in range(PEERS):
-        flat[16 * p : 16 * p + 16] = got_ref[p, 16:32].astype(F32) + got_ref[p, 32:48].astype(F32)
+        pay_ref[p, 16:32] = got
+
+
+def gram_kernel(got_ref, sides_ref, out_ref, flat):
+    for p in range(PEERS):
+        flat[16 * p : 16 * p + 16] = got_ref[p, 16:32].astype(F32)
     shape = (64, 128)
     left, right = [], []
     for o in range(8):
         members = flat[pl.ds(o, 64, stride=8), :]
         mean = jnp.sum(members, axis=0, keepdims=True) * (1.0 / 64)
-        left.append((members - mean) * jnp.broadcast_to(precision_ref[o : o + 1], shape))
-        right.append(jnp.broadcast_to(values_ref[o : o + 1], shape) - members)
+        left.append((members - mean) * jnp.broadcast_to(sides_ref[8 + o : 9 + o], shape))
+        right.append(jnp.broadcast_to(sides_ref[o : o + 1], shape) - members)
     left = jnp.concatenate(left, axis=1)
     right = jnp.concatenate(right, axis=1)
     none = jnp.zeros_like(right)
@@ -195,13 +236,13 @@
         preferred_element_type=F32,
     )
     for t in range(16):
-        out_ref[t] = total
+        out_ref[t] = total.astype(BF16)
 
 
 def update_kernel(got_ref, parts_ref, covariance_ref, back_ref, flat):
-    total = parts_ref[0]
+    total = parts_ref[0].astype(F32)
     for t in range(1, 16):
-        total = total + parts_ref[t]
+        total = total + parts_ref[t].astype(F32)
     total = total * (1.0 / 16384)
     covariance = jnp.concatenate([total[:, 0:64], total[:, 64:128]], axis=0)
     covariance_ref[...] = covariance
@@ -226,15 +267,6 @@
             for t in range(2):
                 at = 128 * (2 * p + t)
                 out_ref[m, :, at : at + 128] = values[8 * m + 4 * t : 8 * m + 4 * t + 4]
-
-
-def observed_weights(weight):
-    taps = jnp.transpose(weight.reshape(3, 3, 64, 8), (0, 1, 3, 2))
-    none = jnp.zeros_like(taps[:, 0])
-    sides = []
-    for h in range(2):
-        sides.append(jnp.concatenate([taps[:, j - h + 1] if 0 <= j - h + 1 <= 2 else none for j in BLOCKS], axis=-1))
-    return jnp.stack(sides, axis=1).reshape(48, 256)
 
 
 def exchange_pairs():
@@ -257,29 +289,34 @@
     outer_row = lax.ppermute(outer_row, TILE, outer)
     inner_row = lax.ppermute(inner_row, TILE, inner)
     chip = lax.all_gather(rows, "c")
-    first, second = kernel_call(
-        weights_kernel, (shaped((2, 768, 512)), shaped((2, 256, 1536))), moved=4_300_000,
-    )(in_weight, jnp.transpose(out_weight, (0, 2, 1)))
-    pay = kernel_call(
+
+    vmem, hbm = pl.BlockSpec(memory_space=pltpu.VMEM), pl.BlockSpec(memory_space=pltpu.HBM)
+    pay, sides = pl.pallas_call(
         denoise_kernel,
-        shaped((PEERS, 48, 128)),
-        [
+        out_shape=(shaped((PEERS, 32, 128)), shaped((16, 128), F32)),
+        in_specs=[vmem] * 4 + [hbm] * 2 + [vmem] * 4,
+        scratch_shapes=[
             pltpu.VMEM((2, 14, PAIRS, 128), BF16),
             pltpu.VMEM((2, 14, PAIRS, 256), BF16),
             pltpu.VMEM((2, 12, PAIRS, 512), BF16),
             pltpu.VMEM((512, 128), F32),
+            pltpu.VMEM((2, 576, 256), BF16),
+            pltpu.VMEM((2, 64, 2304), BF16),
+            pltpu.VMEM((2, 768, 512), BF16),
+            pltpu.VMEM((2, 256, 1536), BF16),
+            pltpu.VMEM((48, 256), F32),
+            pltpu.SemaphoreType.DMA((2,)),
         ],
-        flops=4_000_000_000, moved=4_300_000, limit=40 * 1024 * 1024,
-    )(chip, outer_tile, inner_row, outer_row, first, second, observed_weights(observe_weight),
-      obs_cells.reshape(1, 128))
+        cost_estimate=pl.CostEstimate(flops=4_000_000_000, bytes_accessed=4_300_000, transcendentals=0),
+        compiler_params=pltpu.CompilerParams(vmem_limit_bytes=52 * 1024 * 1024),
+    )(chip, outer_tile, inner_row, outer_row, pltpu.with_memory_space_constraint(in_weight, pltpu.HBM),
+      pltpu.with_memory_space_constraint(jnp.transpose(out_weight, (0, 2, 1)), pltpu.HBM),
+      jnp.transpose(observe_weight), obs_cells, obs_values, obs_precision)
     got = lax.all_to_all(pay, MEM, 0, 0, tiled=True)
 
-    def by_channel(values):
-        return jnp.transpose(values.reshape(4, 32, 8), (2, 0, 1)).reshape(8, 128)
-
     parts = kernel_call(
-        gram_kernel, shaped((16, 32, 128), F32), [pltpu.VMEM((512, 128), F32)], moved=700_000,
-    )(got, by_channel(obs_values), by_channel(obs_precision))
+        gram_kernel, shaped((16, 32, 128)), [pltpu.VMEM((512, 128), F32)], moved=700_000,
+    )(got, sides)
     parts = lax.all_to_all(parts, TILE, 0, 0, tiled=True)
     covariance, back = kernel_call(
         update_kernel, (shaped((64, 64), F32), shaped((PEERS, 16, 128))), [pltpu.VMEM((512, 128), F32)],

time: 89.5 us -> 80.6 us (0.901)
  blocking collectives: 42 us -> 57.8 us
  waiting for transfers between devices: 13.9 us -> 0.01 us
  starting transfers between devices: 18 us -> 10.7 us
  local copies, waits for them, and re-layouts: 4.93 us -> 1.56 us
    all_to_all x0 -> x1, blocking collectives: none -> 21.2 us  [per_device(): got = lax.all_to_all(pay, MEM, 0, 0, tiled=True)]
    all_to_all x1 -> x0, waiting for transfers between devices: 13.9 us -> none  [per_device(): got = lax.all_to_all(pay, MEM, 0, 0, tiled=True)]
    all_to_all x1 -> x0, starting transfers between devices: 7.36 us -> none  [per_device(): got = lax.all_to_all(pay, MEM, 0, 0, tiled=True)]
    all_to_all x1, blocking collectives: 24 us -> 19.2 us  [per_device(): parts = lax.all_to_all(parts, TILE, 0, 0, tiled=True)]
    reshape x6 -> x0, local copies, waits for them, and re-layouts: 1.85 us -> none  [the longest x1 0.79 us: observed_weights(): taps = jnp.transpose(weight.reshape(3, 3, 64, 8), (0, 1, 3, 2))]
    unnamed x10, local copies, waits for them, and re-layouts: 3.04 us -> 1.56 us
    pallas_call x3 -> x2, Pallas kernels: 7.71 us -> 7.92 us  [the longest x1 7.14 us: per_device(): pl.pallas_call(denoise_kernel, out_shape=(shaped((PEERS, 32, 128)), shape...]
  transfers between devices with their start and end apart: 4 -> 3, of which waited for: 1 -> 0; matrix products, arithmetic and copies ran while one was open for 2% -> 0% of each run, Pallas kernels for 0% -> 0%
where the time goes in v2:
time: 80.6 us; the launch traced here: 80.2 us
  blocking collectives  57.8 us (72%)
  starting transfers between devices  10.7 us (13%)
  Pallas kernels  9.42 us (12%)
  local copies, waits for them, and re-layouts  1.56 us (2%)
    all_to_all x1, blocking collectives, per_device(): got = lax.all_to_all(pay, MEM, 0, 0, tiled=True)  21.2 us
    all_to_all x1, blocking collectives, per_device(): parts = lax.all_to_all(parts, TILE, 0, 0, tiled=True)  19.2 us
    all_to_all x1, blocking collectives, per_device(): back = lax.all_to_all(back, MEM, 0, 0, tiled=True)  13.1 us
    pallas_call x1, Pallas kernels, per_device(): pl.pallas_call(denoise_kernel, out_shape=(shaped((PEERS, 32, 128)), shape...  7.14 us
    ppermute x1, starting transfers between devices, per_device(): outer_tile = lax.ppermute(rows, TILE, across)  5.38 us
    all_gather x1, blocking collectives, per_device(): chip = lax.all_gather(rows, 'c')  4.31 us
    ppermute x1, starting transfers between devices, per_device(): inner_row = lax.ppermute(inner_row, TILE, inner)  4 us
  transfers between devices with their start and end apart: 3, of which 0 were waited for; matrix products, arithmetic and copies ran while one was open for 0% of the time, Pallas kernels for 0%

profile of v2, /device:TPU:1, one launch (start us, length us, event | category | flops | bytes accessed | tf_op | source)
XLA Modules:
  0.0 80.2 jit_solution(1728972772064175380)
XLA Ops:
  0.6 0.0 copy-start
  0.6 0.9 %copy-done = bf16[2,4,8192]{2,1,0:T(4,128)(2,1)S(1)} copy-done((bf16[2,4,8192]{2,1,0:T(4,128)(2,1)S(1)}, bf16[2,4,8192]{2,1,0:T(4,128)(2,1)}, u32[]{:S(2)}) %copy-start) | copy-done | bytes 131096
  1.6 5.4 %collective-permute-start = (bf16[2,4,64,128]{3,2,1,0:T(8,128)(2,1)S(1)}, bf16[2,4,64,128]{3,2,1,0:T(8,128)(2,1)S(1)}, u32[]{:S(2)}, u32[]{:S(2)}) collective-permute-start(bf16[2,4,64,128]{3,2,1,0:T(8,128)(2,1)S(1)} %get-tuple-element.9), channel_id=1, source_target_pairs={{1,2},{2,1},{3,4},{4,3},{5,6},{6,5},{7,8},{8,7},{9,10},{10,9},{11,... | collective-permute-start | bytes 393224 | tf_op jit(solution)/shard_map/ppermute | solution.py:288
  7.0 4.0 %collective-permute-start.1 = (bf16[2,64,128]{2,1,0:T(8,128)(2,1)S(1)}, bf16[2,64,128]{2,1,0:T(8,128)(2,1)S(1)}, u32[]{:S(2)}, u32[]{:S(2)}) collective-permute-start(bf16[2,64,128]{2,1,0:T(8,128)(2,1)S(1)} %get-tuple-element.10), channel_id=1, source_target_pairs={{1,3},{2,0},{3,5},{4,2},{5,7},{6,4},{7,9},{8,6},{9,11},{10,8},{11,... | collective-permute-start | bytes 98312 | tf_op jit(solution)/shard_map/ppermute | solution.py:290
  11.0 0.0 copy-start.1
  11.0 1.3 %collective-permute-start.2 = (bf16[2,64,128]{2,1,0:T(8,128)(2,1)S(1)}, bf16[2,64,128]{2,1,0:T(8,128)(2,1)S(1)}, u32[]{:S(2)}, u32[]{:S(2)}) collective-permute-start(bf16[2,64,128]{2,1,0:T(8,128)(2,1)S(1)} %get-tuple-element.11), channel_id=1, source_target_pairs={{0,2},{3,1},{2,4},{5,3},{4,6},{7,5},{6,8},{9,7},{8,10},{11,9},{10,... | collective-permute-start | bytes 98312 | tf_op jit(solution)/shard_map/ppermute | solution.py:289
  12.3 0.0 copy-start.3
  12.3 0.0 copy-start.4
  12.3 4.3 %all-gather = bf16[4,4,64,128]{3,2,1,0:T(8,128)(2,1)S(1)} all-gather(bf16[2,4,64,128]{3,2,1,0:T(8,128)(2,1)S(1)} %get-tuple-element.9), channel_id=2, replica_groups=mesh['y'=8,'x'=4,'z'=8,'c'=2] {'c'}, dimensions={0}, use_global_device_ids=true | all-gather | bytes 393216 | tf_op jit(solution)/shard_map/all_gather | solution.py:291
  16.6 0.0 copy-start.2
  16.6 0.0 collective-permute-done.1.inner_row
  16.6 0.0 collective-permute-done.2.outer_row
  16.6 0.0 collective-permute-done.outer_ref
  16.6 0.0 copy-done.1
  16.6 0.0 copy-done.3
  16.7 0.0 copy-done.4
  16.7 0.6 copy-done.2
  17.3 7.1 %shard_map.87 = (bf16[32,32,128]{2,1,0:T(8,128)(2,1)S(1)}, f32[16,128]{1,0:T(8,128)S(1)}) custom-call(bf16[2,2,4,64,128]{4,3,2,1,0:T(8,128)(2,1)S(1)} %bitcast.3, bf16[2,4,64,128]{3,2,1,0:T(8,128)(2,1)S(1)} %collective-permute-done.outer_ref, bf16[2,64,128]{2,1,0:T(8,128)(2,1)S(1)} %collective-permute-done.1.inner_row, ...), custom_call_target="tpu_custom_call" | custom-call | flops 4000000000 | bytes 4300000 | tf_op jit(solution)/shard_map/pallas_call | solution.py:294
  24.5 21.2 %all_to_all.15.got_ref = bf16[32,32,128]{2,1,0:T(8,128)(2,1)S(1)} all-to-all(bf16[32,32,128]{2,1,0:T(8,128)(2,1)S(1)} %get-tuple-element.12), channel_id=1, replica_groups=mesh['y'=8,'x'=4,'z'=8,'c'=2] {'y','x'}, dimensions={0} | all-to-all | bytes 524288 | tf_op jit(solution)/shard_map/all_to_all | solution.py:315
  45.6 0.8 shard_map.88
  46.4 19.2 %all_to_all.16.parts_ref = bf16[16,32,128]{2,1,0:T(8,128)(2,1)S(1)} all-to-all(bf16[16,32,128]{2,1,0:T(8,128)(2,1)S(1)} %shard_map.88), channel_id=1, replica_groups=mesh['y'=8,'x'=4,'z'=8,'c'=2] {'z','c'}, dimensions={0} | all-to-all | bytes 262144 | tf_op jit(solution)/shard_map/all_to_all | solution.py:320
  65.7 0.7 shard_map.89
  66.4 13.1 %all_to_all.17.got_ref = bf16[32,16,128]{2,1,0:T(8,128)(2,1)S(1)} all-to-all(bf16[32,16,128]{2,1,0:T(8,128)(2,1)S(1)} %get-tuple-element.14), channel_id=1, replica_groups=mesh['y'=8,'x'=4,'z'=8,'c'=2] {'y','x'}, dimensions={0} | all-to-all | bytes 262144 | tf_op jit(solution)/shard_map/all_to_all | solution.py:325
  79.5 0.7 shard_map.90
  (1 shorter events, 0.0 us)
Async XLA Ops:
  0.6 0.9 %copy-start = (bf16[2,4,8192]{2,1,0:T(4,128)(2,1)S(1)}, bf16[2,4,8192]{2,1,0:T(4,128)(2,1)}, u32[]{:S(2)}) copy-start(bf16[2,4,8192]{2,1,0:T(4,128)(2,1)} %x_ref.1) | copy-start | bytes 393220
  1.6 15.0 %collective-permute-start = (bf16[2,4,64,128]{3,2,1,0:T(8,128)(2,1)S(1)}, bf16[2,4,64,128]{3,2,1,0:T(8,128)(2,1)S(1)}, u32[]{:S(2)}, u32[]{:S(2)}) collective-permute-start(bf16[2,4,64,128]{3,2,1,0:T(8,128)(2,1)S(1)} %get-tuple-element.9), channel_id=1, source_target_pairs={{1,2},{2,1},{3,4},{4,3},{5,6},{6,5},{7,8},{8,7},{9,10},{10,9},{11,... | collective-permute-start | bytes 393224 | tf_op jit(solution)/shard_map/ppermute | solution.py:288
  7.0 9.7 %collective-permute-start.1 = (bf16[2,64,128]{2,1,0:T(8,128)(2,1)S(1)}, bf16[2,64,128]{2,1,0:T(8,128)(2,1)S(1)}, u32[]{:S(2)}, u32[]{:S(2)}) collective-permute-start(bf16[2,64,128]{2,1,0:T(8,128)(2,1)S(1)} %get-tuple-element.10), channel_id=1, source_target_pairs={{1,3},{2,0},{3,5},{4,2},{5,7},{6,4},{7,9},{8,6},{9,11},{10,8},{11,... | collective-permute-start | bytes 98312 | tf_op jit(solution)/shard_map/ppermute | solution.py:290
  11.0 5.7 %copy-start.1 = (bf16[576,8]{0,1:T(8,128)(2,1)S(1)}, bf16[576,8]{0,1:T(8,128)(2,1)}, u32[]{:S(2)}) copy-start(bf16[576,8]{0,1:T(8,128)(2,1)} %param.10) | copy-start | bytes 27652
  11.0 5.6 %collective-permute-start.2 = (bf16[2,64,128]{2,1,0:T(8,128)(2,1)S(1)}, bf16[2,64,128]{2,1,0:T(8,128)(2,1)S(1)}, u32[]{:S(2)}, u32[]{:S(2)}) collective-permute-start(bf16[2,64,128]{2,1,0:T(8,128)(2,1)S(1)} %get-tuple-element.11), channel_id=1, source_target_pairs={{0,2},{3,1},{2,4},{5,3},{4,6},{7,5},{6,8},{9,7},{8,10},{11,9},{10,... | collective-permute-start | bytes 98312 | tf_op jit(solution)/shard_map/ppermute | solution.py:289
  12.3 4.4 %copy-start.3 = (f32[4,256]{1,0:T(4,128)S(1)}, f32[4,256]{1,0:T(4,128)}, u32[]{:S(2)}) copy-start(f32[4,256]{1,0:T(4,128)} %precision_ref.1) | copy-start | bytes 12292
  12.3 4.4 %copy-start.4 = (s32[4,32]{1,0:T(4,128)S(1)}, s32[4,32]{1,0:T(4,128)}, u32[]{:S(2)}) copy-start(s32[4,32]{1,0:T(4,128)} %cells_ref.1) | copy-start | bytes 1540
  16.6 0.7 copy-start.2

commit v3 on v2

v3 whole, which is shorter than its diff:
```python
import functools

import jax
import jax.numpy as jnp
from jax import lax
from jax.experimental import pallas as pl
from jax.experimental.pallas import tpu as pltpu
from jax.sharding import Mesh
from jax.sharding import PartitionSpec as P

MEM = ("y", "x")
TILE = ("z", "c")
PAIRS = 64
HID = 256
PEERS = 32
EPS = 1e-06
STEP = 0.5
F32 = jnp.float32
BF16 = jnp.bfloat16
LIMIT = 24 * 1024 * 1024
NT = (((1,), (1,)), ((), ()))
TN = (((0,), (0,)), ((), ()))
BLOCKS = (0, 1, 2, -1)


def kernel_call(body, outs, scratch=(), flops=0, moved=0, limit=LIMIT):
    return pl.pallas_call(
        body,
        out_shape=outs,
        scratch_shapes=scratch,
        cost_estimate=pl.CostEstimate(flops=flops, bytes_accessed=moved, transcendentals=0),
        compiler_params=pltpu.CompilerParams(vmem_limit_bytes=limit),
    )


def shaped(shape, dtype=BF16):
    return jax.ShapeDtypeStruct(shape, dtype)


def rows_kernel(x_ref, rows_ref, flat):
    for m in range(2):
        for t in range(PAIRS):
            flat[256 * m + 4 * t : 256 * m + 4 * t + 4, :] = x_ref[m, :, 128 * t : 128 * t + 128].astype(F32)
    for m in range(2):
        for r in range(4):
            rows_ref[r, m] = flat[pl.ds(256 * m + r, PAIRS, stride=4), :].astype(BF16)


def spread_weights(in_ref, out_ref, seen_ref, first_ref, second_ref, obs_ref):
    first_ref[...] = jnp.zeros_like(first_ref)
    second_ref[...] = jnp.zeros_like(second_ref)
    for layer in range(2):
        for dr in range(3):
            for b, j in enumerate(BLOCKS):
                for h in range(2):
                    dc = j - h + 1
                    if 0 <= dc <= 2:
                        at = 64 * (3 * dr + dc)
                        first_ref[layer, 256 * dr + 64 * b : 256 * dr + 64 * b + 64, 256 * h : 256 * h + 256] = (
                            in_ref[layer, at : at + 64, :] * jnp.asarray(0.5, BF16)
                        )
                    dc = h - j + 1
                    if 0 <= dc <= 2:
                        at = 256 * (3 * dr + dc)
                        second_ref[layer, 64 * b : 64 * b + 64, 512 * dr + 256 * h : 512 * dr + 256 * h + 256] = (
                            out_ref[layer, :, at : at + 256]
                        )
    taps = seen_ref[...].astype(F32)
    none = jnp.zeros((8, 64), F32)
    rows = []
    for dr in range(3):
        for h in range(2):
            blocks = [j - h + 1 for j in BLOCKS]
            rows.append(jnp.concatenate(
                [taps[:, 64 * (3 * dr + dc) : 64 * (3 * dr + dc) + 64] if 0 <= dc <= 2 else none for dc in blocks],
                axis=1,
            ))
    obs_ref[...] = jnp.concatenate(rows, axis=0).astype(BF16)


def beside(values, lower):
    at = lax.broadcasted_iota(jnp.int32, values.shape, 1)
    after = jnp.where(at == PAIRS - 1, 0.0, pltpu.roll(values, PAIRS - 1, 1))
    before = jnp.where(at == 0, 0.0, pltpu.roll(values, 1, 1))
    return jnp.where(lower, after, before), jnp.where(lower, before, after)


def mean_over_channels():
    return jnp.where(
        (lax.broadcasted_iota(jnp.int32, (128, 128), 0) < 64) == (lax.broadcasted_iota(jnp.int32, (128, 128), 1) < 64),
        1.0 / 64, 0.0,
    ).astype(BF16)


def patches(a_ref, m, row, values, norm):
    count = values.shape[0]
    wide = values.astype(F32)
    lower = lax.broadcasted_iota(jnp.int32, wide.shape, 2) < 64
    if norm is not None:
        square = (values * values).reshape(count * PAIRS, 128)
        mean = jnp.dot(square, norm, preferred_element_type=F32).reshape(count, PAIRS, 128)
        wide = wide * lax.rsqrt(mean + EPS)
    a_ref[m, pl.ds(row, count), :, 0:128] = wide.astype(BF16)
    a_ref[m, pl.ds(row, count), :, 128:256] = beside(wide, lower)[0].astype(BF16)


def taps_of(ref, m, row, count):
    width = ref.shape[3]
    return jnp.concatenate(
        [ref[m, pl.ds(row + dr, count)].reshape(count * PAIRS, width) for dr in range(3)], axis=1
    )


def hidden_of(left, weight):
    v = jnp.dot(left, weight, preferred_element_type=F32)
    return v + v * jnp.tanh(v)


def scaled_rows(values, factors):
    return jnp.concatenate(
        [values[i : i + 1] * factors[i] if i in factors else values[i : i + 1] for i in range(values.shape[0])], axis=0
    )


def by_channel(values_ref, precision_ref, sides_ref):
    own = lax.broadcasted_iota(jnp.int32, (8, 256), 1) % 8 == lax.broadcasted_iota(jnp.int32, (8, 256), 0)
    spread = [
        jnp.concatenate(
            [jnp.where(own, jnp.broadcast_to(ref[r : r + 1, :], (8, 256)), 0.0) for r in range(4)], axis=1
        )
        for ref in (values_ref, precision_ref)
    ]
    whole = jnp.concatenate(spread, axis=0)
    at = lax.broadcasted_iota(jnp.int32, (1024, 128), 0)
    place = jnp.where(at // 8 == lax.broadcasted_iota(jnp.int32, (1024, 128), 1), 1.0, 0.0).astype(BF16)
    high = whole.astype(BF16)
    rest = whole - high.astype(F32)
    middle = rest.astype(BF16)
    low = (rest - middle.astype(F32)).astype(BF16)
    placed = jnp.dot(jnp.concatenate([high, middle, low], axis=0), place, preferred_element_type=F32)
    sides_ref[0:16] = placed[0:16] + placed[16:32] + placed[32:48]


def inner_kernel(chip_ref, in_hbm, out_hbm, seen_hbm, cells_hbm, values_hbm, precision_hbm,
                 a_ref, h_ref, w1_ref, w2_ref, obs_ref, pick_ref, sides_ref,
                 in_ref, out_ref, seen_ref, cells_ref, values_ref, precision_ref, sems):
    sources = (cells_hbm, values_hbm, precision_hbm, seen_hbm, in_hbm, out_hbm)
    targets = (cells_ref, values_ref, precision_ref, seen_ref, in_ref, out_ref)
    fetches = [pltpu.make_async_copy(a, b, sems.at[i]) for i, (a, b) in enumerate(zip(sources, targets))]
    for fetch in fetches:
        fetch.start()
    norm = mean_over_channels()
    for m in range(2):
        for row in (0, 4):
            patches(a_ref, m, row, chip_ref[row : row + 4, m], norm)
    for fetch in fetches[:3]:
        fetch.wait()
    by_channel(values_ref, precision_ref, sides_ref)
    cell = jnp.concatenate([cells_ref[r : r + 1, :] for r in range(4)], axis=1)
    pair = lax.shift_right_logical(cell, 1)
    lane_row = lax.broadcasted_iota(jnp.int32, (1, 128), 1) // 32
    index = lax.broadcasted_iota(jnp.int32, (384, 128), 0)
    for dr in range(3):
        pick_ref[384 * dr : 384 * dr + 384, :] = jnp.where(index == (lane_row + dr) * PAIRS + pair, 1.0, 0.0).astype(BF16)
    sides_ref[16:24] = jnp.broadcast_to((cell & 1).astype(F32), (8, 128))
    for fetch in fetches[3:]:
        fetch.wait()
    spread_weights(in_ref, out_ref, seen_ref, w1_ref, w2_ref, obs_ref)
    for m in range(2):
        for row in (0, 3):
            hidden = hidden_of(taps_of(a_ref, m, row, 3), w1_ref[0])
            h_ref[m, row : row + 3] = hidden.astype(BF16).reshape(3, PAIRS, 512)


def denoise_kernel(chip_ref, outer_ref, edge_ref, a_part, h_part, w1_ref, w2_ref, obs_ref, pick_ref, sides_ref,
                   pay_ref, x_ref, a_ref, h_ref, flat, sems):
    c = lax.axis_index("c")
    tile = 2 * lax.axis_index("z") + c
    first = jnp.where(tile == 0, 0.0, 1.0).astype(F32)
    last = jnp.where(tile == 15, 0.0, 1.0).astype(F32)
    start = 5 - 4 * c
    moves = [
        pltpu.make_async_copy(a_part.at[m], a_ref.at[m, pl.ds(start, 8)], sems.at[m]) for m in range(2)
    ] + [
        pltpu.make_async_copy(h_part.at[m], h_ref.at[m, pl.ds(start, 6)], sems.at[2 + m]) for m in range(2)
    ] + [pltpu.make_async_copy(chip_ref, x_ref.at[pl.ds(start, 8)], sems.at[4])]
    for move in moves:
        move.start()
    norm = mean_over_channels()
    edge = edge_ref[1 - c]
    for m in range(2):
        patches(a_ref, m, 9 * c, outer_ref[:, m], norm)
        patches(a_ref, m, 13 - 13 * c, edge[m : m + 1], norm)
    x_ref[pl.ds(9 * c, 5)] = outer_ref[...]
    x_ref[13 - 13 * c] = edge
    for move in moves:
        move.wait()
    upper = c == 1
    group = {q: jnp.where(upper, last if q else 1.0, first if q < 4 else 1.0) for q in range(5)}
    for m in range(2):
        left = jnp.concatenate([taps_of(a_ref, m, 7 * c, 5), taps_of(a_ref, m, 11 - 11 * c, 1)], axis=0)
        hidden = hidden_of(left, w1_ref[0])
        outer = scaled_rows(hidden[0 : 5 * PAIRS].reshape(5, PAIRS, 512), group)
        h_ref[m, pl.ds(7 * c, 5)] = outer.astype(BF16)
        h_ref[m, 11 - 11 * c] = hidden[5 * PAIRS :].astype(BF16)

    def finish(layer, m, kept, step, factors):
        for row in range(0, kept, step):
            y = lax.dot_general(taps_of(h_ref, m, row, step), w2_ref[layer], NT, preferred_element_type=F32)
            own = y[:, 0:128].reshape(step, PAIRS, 128)
            side = y[:, 128:256].reshape(step, PAIRS, 128)
            lower = lax.broadcasted_iota(jnp.int32, side.shape, 2) < 64
            total = x_ref[row + 2 : row + 2 + step, m].astype(F32) + own + beside(side, lower)[1]
            total = scaled_rows(total, {i - row: f for i, f in factors.items() if row <= i < row + step})
            x_ref[row : row + step, m] = total.astype(BF16)

    edges = {**{i: first for i in range(3)}, **{i: last for i in range(7, 10)}}
    for m in range(2):
        finish(0, m, 10, 5, edges)
    for m in range(2):
        for row in (0, 5):
            patches(a_ref, m, row, x_ref[row : row + 5, m], norm)
        for row, factors in ((0, {0: first, 1: first}), (4, {2: last, 3: last})):
            hidden = hidden_of(taps_of(a_ref, m, row, 4), w1_ref[1]).reshape(4, PAIRS, 512)
            h_ref[m, row : row + 4] = scaled_rows(hidden, factors).astype(BF16)
    seen = []
    for m in range(2):
        finish(1, m, 6, 3, {0: first, 5: last})
        patches(a_ref, m, 0, x_ref[0:6, m], None)
        y = lax.dot_general(obs_ref[...], a_ref[m, 0:6].reshape(384, 256), NT, preferred_element_type=F32)
        whole = jnp.concatenate([y[16 * dr : 16 * dr + 16] for dr in range(3)], axis=1)
        high = whole.astype(BF16).astype(F32)
        both = jnp.concatenate([high, whole - high], axis=0).astype(BF16)
        picked = jnp.dot(both, pick_ref[...], preferred_element_type=F32)
        seen.append(picked[0:16] + picked[16:32])
    odd = sides_ref[16:24] > 0.5
    got = jnp.concatenate([jnp.where(odd, y[8:16], y[0:8]) for y in seen], axis=0).astype(BF16)
    for m in range(2):
        for r in range(4):
            flat[pl.ds(256 * m + r, PAIRS, stride=4), :] = x_ref[1 + r, m].astype(F32)
    for p in range(PEERS):
        both = jnp.concatenate([flat[8 * p : 8 * p + 8], flat[256 + 8 * p : 256 + 8 * p + 8]], axis=0)
        pay_ref[p, 0:16] = both.astype(BF16)
        pay_ref[p, 16:32] = got


def gram_kernel(got_ref, sides_ref, out_ref, flat):
    for p in range(PEERS):
        flat[16 * p : 16 * p + 16] = got_ref[p, 16:32].astype(F32)
    shape = (64, 128)
    left, right = [], []
    for o in range(8):
        members = flat[pl.ds(o, 64, stride=8), :]
        mean = jnp.sum(members, axis=0, keepdims=True) * (1.0 / 64)
        left.append((members - mean) * jnp.broadcast_to(sides_ref[8 + o : 9 + o], shape))
        right.append(jnp.broadcast_to(sides_ref[o : o + 1], shape) - members)
    left = jnp.concatenate(left, axis=1)
    right = jnp.concatenate(right, axis=1)
    none = jnp.zeros_like(right)
    total = lax.dot_general(
        left[0:32], jnp.concatenate([right, none], axis=0), NT, precision=lax.Precision.HIGHEST,
        preferred_element_type=F32,
    ) + lax.dot_general(
        left[32:64], jnp.concatenate([none, right], axis=0), NT, precision=lax.Precision.HIGHEST,
        preferred_element_type=F32,
    )
    for t in range(16):
        out_ref[t] = total.astype(BF16)


def update_kernel(got_ref, parts_ref, covariance_ref, back_ref, flat):
    total = parts_ref[0].astype(F32)
    for t in range(1, 16):
        total = total + parts_ref[t].astype(F32)
    total = total * (1.0 / 16384)
    covariance = jnp.concatenate([total[:, 0:64], total[:, 64:128]], axis=0)
    covariance_ref[...] = covariance
    center = (covariance - jnp.mean(covariance, axis=0, keepdims=True)) * STEP
    high = center.astype(BF16)
    both = jnp.concatenate([high, (center - high.astype(F32)).astype(BF16)], axis=0)
    for p in range(PEERS):
        flat[16 * p : 16 * p + 16] = got_ref[p, 0:16].astype(F32)
    for s in range(8):
        members = flat[pl.ds(s, 64, stride=8), :]
        narrow = members.astype(BF16)
        moved = lax.dot_general(both, jnp.concatenate([narrow, narrow], axis=0), TN, preferred_element_type=F32)
        flat[pl.ds(s, 64, stride=8), :] = members + moved
    for p in range(PEERS):
        back_ref[p] = flat[16 * p : 16 * p + 16].astype(BF16)


def final_kernel(got_ref, out_ref):
    for p in range(PEERS):
        values = got_ref[p].astype(F32)
        for m in range(2):
            for t in range(2):
                at = 128 * (2 * p + t)
                out_ref[m, :, at : at + 128] = values[8 * m + 4 * t : 8 * m + 4 * t + 4]


def per_device(latents, in_weight, out_weight, observe_weight, obs_cells, obs_values, obs_precision):
    c = lax.axis_index("c")
    across = [pair for z in range(7) for pair in ((2 * z + 1, 2 * z + 2), (2 * z + 2, 2 * z + 1))]
    vmem = pl.BlockSpec(memory_space=pltpu.VMEM)
    hbm = pl.BlockSpec(memory_space=pltpu.HBM)
    rows = kernel_call(
        rows_kernel, shaped((4, 2, PAIRS, 128)), [pltpu.VMEM((512, 128), F32)], moved=300_000,
    )(latents)
    chip = lax.all_gather(rows, "c", axis=0, tiled=True)
    outer = lax.ppermute(lax.dynamic_slice_in_dim(chip, 3 * c, 5, axis=0), TILE, across)
    a_part, h_part, first, second, obs, pick, sides = pl.pallas_call(
        inner_kernel,
        out_shape=(
            shaped((2, 8, PAIRS, 256)), shaped((2, 6, PAIRS, 512)), shaped((2, 768, 512)), shaped((2, 256, 1536)),
            shaped((48, 256)), shaped((1152, 128)), shaped((24, 128), F32),
        ),
        in_specs=[vmem] + [hbm] * 6,
        scratch_shapes=[
            pltpu.VMEM((2, 576, 256), BF16), pltpu.VMEM((2, 64, 2304), BF16), pltpu.VMEM((8, 576), BF16),
            pltpu.VMEM((4, 32), jnp.int32), pltpu.VMEM((4, 256), F32), pltpu.VMEM((4, 256), F32),
            pltpu.SemaphoreType.DMA((6,)),
        ],
        cost_estimate=pl.CostEstimate(flops=1_000_000_000, bytes_accessed=6_000_000, transcendentals=0),
        compiler_params=pltpu.CompilerParams(vmem_limit_bytes=16 * 1024 * 1024),
    )(chip, *(pltpu.with_memory_space_constraint(v, pltpu.HBM) for v in (
        in_weight, jnp.transpose(out_weight, (0, 2, 1)), jnp.transpose(observe_weight), obs_cells, obs_values,
        obs_precision,
    )))
    edge = lax.all_gather(lax.dynamic_slice_in_dim(outer, 4 * (1 - c), 1, axis=0), "c", axis=0, tiled=True)
    pay = kernel_call(
        denoise_kernel,
        shaped((PEERS, 32, 128)),
        [
            pltpu.VMEM((14, 2, PAIRS, 128), BF16),
            pltpu.VMEM((2, 14, PAIRS, 256), BF16),
            pltpu.VMEM((2, 12, PAIRS, 512), BF16),
            pltpu.VMEM((512, 128), F32),
            pltpu.SemaphoreType.DMA((5,)),
        ],
        flops=4_000_000_000, moved=4_300_000,
    )(chip, outer, edge, a_part, h_part, first, second, obs, pick, sides)
    got = lax.all_to_all(pay, MEM, 0, 0, tiled=True)

    parts = kernel_call(
        gram_kernel, shaped((16, 32, 128)), [pltpu.VMEM((512, 128), F32)], moved=700_000,
    )(got, sides)
    parts = lax.all_to_all(parts, TILE, 0, 0, tiled=True)
    covariance, back = kernel_call(
        update_kernel, (shaped((64, 64), F32), shaped((PEERS, 16, 128))), [pltpu.VMEM((512, 128), F32)],
        moved=700_000,
    )(got, parts)
    back = lax.all_to_all(back, MEM, 0, 0, tiled=True)
    analysis = kernel_call(final_kernel, shaped((2, 4, 8192), F32), moved=400_000)(back)
    return analysis, covariance


def solution(mesh):
    split = Mesh(mesh.devices.reshape(8, 4, 8, 2), ("y", "x", "z", "c"))
    return jax.shard_map(
        per_device,
        mesh=split,
        in_specs=(P(MEM, TILE, None), P(), P(), P(), P(TILE, None), P(TILE, None), P(TILE, None)),
        out_specs=(P(MEM, TILE, None), P()),
        check_vma=False,
    )
```

time: 80.6 us -> 78.2 us (0.970)
  starting transfers between devices: 10.7 us -> 1.92 us
  blocking collectives: 57.8 us -> 61.7 us
  waiting for transfers between devices: 0.01 us -> 2.37 us
  Pallas kernels: 9.42 us -> 10.3 us
    ppermute x3 -> x1, starting transfers between devices: 10.7 us -> 1.92 us  [per_device(): lax.ppermute(lax.dynamic_slice_in_dim(chip, 3 * c, 5, axis=0), TILE, across)]
    all_gather x1 -> x2, blocking collectives: 4.31 us -> 10.3 us  [the longest x1 8.47 us: per_device(): chip = lax.all_gather(rows, 'c', axis=0, tiled=True)]
    all_to_all x1, blocking collectives: 21.2 us -> 16.4 us  [per_device(): got = lax.all_to_all(pay, MEM, 0, 0, tiled=True)]
    all_to_all x1, blocking collectives: 19.2 us -> 21.9 us  [per_device(): parts = lax.all_to_all(parts, TILE, 0, 0, tiled=True)]
    ppermute x3 -> x1, waiting for transfers between devices: 0.01 us -> 2.37 us  [per_device(): lax.ppermute(lax.dynamic_slice_in_dim(chip, 3 * c, 5, axis=0), TILE, across)]
    pallas_call x2 -> x3, Pallas kernels: 7.19 us -> 8.08 us  [the longest x1 5.72 us: per_device(): kernel_call(denoise_kernel, shaped((PEERS, 32, 128)), [pltpu.VMEM((14, 2,...]
  transfers between devices with their start and end apart: 3 -> 1, of which waited for: 0 -> 1; matrix products, arithmetic and copies ran while one was open for 0% -> 0% of each run, Pallas kernels for 0% -> 3%
where the time goes in v3:
time: 78.2 us; the launch traced here: 77.9 us
  blocking collectives  61.7 us (79%)
  Pallas kernels  10.3 us (13%)
  waiting for transfers between devices  2.37 us (3%)
  starting transfers between devices  1.92 us (2%)
  local copies, waits for them, and re-layouts  0.91 us (1%)
    all_to_all x1, blocking collectives, per_device(): parts = lax.all_to_all(parts, TILE, 0, 0, tiled=True)  21.9 us
    all_to_all x1, blocking collectives, per_device(): got = lax.all_to_all(pay, MEM, 0, 0, tiled=True)  16.4 us
    all_to_all x1, blocking collectives, per_device(): back = lax.all_to_all(back, MEM, 0, 0, tiled=True)  13.2 us
    all_gather x1, blocking collectives, per_device(): chip = lax.all_gather(rows, 'c', axis=0, tiled=True)  8.47 us
    pallas_call x1, Pallas kernels, per_device(): kernel_call(denoise_kernel, shaped((PEERS, 32, 128)), [pltpu.VMEM((14, 2,...  5.72 us
    ppermute x1, waiting for transfers between devices, per_device(): lax.ppermute(lax.dynamic_slice_in_dim(chip, 3 * c, 5, axis=0), TILE, across)  2.37 us
    pallas_call x1, Pallas kernels, per_device(): pl.pallas_call(inner_kernel, out_shape=(shaped((2, 8, PAIRS, 256)), shape...  2.32 us
    ppermute x1, starting transfers between devices, per_device(): lax.ppermute(lax.dynamic_slice_in_dim(chip, 3 * c, 5, axis=0), TILE, across)  1.92 us
  transfers between devices with their start and end apart: 1, of which 1 were waited for; matrix products, arithmetic and copies ran while one was open for 0% of the time, Pallas kernels for 3%

profile of v3, /device:TPU:1, one launch (start us, length us, event | category | flops | bytes accessed | tf_op | source)
XLA Modules:
  0.0 77.9 jit_solution(3529428192632138750)
XLA Ops:
  0.6 0.0 copy-start
  0.6 0.9 %copy-done = bf16[2,4,8192]{2,1,0:T(4,128)(2,1)S(1)} copy-done((bf16[2,4,8192]{2,1,0:T(4,128)(2,1)S(1)}, bf16[2,4,8192]{2,1,0:T(4,128)(2,1)}, u32[]{:S(2)}) %copy-start) | copy-done | bytes 131096
  1.6 8.5 %all_gather.6.chip_ref = bf16[8,2,64,128]{3,2,1,0:T(8,128)(2,1)S(1)} all-gather(bf16[4,2,64,128]{3,2,1,0:T(8,128)(2,1)S(1)} %shard_map.86), channel_id=1, replica_groups=mesh['y'=8,'x'=4,'z'=8,'c'=2] {'c'}, dimensions={0}, use_global_device_ids=true | all-gather | bytes 393216 | tf_op jit(solution)/shard_map/all_gather | solution.py:309
  10.1 1.9 %collective-permute-start = (bf16[5,2,64,128]{3,2,1,0:T(8,128)(2,1)S(1)}, bf16[5,2,64,128]{3,2,1,0:T(8,128)(2,1)S(1)}, u32[]{:S(2)}, u32[]{:S(2)}) collective-permute-start(bf16[5,2,64,128]{3,2,1,0:T(8,128)(2,1)S(1)} %constant_dynamic-slice_fusion.1), channel_id=1, source_target_pairs={{1,2},{2,1},{3,4},{4,3},{5,6},{6,5},{7,8},{8,7},{9,10},{10,9},{11,... | collective-permute-start | bytes 491528 | tf_op jit(solution)/shard_map/ppermute | solution.py:310
  12.0 2.3 %shard_map.87 = (bf16[2,8,64,256]{3,2,1,0:T(8,128)(2,1)S(1)}, bf16[2,6,64,512]{3,2,1,0:T(8,128)(2,1)S(1)}, bf16[2,768,512]{2,1,0:T(8,128)(2,1)S(1)}, bf16[2,256,...) custom-call(bf16[8,2,64,128]{3,2,1,0:T(8,128)(2,1)S(1)} %all_gather., ...), custom_call_target="tpu_custom_call" | custom-call | flops 1000000000 | bytes 6000000 | tf_op jit(solution)/shard_map/pallas_call | solution.py:311
  14.3 2.4 %collective-permute-done.outer_ref = bf16[5,2,64,128]{3,2,1,0:T(8,128)(2,1)S(1)} collective-permute-done((bf16[5,2,64,128]{3,2,1,0:T(8,128)(2,1)S(1)}, bf16[5,2,64,128]{3,2,1,0:T(8,128)(2,1)S(1)}, u32[]{:S(2)}, u32[]{:S(2)}) %collective-permute-start) | collective-permute-done | bytes 163872 | tf_op jit(solution)/shard_map/ppermute | solution.py:310
  16.7 1.8 %all_gather.7.edge_ref = bf16[2,2,64,128]{3,2,1,0:T(8,128)(2,1)S(1)} all-gather(bf16[1,2,64,128]{3,2,1,0:T(8,128)(2,1)S(1)} %constant_dynamic-slice_fusion), channel_id=1, replica_groups=mesh['y'=8,'x'=4,'z'=8,'c'=2] {'c'}, dimensions={0}, use_global_device_ids=true | all-gather | bytes 98304 | tf_op jit(solution)/shard_map/all_gather | solution.py:329
  18.6 5.7 %shard_map.88 = bf16[32,32,128]{2,1,0:T(8,128)(2,1)S(1)} custom-call(bf16[8,2,64,128]{3,2,1,0:T(8,128)(2,1)S(1)} %all_gather.6.chip_ref, bf16[5,2,64,128]{3,2,1,0:T(8,128)(2,1)S(1)} %collective-permute-done.outer_ref, bf16[2,2,64,128]{3,2,1,0:T(8,128)(2,1)S(1)} %all_gather.7.edge_ref, bf16[2,8,64,256]{3,2,1,0:T(8,128)(2,1)S(1)} %get-tuple-element.11.a_part, ...), custom_call_target="tpu_custom_call" | custom-call | flops 4000000000 | bytes 4300000 | tf_op jit(solution)/shard_map/pallas_call | solution.py:330
  24.3 16.4 %all_to_all.15.got_ref = bf16[32,32,128]{2,1,0:T(8,128)(2,1)S(1)} all-to-all(bf16[32,32,128]{2,1,0:T(8,128)(2,1)S(1)} %shard_map.88), channel_id=1, replica_groups=mesh['y'=8,'x'=4,'z'=8,'c'=2] {'y','x'}, dimensions={0} | all-to-all | bytes 524288 | tf_op jit(solution)/shard_map/all_to_all | solution.py:342
  40.6 0.8 %shard_map.89 = bf16[16,32,128]{2,1,0:T(8,128)(2,1)S(1)} custom-call(bf16[32,32,128]{2,1,0:T(8,128)(2,1)S(1)} %all_to_all.15.got_ref, f32[24,128]{1,0:T(8,128)S(1)} %get-tuple-element.17.sides_ref), custom_call_target="tpu_custom_call" | custom-call | bytes 700000 | tf_op jit(solution)/shard_map/pallas_call | solution.py:344
  41.4 21.9 %all_to_all.16.parts_ref = bf16[16,32,128]{2,1,0:T(8,128)(2,1)S(1)} all-to-all(bf16[16,32,128]{2,1,0:T(8,128)(2,1)S(1)} %shard_map.89), channel_id=1, replica_groups=mesh['y'=8,'x'=4,'z'=8,'c'=2] {'z','c'}, dimensions={0} | all-to-all | bytes 262144 | tf_op jit(solution)/shard_map/all_to_all | solution.py:347
  63.3 0.7 shard_map.90
  64.0 13.2 %all_to_all.17.got_ref = bf16[32,16,128]{2,1,0:T(8,128)(2,1)S(1)} all-to-all(bf16[32,16,128]{2,1,0:T(8,128)(2,1)S(1)} %get-tuple-element.18), channel_id=1, replica_groups=mesh['y'=8,'x'=4,'z'=8,'c'=2] {'y','x'}, dimensions={0} | all-to-all | bytes 262144 | tf_op jit(solution)/shard_map/all_to_all | solution.py:352
  77.2 0.7 shard_map.91
  (3 shorter events, 0.1 us)
Async XLA Ops:
  0.6 0.9 %copy-start = (bf16[2,4,8192]{2,1,0:T(4,128)(2,1)S(1)}, bf16[2,4,8192]{2,1,0:T(4,128)(2,1)}, u32[]{:S(2)}) copy-start(bf16[2,4,8192]{2,1,0:T(4,128)(2,1)} %x_ref.1) | copy-start | bytes 393220
  10.1 6.6 %collective-permute-start = (bf16[5,2,64,128]{3,2,1,0:T(8,128)(2,1)S(1)}, bf16[5,2,64,128]{3,2,1,0:T(8,128)(2,1)S(1)}, u32[]{:S(2)}, u32[]{:S(2)}) collective-permute-start(bf16[5,2,64,128]{3,2,1,0:T(8,128)(2,1)S(1)} %constant_dynamic-slice_fusion.1), channel_id=1, source_target_pairs={{1,2},{2,1},{3,4},{4,3},{5,6},{6,5},{7,8},{8,7},{9,10},{10,9},{11,... | collective-permute-start | bytes 491528 | tf_op jit(solution)/shard_map/ppermute | solution.py:310

commit v4 on v3

--- a/solution.py
+++ b/solution.py
@@ -37,13 +37,17 @@
     return jax.ShapeDtypeStruct(shape, dtype)
 
 
-def rows_kernel(x_ref, rows_ref, flat):
-    for m in range(2):
-        for t in range(PAIRS):
-            flat[256 * m + 4 * t : 256 * m + 4 * t + 4, :] = x_ref[m, :, 128 * t : 128 * t + 128].astype(F32)
-    for m in range(2):
-        for r in range(4):
-            rows_ref[r, m] = flat[pl.ds(256 * m + r, PAIRS, stride=4), :].astype(BF16)
+def rows_kernel(x_ref, chip_ref, five_ref, one_ref, flat):
+    c = lax.axis_index("c")
+    for k in range(2):
+        for m in range(2):
+            for t in range(PAIRS):
+                flat[256 * m + 4 * t : 256 * m + 4 * t + 4, :] = x_ref[k, m, :, 128 * t : 128 * t + 128].astype(F32)
+        for m in range(2):
+            for r in range(4):
+                chip_ref[4 * k + r, m] = flat[pl.ds(256 * m + r, PAIRS, stride=4), :].astype(BF16)
+    five_ref[...] = chip_ref[pl.ds(3 * c, 5)]
+    one_ref[...] = chip_ref[7 * c]
 
 
 def spread_weights(in_ref, out_ref, seen_ref, first_ref, second_ref, obs_ref):
@@ -122,6 +126,15 @@
     )
 
 
+def updated(left, weight, current):
+    count = current.shape[0]
+    y = lax.dot_general(left, weight, NT, preferred_element_type=F32)
+    own = y[:, 0:128].reshape(count, PAIRS, 128)
+    side = y[:, 128:256].reshape(count, PAIRS, 128)
+    lower = lax.broadcasted_iota(jnp.int32, side.shape, 2) < 64
+    return current.astype(F32) + own + beside(side, lower)[1]
+
+
 def by_channel(values_ref, precision_ref, sides_ref):
     own = lax.broadcasted_iota(jnp.int32, (8, 256), 1) % 8 == lax.broadcasted_iota(jnp.int32, (8, 256), 0)
     spread = [
@@ -142,7 +155,7 @@
 
 
 def inner_kernel(chip_ref, in_hbm, out_hbm, seen_hbm, cells_hbm, values_hbm, precision_hbm,
-                 a_ref, h_ref, w1_ref, w2_ref, obs_ref, pick_ref, sides_ref,
+                 a_ref, h_ref, x1_ref, a2_ref, h2_ref, w1_ref, w2_ref, obs_ref, pick_ref, sides_ref,
                  in_ref, out_ref, seen_ref, cells_ref, values_ref, precision_ref, sems):
     sources = (cells_hbm, values_hbm, precision_hbm, seen_hbm, in_hbm, out_hbm)
     targets = (cells_ref, values_ref, precision_ref, seen_ref, in_ref, out_ref)
@@ -170,63 +183,72 @@
         for row in (0, 3):
             hidden = hidden_of(taps_of(a_ref, m, row, 3), w1_ref[0])
             h_ref[m, row : row + 3] = hidden.astype(BF16).reshape(3, PAIRS, 512)
-
-
-def denoise_kernel(chip_ref, outer_ref, edge_ref, a_part, h_part, w1_ref, w2_ref, obs_ref, pick_ref, sides_ref,
-                   pay_ref, x_ref, a_ref, h_ref, flat, sems):
+    for m in range(2):
+        x1_ref[:, m] = updated(taps_of(h_ref, m, 0, 4), w2_ref[0], chip_ref[2:6, m]).astype(BF16)
+        patches(a2_ref, m, 0, x1_ref[:, m], norm)
+    for m in range(2):
+        h2_ref[m] = hidden_of(taps_of(a2_ref, m, 0, 2), w1_ref[1]).astype(BF16).reshape(2, PAIRS, 512)
+
+
+def denoise_kernel(chip_ref, five_ref, one_ref, a_part, h_part, x1_part, a2_part, h2_part, w1_ref, w2_ref, obs_ref,
+                   pick_ref, sides_ref, pay_ref, x_ref, a_ref, h_ref, x1_ref, a2_ref, h2_ref, x2_ref, flat, sems):
     c = lax.axis_index("c")
     tile = 2 * lax.axis_index("z") + c
     first = jnp.where(tile == 0, 0.0, 1.0).astype(F32)
     last = jnp.where(tile == 15, 0.0, 1.0).astype(F32)
     start = 5 - 4 * c
-    moves = [
-        pltpu.make_async_copy(a_part.at[m], a_ref.at[m, pl.ds(start, 8)], sems.at[m]) for m in range(2)
-    ] + [
-        pltpu.make_async_copy(h_part.at[m], h_ref.at[m, pl.ds(start, 6)], sems.at[2 + m]) for m in range(2)
-    ] + [pltpu.make_async_copy(chip_ref, x_ref.at[pl.ds(start, 8)], sems.at[4])]
+    pairs = [(chip_ref, x_ref.at[pl.ds(start, 8)]), (x1_part, x1_ref.at[pl.ds(start, 4)])]
+    for m in range(2):
+        for k in (0, 6):
+            pairs.append((a_part.at[m, pl.ds(k, 2)], a_ref.at[m, pl.ds(start + k, 2)]))
+        for k in (0, 4):
+            pairs.append((h_part.at[m, pl.ds(k, 2)], h_ref.at[m, pl.ds(start + k, 2)]))
+        pairs.append((a2_part.at[m], a2_ref.at[m, pl.ds(start, 4)]))
+        pairs.append((h2_part.at[m], h2_ref.at[m, pl.ds(start, 2)]))
+    moves = [pltpu.make_async_copy(source, target, sems.at[i]) for i, (source, target) in enumerate(pairs)]
     for move in moves:
         move.start()
     norm = mean_over_channels()
-    edge = edge_ref[1 - c]
-    for m in range(2):
-        patches(a_ref, m, 9 * c, outer_ref[:, m], norm)
-        patches(a_ref, m, 13 - 13 * c, edge[m : m + 1], norm)
-    x_ref[pl.ds(9 * c, 5)] = outer_ref[...]
-    x_ref[13 - 13 * c] = edge
+    for m in range(2):
+        patches(a_ref, m, 9 * c, five_ref[:, m], norm)
+        patches(a_ref, m, 13 - 13 * c, one_ref[m : m + 1], norm)
+    x_ref[pl.ds(9 * c, 5)] = five_ref[...]
+    x_ref[13 - 13 * c] = one_ref[...]
     for move in moves:
         move.wait()
-    upper = c == 1
-    group = {q: jnp.where(upper, last if q else 1.0, first if q < 4 else 1.0) for q in range(5)}
+
+    def edges(low, high):
+        group = {}
+        for q in range(5):
+            if q < low or q >= high:
+                group[q] = jnp.where(c == 1, last if q >= high else 1.0, first if q < low else 1.0)
+        return group
+
+    def split(values, factors):
+        width = values.shape[1]
+        rows = values.reshape(6, PAIRS, width)
+        return scaled_rows(rows[0:5], factors).astype(BF16), rows[5].astype(BF16)
+
     for m in range(2):
         left = jnp.concatenate([taps_of(a_ref, m, 7 * c, 5), taps_of(a_ref, m, 11 - 11 * c, 1)], axis=0)
-        hidden = hidden_of(left, w1_ref[0])
-        outer = scaled_rows(hidden[0 : 5 * PAIRS].reshape(5, PAIRS, 512), group)
-        h_ref[m, pl.ds(7 * c, 5)] = outer.astype(BF16)
-        h_ref[m, 11 - 11 * c] = hidden[5 * PAIRS :].astype(BF16)
-
-    def finish(layer, m, kept, step, factors):
-        for row in range(0, kept, step):
-            y = lax.dot_general(taps_of(h_ref, m, row, step), w2_ref[layer], NT, preferred_element_type=F32)
-            own = y[:, 0:128].reshape(step, PAIRS, 128)
-            side = y[:, 128:256].reshape(step, PAIRS, 128)
-            lower = lax.broadcasted_iota(jnp.int32, side.shape, 2) < 64
-            total = x_ref[row + 2 : row + 2 + step, m].astype(F32) + own + beside(side, lower)[1]
-            total = scaled_rows(total, {i - row: f for i, f in factors.items() if row <= i < row + step})
-            x_ref[row : row + step, m] = total.astype(BF16)
-
-    edges = {**{i: first for i in range(3)}, **{i: last for i in range(7, 10)}}
-    for m in range(2):
-        finish(0, m, 10, 5, edges)
-    for m in range(2):
-        for row in (0, 5):
-            patches(a_ref, m, row, x_ref[row : row + 5, m], norm)
-        for row, factors in ((0, {0: first, 1: first}), (4, {2: last, 3: last})):
-            hidden = hidden_of(taps_of(a_ref, m, row, 4), w1_ref[1]).reshape(4, PAIRS, 512)
-            h_ref[m, row : row + 4] = scaled_rows(hidden, factors).astype(BF16)
+        h_ref[m, pl.ds(7 * c, 5)], h_ref[m, 11 - 11 * c] = split(hidden_of(left, w1_ref[0]), edges(4, 1))
+    for m in range(2):
+        left = jnp.concatenate([taps_of(h_ref, m, 5 * c, 5), taps_of(h_ref, m, 9 - 9 * c, 1)], axis=0)
+        current = jnp.concatenate([x_ref[pl.ds(5 * c + 2, 5), m], x_ref[pl.ds(11 - 9 * c, 1), m]], axis=0)
+        group, single = split(updated(left, w2_ref[0], current).reshape(6 * PAIRS, 128), edges(3, 2))
+        x1_ref[pl.ds(5 * c, 5), m] = group
+        x1_ref[9 - 9 * c, m] = single
+        patches(a2_ref, m, 5 * c, group, norm)
+        patches(a2_ref, m, 9 - 9 * c, single[None], norm)
+    for m in range(2):
+        left = jnp.concatenate([taps_of(a2_ref, m, 3 * c, 5), taps_of(a2_ref, m, 7 - 7 * c, 1)], axis=0)
+        h2_ref[m, pl.ds(3 * c, 5)], h2_ref[m, 7 - 7 * c] = split(hidden_of(left, w1_ref[1]), edges(2, 3))
     seen = []
     for m in range(2):
-        finish(1, m, 6, 3, {0: first, 5: last})
-        patches(a_ref, m, 0, x_ref[0:6, m], None)
+        for row, factors in ((0, {0: first}), (3, {2: last})):
+            rows = updated(taps_of(h2_ref, m, row, 3), w2_ref[1], x1_ref[row + 2 : row + 5, m])
+            x2_ref[row : row + 3, m] = scaled_rows(rows, factors).astype(BF16)
+        patches(a_ref, m, 0, x2_ref[:, m], None)
         y = lax.dot_general(obs_ref[...], a_ref[m, 0:6].reshape(384, 256), NT, preferred_element_type=F32)
         whole = jnp.concatenate([y[16 * dr : 16 * dr + 16] for dr in range(3)], axis=1)
         high = whole.astype(BF16).astype(F32)
@@ -237,7 +259,7 @@
     got = jnp.concatenate([jnp.where(odd, y[8:16], y[0:8]) for y in seen], axis=0).astype(BF16)
     for m in range(2):
         for r in range(4):
-            flat[pl.ds(256 * m + r, PAIRS, stride=4), :] = x_ref[1 + r, m].astype(F32)
+            flat[pl.ds(256 * m + r, PAIRS, stride=4), :] = x2_ref[1 + r, m].astype(F32)
     for p in range(PEERS):
         both = jnp.concatenate([flat[8 * p : 8 * p + 8], flat[256 + 8 * p : 256 + 8 * p + 8]], axis=0)
         pay_ref[p, 0:16] = both.astype(BF16)
@@ -248,24 +270,24 @@
     for p in range(PEERS):
         flat[16 * p : 16 * p + 16] = got_ref[p, 16:32].astype(F32)
     shape = (64, 128)
-    left, right = [], []
+    left, right, values = [], [], []
     for o in range(8):
         members = flat[pl.ds(o, 64, stride=8), :]
         mean = jnp.sum(members, axis=0, keepdims=True) * (1.0 / 64)
         left.append((members - mean) * jnp.broadcast_to(sides_ref[8 + o : 9 + o], shape))
-        right.append(jnp.broadcast_to(sides_ref[o : o + 1], shape) - members)
+        right.append(members.astype(BF16))
+        values.append(left[-1] * jnp.broadcast_to(sides_ref[o : o + 1], shape))
+    offset = jnp.sum(functools.reduce(jnp.add, values), axis=1, keepdims=True)
     left = jnp.concatenate(left, axis=1)
     right = jnp.concatenate(right, axis=1)
-    none = jnp.zeros_like(right)
-    total = lax.dot_general(
-        left[0:32], jnp.concatenate([right, none], axis=0), NT, precision=lax.Precision.HIGHEST,
-        preferred_element_type=F32,
-    ) + lax.dot_general(
-        left[32:64], jnp.concatenate([none, right], axis=0), NT, precision=lax.Precision.HIGHEST,
-        preferred_element_type=F32,
-    )
+    high = left.astype(BF16)
+    halves = jnp.concatenate([high, (left - high.astype(F32)).astype(BF16)], axis=0)
+    product = lax.dot_general(halves, jnp.concatenate([right, right], axis=0), NT, preferred_element_type=F32)
+    total = offset - (product[0:64] + product[64:128])
+    lower = lax.broadcasted_iota(jnp.int32, (32, 128), 1) < 64
+    packed = jnp.where(lower, total[0:32], total[32:64]).astype(BF16)
     for t in range(16):
-        out_ref[t] = total.astype(BF16)
+        out_ref[t] = packed
 
 
 def update_kernel(got_ref, parts_ref, covariance_ref, back_ref, flat):
@@ -299,19 +321,21 @@
 
 
 def per_device(latents, in_weight, out_weight, observe_weight, obs_cells, obs_values, obs_precision):
-    c = lax.axis_index("c")
     across = [pair for z in range(7) for pair in ((2 * z + 1, 2 * z + 2), (2 * z + 2, 2 * z + 1))]
+    along = [pair for z in range(7) for pair in ((2 * z + 1, 2 * z + 3), (2 * z + 2, 2 * z))]
     vmem = pl.BlockSpec(memory_space=pltpu.VMEM)
     hbm = pl.BlockSpec(memory_space=pltpu.HBM)
-    rows = kernel_call(
-        rows_kernel, shaped((4, 2, PAIRS, 128)), [pltpu.VMEM((512, 128), F32)], moved=300_000,
-    )(latents)
-    chip = lax.all_gather(rows, "c", axis=0, tiled=True)
-    outer = lax.ppermute(lax.dynamic_slice_in_dim(chip, 3 * c, 5, axis=0), TILE, across)
-    a_part, h_part, first, second, obs, pick, sides = pl.pallas_call(
+    chip, five, one = kernel_call(
+        rows_kernel, (shaped((8, 2, PAIRS, 128)), shaped((5, 2, PAIRS, 128)), shaped((2, PAIRS, 128))),
+        [pltpu.VMEM((512, 128), F32)], moved=300_000,
+    )(lax.all_gather(latents, "c"))
+    five = lax.ppermute(five, TILE, across)
+    one = lax.ppermute(one, TILE, along)
+    *parts, sides = pl.pallas_call(
         inner_kernel,
         out_shape=(
-            shaped((2, 8, PAIRS, 256)), shaped((2, 6, PAIRS, 512)), shaped((2, 768, 512)), shaped((2, 256, 1536)),
+            shaped((2, 8, PAIRS, 256)), shaped((2, 6, PAIRS, 512)), shaped((4, 2, PAIRS, 128)),
+            shaped((2, 4, PAIRS, 256)), shaped((2, 2, PAIRS, 512)), shaped((2, 768, 512)), shaped((2, 256, 1536)),
             shaped((48, 256)), shaped((1152, 128)), shaped((24, 128), F32),
         ),
         in_specs=[vmem] + [hbm] * 6,
@@ -320,13 +344,12 @@
             pltpu.VMEM((4, 32), jnp.int32), pltpu.VMEM((4, 256), F32), pltpu.VMEM((4, 256), F32),
             pltpu.SemaphoreType.DMA((6,)),
         ],
-        cost_estimate=pl.CostEstimate(flops=1_000_000_000, bytes_accessed=6_000_000, transcendentals=0),
+        cost_estimate=pl.CostEstimate(flops=2_000_000_000, bytes_accessed=6_000_000, transcendentals=0),
         compiler_params=pltpu.CompilerParams(vmem_limit_bytes=16 * 1024 * 1024),
     )(chip, *(pltpu.with_memory_space_constraint(v, pltpu.HBM) for v in (
         in_weight, jnp.transpose(out_weight, (0, 2, 1)), jnp.transpose(observe_weight), obs_cells, obs_values,
         obs_precision,
     )))
-    edge = lax.all_gather(lax.dynamic_slice_in_dim(outer, 4 * (1 - c), 1, axis=0), "c", axis=0, tiled=True)
     pay = kernel_call(
         denoise_kernel,
         shaped((PEERS, 32, 128)),
@@ -334,11 +357,15 @@
             pltpu.VMEM((14, 2, PAIRS, 128), BF16),
             pltpu.VMEM((2, 14, PAIRS, 256), BF16),
             pltpu.VMEM((2, 12, PAIRS, 512), BF16),
+            pltpu.VMEM((10, 2, PAIRS, 128), BF16),
+            pltpu.VMEM((2, 10, PAIRS, 256), BF16),
+            pltpu.VMEM((2, 8, PAIRS, 512), BF16),
+            pltpu.VMEM((6, 2, PAIRS, 128), BF16),
             pltpu.VMEM((512, 128), F32),
-            pltpu.SemaphoreType.DMA((5,)),
+            pltpu.SemaphoreType.DMA((14,)),
         ],
-        flops=4_000_000_000, moved=4_300_000,
-    )(chip, outer, edge, a_part, h_part, first, second, obs, pick, sides)
+        flops=3_000_000_000, moved=4_300_000,
+    )(chip, five, one, *parts, sides)
     got = lax.all_to_all(pay, MEM, 0, 0, tiled=True)
 
     parts = kernel_call(

time: 78.2 us -> 78.6 us (level)
  starting transfers between devices: 1.92 us -> 5.81 us
  blocking collectives: 61.7 us -> 59.2 us
  Pallas kernels: 10.3 us -> 12.7 us
  waiting for transfers between devices: 2.37 us -> 0.01 us
  local copies, waits for them, and re-layouts: 0.91 us -> 0 us
    ppermute x1 -> x2, starting transfers between devices: 1.92 us -> 5.81 us  [the longest x1 4.52 us: per_device(): five = lax.ppermute(five, TILE, across)]
    ppermute x1 -> x2, waiting for transfers between devices: 2.37 us -> 0.01 us  [the longest x1 0.01 us: per_device(): one = lax.ppermute(one, TILE, along)]
    all_gather x2 -> x1, blocking collectives: 10.3 us -> 8.68 us  [per_device(): lax.all_gather(latents, 'c')]
    pallas_call x1, Pallas kernels: 5.72 us -> 7.26 us  [per_device(): kernel_call(denoise_kernel, shaped((PEERS, 32, 128)), [pltpu.VMEM((14, 2,...]
    pallas_call x1, Pallas kernels: 2.32 us -> 3.59 us  [per_device(): pl.pallas_call(inner_kernel, out_shape=(shaped((2, 8, PAIRS, 256)), shape...]
    unnamed x2 -> x0, local copies, waits for them, and re-layouts: 0.9 us -> none
  transfers between devices with their start and end apart: 1 -> 2, of which waited for: 1 -> 0; matrix products, arithmetic and copies ran while one was open for 0% -> 0% of each run, Pallas kernels for 3% -> 5%
where the time goes in v4:
time: 78.6 us; the launch traced here: 78.4 us
  blocking collectives  59.2 us (75%)
  Pallas kernels  12.7 us (16%)
  starting transfers between devices  5.81 us (7%)
    all_to_all x1, blocking collectives, per_device(): parts = lax.all_to_all(parts, TILE, 0, 0, tiled=True)  21.5 us
    all_to_all x1, blocking collectives, per_device(): got = lax.all_to_all(pay, MEM, 0, 0, tiled=True)  15.8 us
    all_to_all x1, blocking collectives, per_device(): back = lax.all_to_all(back, MEM, 0, 0, tiled=True)  13.2 us
    all_gather x1, blocking collectives, per_device(): lax.all_gather(latents, 'c')  8.68 us
    pallas_call x1, Pallas kernels, per_device(): kernel_call(denoise_kernel, shaped((PEERS, 32, 128)), [pltpu.VMEM((14, 2,...  7.26 us
    ppermute x1, starting transfers between devices, per_device(): five = lax.ppermute(five, TILE, across)  4.52 us
    pallas_call x1, Pallas kernels, per_device(): pl.pallas_call(inner_kernel, out_shape=(shaped((2, 8, PAIRS, 256)), shape...  3.59 us
  transfers between devices with their start and end apart: 2, of which 0 were waited for; matrix products, arithmetic and copies ran while one was open for 0% of the time, Pallas kernels for 5%

profile of v4, /device:TPU:1, one launch (start us, length us, event | category | flops | bytes accessed | tf_op | source)
XLA Modules:
  0.0 78.4 jit_solution(8570472504726538338)
XLA Ops:
  0.6 8.7 %all-gather = bf16[4,4,8192]{2,1,0:T(4,128)(2,1)S(1)} all-gather(bf16[2,4,8192]{2,1,0:T(4,128)(2,1)} %param.7), channel_id=2, replica_groups=mesh['y'=8,'x'=4,'z'=8,'c'=2] {'c'}, dimensions={0}, use_global_device_ids=true | all-gather | bytes 393216 | tf_op jit(solution)/shard_map/all_gather | solution.py:331
  9.3 0.1 shard_map.86
  9.4 1.3 %collective-permute-start.1 = (bf16[2,64,128]{2,1,0:T(8,128)(2,1)S(1)}, bf16[2,64,128]{2,1,0:T(8,128)(2,1)S(1)}, u32[]{:S(2)}, u32[]{:S(2)}) collective-permute-start(bf16[2,64,128]{2,1,0:T(8,128)(2,1)S(1)} %get-tuple-element.19), channel_id=1, source_target_pairs={{1,3},{2,0},{3,5},{4,2},{5,7},{6,4},{7,9},{8,6},{9,11},{10,8},{11,... | collective-permute-start | bytes 98312 | tf_op jit(solution)/shard_map/ppermute | solution.py:333
  10.7 4.5 %collective-permute-start = (bf16[5,2,64,128]{3,2,1,0:T(8,128)(2,1)S(1)}, bf16[5,2,64,128]{3,2,1,0:T(8,128)(2,1)S(1)}, u32[]{:S(2)}, u32[]{:S(2)}) collective-permute-start(bf16[5,2,64,128]{3,2,1,0:T(8,128)(2,1)S(1)} %get-tuple-element.18), channel_id=1, source_target_pairs={{1,2},{2,1},{3,4},{4,3},{5,6},{6,5},{7,8},{8,7},{9,10},{10,9},{11,... | collective-permute-start | bytes 491528 | tf_op jit(solution)/shard_map/ppermute | solution.py:332
  15.2 3.6 %shard_map.87 = (bf16[2,8,64,256]{3,2,1,0:T(8,128)(2,1)S(1)}, bf16[2,6,64,512]{3,2,1,0:T(8,128)(2,1)S(1)}, bf16[4,2,64,128]{3,2,1,0:T(8,128)(2,1)S(1)}, bf16[2,4...) custom-call(bf16[8,2,64,128]{3,2,1,0:T(8,128)(2,1)S(1)} %get-tuple-e, ...), custom_call_target="tpu_custom_call" | custom-call | flops 2000000000 | bytes 6000000 | tf_op jit(solution)/shard_map/pallas_call | solution.py:334
  18.8 0.0 collective-permute-done.1.one_ref
  18.9 0.0 collective-permute-done.five_ref
  18.9 7.3 %shard_map.88 = bf16[32,32,128]{2,1,0:T(8,128)(2,1)S(1)} custom-call(bf16[8,2,64,128]{3,2,1,0:T(8,128)(2,1)S(1)} %get-tuple-element.17.chip_ref, bf16[5,2,64,128]{3,2,1,0:T(8,128)(2,1)S(1)} %collective-permute-done.five_ref, bf16[2,64,128]{2,1,0:T(8,128)(2,1)S(1)} %collective-permute-done.1.one_ref, bf16[2,8,64,256]{3,2,1,0:T(8,128)(2,1)S(1)} %get-tuple-element.20.a_part, ...), custom_call_target="tpu_custom_call" | custom-call | flops 3000000000 | bytes 4300000 | tf_op jit(solution)/shard_map/pallas_call | solution.py:353
  26.1 15.8 %all_to_all.15.got_ref = bf16[32,32,128]{2,1,0:T(8,128)(2,1)S(1)} all-to-all(bf16[32,32,128]{2,1,0:T(8,128)(2,1)S(1)} %shard_map.88), channel_id=1, replica_groups=mesh['y'=8,'x'=4,'z'=8,'c'=2] {'y','x'}, dimensions={0} | all-to-all | bytes 524288 | tf_op jit(solution)/shard_map/all_to_all | solution.py:369
  41.9 0.3 shard_map.89
  42.2 21.5 %all_to_all.16.parts_ref = bf16[16,32,128]{2,1,0:T(8,128)(2,1)S(1)} all-to-all(bf16[16,32,128]{2,1,0:T(8,128)(2,1)S(1)} %shard_map.89), channel_id=1, replica_groups=mesh['y'=8,'x'=4,'z'=8,'c'=2] {'z','c'}, dimensions={0} | all-to-all | bytes 262144 | tf_op jit(solution)/shard_map/all_to_all | solution.py:374
  63.7 0.7 shard_map.90
  64.4 13.2 %all_to_all.17.got_ref = bf16[32,16,128]{2,1,0:T(8,128)(2,1)S(1)} all-to-all(bf16[32,16,128]{2,1,0:T(8,128)(2,1)S(1)} %get-tuple-element.30), channel_id=1, replica_groups=mesh['y'=8,'x'=4,'z'=8,'c'=2] {'y','x'}, dimensions={0} | all-to-all | bytes 262144 | tf_op jit(solution)/shard_map/all_to_all | solution.py:379
  77.6 0.7 shard_map.91
Async XLA Ops:
  9.4 9.4 %collective-permute-start.1 = (bf16[2,64,128]{2,1,0:T(8,128)(2,1)S(1)}, bf16[2,64,128]{2,1,0:T(8,128)(2,1)S(1)}, u32[]{:S(2)}, u32[]{:S(2)}) collective-permute-start(bf16[2,64,128]{2,1,0:T(8,128)(2,1)S(1)} %get-tuple-element.19), channel_id=1, source_target_pairs={{1,3},{2,0},{3,5},{4,2},{5,7},{6,4},{7,9},{8,6},{9,11},{10,8},{11,... | collective-permute-start | bytes 98312 | tf_op jit(solution)/shard_map/ppermute | solution.py:333
  10.7 8.1 %collective-permute-start = (bf16[5,2,64,128]{3,2,1,0:T(8,128)(2,1)S(1)}, bf16[5,2,64,128]{3,2,1,0:T(8,128)(2,1)S(1)}, u32[]{:S(2)}, u32[]{:S(2)}) collective-permute-start(bf16[5,2,64,128]{3,2,1,0:T(8,128)(2,1)S(1)} %get-tuple-element.18), channel_id=1, source_target_pairs={{1,2},{2,1},{3,4},{4,3},{5,6},{6,5},{7,8},{8,7},{9,10},{10,9},{11,... | collective-permute-start | bytes 491528 | tf_op jit(solution)/shard_map/ppermute | solution.py:332

commit v5 on v4

--- a/solution.py
+++ b/solution.py
@@ -37,7 +37,7 @@
     return jax.ShapeDtypeStruct(shape, dtype)
 
 
-def rows_kernel(x_ref, chip_ref, five_ref, one_ref, flat):
+def rows_kernel(x_ref, chip_ref, five_ref, flat):
     c = lax.axis_index("c")
     for k in range(2):
         for m in range(2):
@@ -47,7 +47,6 @@
             for r in range(4):
                 chip_ref[4 * k + r, m] = flat[pl.ds(256 * m + r, PAIRS, stride=4), :].astype(BF16)
     five_ref[...] = chip_ref[pl.ds(3 * c, 5)]
-    one_ref[...] = chip_ref[7 * c]
 
 
 def spread_weights(in_ref, out_ref, seen_ref, first_ref, second_ref, obs_ref):
@@ -126,9 +125,14 @@
     )
 
 
-def updated(left, weight, current):
+def second(left, weight):
+    half = left.shape[1] // 2
+    return [lax.dot_general(left[:, k : k + half], weight[:, k : k + half], NT, preferred_element_type=F32) for k in (0, half)]
+
+
+def updated(products, current):
     count = current.shape[0]
-    y = lax.dot_general(left, weight, NT, preferred_element_type=F32)
+    y = products[0] + products[1]
     own = y[:, 0:128].reshape(count, PAIRS, 128)
     side = y[:, 128:256].reshape(count, PAIRS, 128)
     lower = lax.broadcasted_iota(jnp.int32, side.shape, 2) < 64
@@ -183,39 +187,35 @@
         for row in (0, 3):
             hidden = hidden_of(taps_of(a_ref, m, row, 3), w1_ref[0])
             h_ref[m, row : row + 3] = hidden.astype(BF16).reshape(3, PAIRS, 512)
-    for m in range(2):
-        x1_ref[:, m] = updated(taps_of(h_ref, m, 0, 4), w2_ref[0], chip_ref[2:6, m]).astype(BF16)
+    products = [second(taps_of(h_ref, m, 0, 4), w2_ref[0]) for m in range(2)]
+    for m in range(2):
+        x1_ref[:, m] = updated(products[m], chip_ref[2:6, m]).astype(BF16)
         patches(a2_ref, m, 0, x1_ref[:, m], norm)
     for m in range(2):
         h2_ref[m] = hidden_of(taps_of(a2_ref, m, 0, 2), w1_ref[1]).astype(BF16).reshape(2, PAIRS, 512)
 
 
 def denoise_kernel(chip_ref, five_ref, one_ref, a_part, h_part, x1_part, a2_part, h2_part, w1_ref, w2_ref, obs_ref,
-                   pick_ref, sides_ref, pay_ref, x_ref, a_ref, h_ref, x1_ref, a2_ref, h2_ref, x2_ref, flat, sems):
+                   pick_ref, sides_ref, pay_ref, x_ref, a_ref, h_ref, x1_ref, a2_ref, h2_ref, x2_ref, flat):
     c = lax.axis_index("c")
     tile = 2 * lax.axis_index("z") + c
     first = jnp.where(tile == 0, 0.0, 1.0).astype(F32)
     last = jnp.where(tile == 15, 0.0, 1.0).astype(F32)
     start = 5 - 4 * c
-    pairs = [(chip_ref, x_ref.at[pl.ds(start, 8)]), (x1_part, x1_ref.at[pl.ds(start, 4)])]
-    for m in range(2):
+    one = one_ref[1 - c]
+    norm = mean_over_channels()
+    for m in range(2):
+        patches(a_ref, m, 9 * c, five_ref[:, m], norm)
+        patches(a_ref, m, 13 - 13 * c, one[m : m + 1], norm)
         for k in (0, 6):
-            pairs.append((a_part.at[m, pl.ds(k, 2)], a_ref.at[m, pl.ds(start + k, 2)]))
+            a_ref[m, pl.ds(start + k, 2)] = a_part[m, k : k + 2]
         for k in (0, 4):
-            pairs.append((h_part.at[m, pl.ds(k, 2)], h_ref.at[m, pl.ds(start + k, 2)]))
-        pairs.append((a2_part.at[m], a2_ref.at[m, pl.ds(start, 4)]))
-        pairs.append((h2_part.at[m], h2_ref.at[m, pl.ds(start, 2)]))
-    moves = [pltpu.make_async_copy(source, target, sems.at[i]) for i, (source, target) in enumerate(pairs)]
-    for move in moves:
-        move.start()
-    norm = mean_over_channels()
-    for m in range(2):
-        patches(a_ref, m, 9 * c, five_ref[:, m], norm)
-        patches(a_ref, m, 13 - 13 * c, one_ref[m : m + 1], norm)
+            h_ref[m, pl.ds(start + k, 2)] = h_part[m, k : k + 2]
+        a2_ref[m, pl.ds(start, 4)] = a2_part[m]
+        h2_ref[m, pl.ds(start, 2)] = h2_part[m]
+    x_ref[pl.ds(start, 8)] = chip_ref[...]
+    x1_ref[pl.ds(start, 4)] = x1_part[...]
     x_ref[pl.ds(9 * c, 5)] = five_ref[...]
-    x_ref[13 - 13 * c] = one_ref[...]
-    for move in moves:
-        move.wait()
 
     def edges(low, high):
         group = {}
@@ -232,10 +232,13 @@
     for m in range(2):
         left = jnp.concatenate([taps_of(a_ref, m, 7 * c, 5), taps_of(a_ref, m, 11 - 11 * c, 1)], axis=0)
         h_ref[m, pl.ds(7 * c, 5)], h_ref[m, 11 - 11 * c] = split(hidden_of(left, w1_ref[0]), edges(4, 1))
+    products = []
     for m in range(2):
         left = jnp.concatenate([taps_of(h_ref, m, 5 * c, 5), taps_of(h_ref, m, 9 - 9 * c, 1)], axis=0)
+        products.append(second(left, w2_ref[0]))
+    for m in range(2):
         current = jnp.concatenate([x_ref[pl.ds(5 * c + 2, 5), m], x_ref[pl.ds(11 - 9 * c, 1), m]], axis=0)
-        group, single = split(updated(left, w2_ref[0], current).reshape(6 * PAIRS, 128), edges(3, 2))
+        group, single = split(updated(products[m], current).reshape(6 * PAIRS, 128), edges(3, 2))
         x1_ref[pl.ds(5 * c, 5), m] = group
         x1_ref[9 - 9 * c, m] = single
         patches(a2_ref, m, 5 * c, group, norm)
@@ -243,11 +246,10 @@
     for m in range(2):
         left = jnp.concatenate([taps_of(a2_ref, m, 3 * c, 5), taps_of(a2_ref, m, 7 - 7 * c, 1)], axis=0)
         h2_ref[m, pl.ds(3 * c, 5)], h2_ref[m, 7 - 7 * c] = split(hidden_of(left, w1_ref[1]), edges(2, 3))
+    products = [second(taps_of(h2_ref, m, 0, 6), w2_ref[1]) for m in range(2)]
     seen = []
     for m in range(2):
-        for row, factors in ((0, {0: first}), (3, {2: last})):
-            rows = updated(taps_of(h2_ref, m, row, 3), w2_ref[1], x1_ref[row + 2 : row + 5, m])
-            x2_ref[row : row + 3, m] = scaled_rows(rows, factors).astype(BF16)
+        x2_ref[:, m] = scaled_rows(updated(products[m], x1_ref[2:8, m]), {0: first, 5: last}).astype(BF16)
         patches(a_ref, m, 0, x2_ref[:, m], None)
         y = lax.dot_general(obs_ref[...], a_ref[m, 0:6].reshape(384, 256), NT, preferred_element_type=F32)
         whole = jnp.concatenate([y[16 * dr : 16 * dr + 16] for dr in range(3)], axis=1)
@@ -311,7 +313,8 @@
         back_ref[p] = flat[16 * p : 16 * p + 16].astype(BF16)
 
 
-def final_kernel(got_ref, out_ref):
+def final_kernel(got_ref, covariance_in, out_ref, covariance_ref):
+    covariance_ref[...] = covariance_in[...]
     for p in range(PEERS):
         values = got_ref[p].astype(F32)
         for m in range(2):
@@ -321,16 +324,15 @@
 
 
 def per_device(latents, in_weight, out_weight, observe_weight, obs_cells, obs_values, obs_precision):
+    c = lax.axis_index("c")
     across = [pair for z in range(7) for pair in ((2 * z + 1, 2 * z + 2), (2 * z + 2, 2 * z + 1))]
-    along = [pair for z in range(7) for pair in ((2 * z + 1, 2 * z + 3), (2 * z + 2, 2 * z))]
     vmem = pl.BlockSpec(memory_space=pltpu.VMEM)
     hbm = pl.BlockSpec(memory_space=pltpu.HBM)
-    chip, five, one = kernel_call(
-        rows_kernel, (shaped((8, 2, PAIRS, 128)), shaped((5, 2, PAIRS, 128)), shaped((2, PAIRS, 128))),
+    chip, five = kernel_call(
+        rows_kernel, (shaped((8, 2, PAIRS, 128)), shaped((5, 2, PAIRS, 128))),
         [pltpu.VMEM((512, 128), F32)], moved=300_000,
     )(lax.all_gather(latents, "c"))
     five = lax.ppermute(five, TILE, across)
-    one = lax.ppermute(one, TILE, along)
     *parts, sides = pl.pallas_call(
         inner_kernel,
         out_shape=(
@@ -350,6 +352,7 @@
         in_weight, jnp.transpose(out_weight, (0, 2, 1)), jnp.transpose(observe_weight), obs_cells, obs_values,
         obs_precision,
     )))
+    one = lax.all_gather(lax.dynamic_slice_in_dim(five, 4 * (1 - c), 1, axis=0), "c", axis=0, tiled=True)
     pay = kernel_call(
         denoise_kernel,
         shaped((PEERS, 32, 128)),
@@ -362,7 +365,6 @@
             pltpu.VMEM((2, 8, PAIRS, 512), BF16),
             pltpu.VMEM((6, 2, PAIRS, 128), BF16),
             pltpu.VMEM((512, 128), F32),
-            pltpu.SemaphoreType.DMA((14,)),
         ],
         flops=3_000_000_000, moved=4_300_000,
     )(chip, five, one, *parts, sides)
@@ -377,8 +379,7 @@
         moved=700_000,
     )(got, parts)
     back = lax.all_to_all(back, MEM, 0, 0, tiled=True)
-    analysis = kernel_call(final_kernel, shaped((2, 4, 8192), F32), moved=400_000)(back)
-    return analysis, covariance
+    return kernel_call(final_kernel, (shaped((2, 4, 8192), F32), shaped((64, 64), F32)), moved=400_000)(back, covariance)
 
 
 def solution(mesh):

time: 78.6 us -> 75.9 us (0.966)
  starting transfers between devices: 5.81 us -> 1.92 us
  Pallas kernels: 12.7 us -> 9.79 us
  blocking collectives: 59.2 us -> 62 us
  waiting for transfers between devices: 0.01 us -> 1.3 us
    ppermute x1, starting transfers between devices: 4.52 us -> 1.92 us  [per_device(): five = lax.ppermute(five, TILE, across)]
    pallas_call x1, Pallas kernels: 7.26 us -> 4.92 us  [per_device(): kernel_call(denoise_kernel, shaped((PEERS, 32, 128)), [pltpu.VMEM((14, 2,...]
    all_gather x0 -> x1, blocking collectives: none -> 1.84 us  [per_device(): lax.all_gather(lax.dynamic_slice_in_dim(five, 4 * (1 - c), 1, axis=0), 'c...]
    ppermute x1, waiting for transfers between devices: 0.01 us -> 1.3 us  [per_device(): five = lax.ppermute(five, TILE, across)]
    ppermute x1 -> x0, starting transfers between devices: 1.29 us -> none  [per_device(): one = lax.ppermute(one, TILE, along)]
    all_to_all x1, blocking collectives: 15.8 us -> 16.8 us  [per_device(): got = lax.all_to_all(pay, MEM, 0, 0, tiled=True)]
  transfers between devices with their start and end apart: 2 -> 1, of which waited for: 0 -> 1; matrix products, arithmetic and copies ran while one was open for 0% -> 0% of each run, Pallas kernels for 5% -> 4%
where the time goes in v5:
time: 75.9 us; the launch traced here: 75.7 us
  blocking collectives  62 us (82%)
  Pallas kernels  9.79 us (13%)
  starting transfers between devices  1.92 us (3%)
  waiting for transfers between devices  1.3 us (2%)
    all_to_all x1, blocking collectives, per_device(): parts = lax.all_to_all(parts, TILE, 0, 0, tiled=True)  21.4 us
    all_to_all x1, blocking collectives, per_device(): got = lax.all_to_all(pay, MEM, 0, 0, tiled=True)  16.8 us
    all_to_all x1, blocking collectives, per_device(): back = lax.all_to_all(back, MEM, 0, 0, tiled=True)  13.2 us
    all_gather x1, blocking collectives, per_device(): lax.all_gather(latents, 'c')  8.68 us
    pallas_call x1, Pallas kernels, per_device(): kernel_call(denoise_kernel, shaped((PEERS, 32, 128)), [pltpu.VMEM((14, 2,...  4.92 us
    pallas_call x1, Pallas kernels, per_device(): pl.pallas_call(inner_kernel, out_shape=(shaped((2, 8, PAIRS, 256)), shape...  3.39 us
    ppermute x1, starting transfers between devices, per_device(): five = lax.ppermute(five, TILE, across)  1.92 us
    all_gather x1, blocking collectives, per_device(): lax.all_gather(lax.dynamic_slice_in_dim(five, 4 * (1 - c), 1, axis=0), 'c...  1.84 us
  transfers between devices with their start and end apart: 1, of which 1 were waited for; matrix products, arithmetic and copies ran while one was open for 0% of the time, Pallas kernels for 4%

profile of v5, /device:TPU:1, one launch (start us, length us, event | category | flops | bytes accessed | tf_op | source)
XLA Modules:
  0.0 75.7 jit_solution(17868573810602600867)
XLA Ops:
  0.6 8.7 %all-gather = bf16[4,4,8192]{2,1,0:T(4,128)(2,1)S(1)} all-gather(bf16[2,4,8192]{2,1,0:T(4,128)(2,1)} %param.7), channel_id=2, replica_groups=mesh['y'=8,'x'=4,'z'=8,'c'=2] {'c'}, dimensions={0}, use_global_device_ids=true | all-gather | bytes 393216 | tf_op jit(solution)/shard_map/all_gather | solution.py:334
  9.3 0.1 shard_map.86
  9.4 1.9 %collective-permute-start = (bf16[5,2,64,128]{3,2,1,0:T(8,128)(2,1)S(1)}, bf16[5,2,64,128]{3,2,1,0:T(8,128)(2,1)S(1)}, u32[]{:S(2)}, u32[]{:S(2)}) collective-permute-start(bf16[5,2,64,128]{3,2,1,0:T(8,128)(2,1)S(1)} %get-tuple-element.17), channel_id=1, source_target_pairs={{1,2},{2,1},{3,4},{4,3},{5,6},{6,5},{7,8},{8,7},{9,10},{10,9},{11,... | collective-permute-start | bytes 491528 | tf_op jit(solution)/shard_map/ppermute | solution.py:335
  11.3 3.4 %shard_map.87 = (bf16[2,8,64,256]{3,2,1,0:T(8,128)(2,1)S(1)}, bf16[2,6,64,512]{3,2,1,0:T(8,128)(2,1)S(1)}, bf16[4,2,64,128]{3,2,1,0:T(8,128)(2,1)S(1)}, bf16[2,4...) custom-call(bf16[8,2,64,128]{3,2,1,0:T(8,128)(2,1)S(1)} %get-tuple-e, ...), custom_call_target="tpu_custom_call" | custom-call | flops 2000000000 | bytes 6000000 | tf_op jit(solution)/shard_map/pallas_call | solution.py:336
  14.8 1.3 %collective-permute-done.five_ref = bf16[5,2,64,128]{3,2,1,0:T(8,128)(2,1)S(1)} collective-permute-done((bf16[5,2,64,128]{3,2,1,0:T(8,128)(2,1)S(1)}, bf16[5,2,64,128]{3,2,1,0:T(8,128)(2,1)S(1)}, u32[]{:S(2)}, u32[]{:S(2)}) %collective-permute-start) | collective-permute-done | bytes 163872 | tf_op jit(solution)/shard_map/ppermute | solution.py:335
  16.1 1.8 %all_gather.11.one_ref = bf16[2,2,64,128]{3,2,1,0:T(8,128)(2,1)S(1)} all-gather(bf16[1,2,64,128]{3,2,1,0:T(8,128)(2,1)S(1)} %constant_dynamic-slice_fusion), channel_id=1, replica_groups=mesh['y'=8,'x'=4,'z'=8,'c'=2] {'c'}, dimensions={0}, use_global_device_ids=true | all-gather | bytes 98304 | tf_op jit(solution)/shard_map/all_gather | solution.py:355
  17.9 4.9 %shard_map.88 = bf16[32,32,128]{2,1,0:T(8,128)(2,1)S(1)} custom-call(bf16[8,2,64,128]{3,2,1,0:T(8,128)(2,1)S(1)} %get-tuple-element.16.chip_ref, bf16[5,2,64,128]{3,2,1,0:T(8,128)(2,1)S(1)} %collective-permute-done.five_ref, bf16[2,2,64,128]{3,2,1,0:T(8,128)(2,1)S(1)} %all_gather.11.one_ref, bf16[2,8,64,256]{3,2,1,0:T(8,128)(2,1)S(1)} %get-tuple-element.18.a_part, ...), custom_call_target="tpu_custom_call" | custom-call | flops 3000000000 | bytes 4300000 | tf_op jit(solution)/shard_map/pallas_call | solution.py:356
  22.8 16.8 %all_to_all.15.got_ref = bf16[32,32,128]{2,1,0:T(8,128)(2,1)S(1)} all-to-all(bf16[32,32,128]{2,1,0:T(8,128)(2,1)S(1)} %shard_map.88), channel_id=1, replica_groups=mesh['y'=8,'x'=4,'z'=8,'c'=2] {'y','x'}, dimensions={0} | all-to-all | bytes 524288 | tf_op jit(solution)/shard_map/all_to_all | solution.py:371
  39.7 0.3 shard_map.89
  39.9 21.4 %all_to_all.16.parts_ref = bf16[16,32,128]{2,1,0:T(8,128)(2,1)S(1)} all-to-all(bf16[16,32,128]{2,1,0:T(8,128)(2,1)S(1)} %shard_map.89), channel_id=1, replica_groups=mesh['y'=8,'x'=4,'z'=8,'c'=2] {'z','c'}, dimensions={0} | all-to-all | bytes 262144 | tf_op jit(solution)/shard_map/all_to_all | solution.py:376
  61.3 0.4 shard_map.90
  61.7 13.2 %all_to_all.17.got_ref = bf16[32,16,128]{2,1,0:T(8,128)(2,1)S(1)} all-to-all(bf16[32,16,128]{2,1,0:T(8,128)(2,1)S(1)} %get-tuple-element.28), channel_id=1, replica_groups=mesh['y'=8,'x'=4,'z'=8,'c'=2] {'y','x'}, dimensions={0} | all-to-all | bytes 262144 | tf_op jit(solution)/shard_map/all_to_all | solution.py:381
  74.9 0.7 shard_map.91
  (1 shorter events, 0.0 us)
Async XLA Ops:
  9.4 6.6 %collective-permute-start = (bf16[5,2,64,128]{3,2,1,0:T(8,128)(2,1)S(1)}, bf16[5,2,64,128]{3,2,1,0:T(8,128)(2,1)S(1)}, u32[]{:S(2)}, u32[]{:S(2)}) collective-permute-start(bf16[5,2,64,128]{3,2,1,0:T(8,128)(2,1)S(1)} %get-tuple-element.17), channel_id=1, source_target_pairs={{1,2},{2,1},{3,4},{4,3},{5,6},{6,5},{7,8},{8,7},{9,10},{10,9},{11,... | collective-permute-start | bytes 491528 | tf_op jit(solution)/shard_map/ppermute | solution.py:335

commit v6 on v5

--- a/solution.py
+++ b/solution.py
@@ -114,9 +114,16 @@
     )
 
 
+def first_of(left, weight):
+    return jnp.dot(left, weight, preferred_element_type=F32)
+
+
+def silu(v):
+    return v + v * jnp.tanh(v)
+
+
 def hidden_of(left, weight):
-    v = jnp.dot(left, weight, preferred_element_type=F32)
-    return v + v * jnp.tanh(v)
+    return silu(first_of(left, weight))
 
 
 def scaled_rows(values, factors):
@@ -126,13 +133,12 @@
 
 
 def second(left, weight):
-    half = left.shape[1] // 2
-    return [lax.dot_general(left[:, k : k + half], weight[:, k : k + half], NT, preferred_element_type=F32) for k in (0, half)]
+    return lax.dot_general(left, weight, NT, preferred_element_type=F32)
 
 
 def updated(products, current):
     count = current.shape[0]
-    y = products[0] + products[1]
+    y = products
     own = y[:, 0:128].reshape(count, PAIRS, 128)
     side = y[:, 128:256].reshape(count, PAIRS, 128)
     lower = lax.broadcasted_iota(jnp.int32, side.shape, 2) < 64
@@ -229,9 +235,12 @@
         rows = values.reshape(6, PAIRS, width)
         return scaled_rows(rows[0:5], factors).astype(BF16), rows[5].astype(BF16)
 
+    products = []
     for m in range(2):
         left = jnp.concatenate([taps_of(a_ref, m, 7 * c, 5), taps_of(a_ref, m, 11 - 11 * c, 1)], axis=0)
-        h_ref[m, pl.ds(7 * c, 5)], h_ref[m, 11 - 11 * c] = split(hidden_of(left, w1_ref[0]), edges(4, 1))
+        products.append(first_of(left, w1_ref[0]))
+    for m in range(2):
+        h_ref[m, pl.ds(7 * c, 5)], h_ref[m, 11 - 11 * c] = split(silu(products[m]), edges(4, 1))
     products = []
     for m in range(2):
         left = jnp.concatenate([taps_of(h_ref, m, 5 * c, 5), taps_of(h_ref, m, 9 - 9 * c, 1)], axis=0)
@@ -243,9 +252,12 @@
         x1_ref[9 - 9 * c, m] = single
         patches(a2_ref, m, 5 * c, group, norm)
         patches(a2_ref, m, 9 - 9 * c, single[None], norm)
+    products = []
     for m in range(2):
         left = jnp.concatenate([taps_of(a2_ref, m, 3 * c, 5), taps_of(a2_ref, m, 7 - 7 * c, 1)], axis=0)
-        h2_ref[m, pl.ds(3 * c, 5)], h2_ref[m, 7 - 7 * c] = split(hidden_of(left, w1_ref[1]), edges(2, 3))
+        products.append(first_of(left, w1_ref[1]))
+    for m in range(2):
+        h2_ref[m, pl.ds(3 * c, 5)], h2_ref[m, 7 - 7 * c] = split(silu(products[m]), edges(2, 3))
     products = [second(taps_of(h2_ref, m, 0, 6), w2_ref[1]) for m in range(2)]
     seen = []
     for m in range(2):

time: 75.9 us -> 75 us (0.988)
  Pallas kernels: 9.79 us -> 8.65 us
    pallas_call x1, Pallas kernels: 4.92 us -> 3.96 us  [per_device(): kernel_call(denoise_kernel, shaped((PEERS, 32, 128)), [pltpu.VMEM((14, 2,...]
where the time goes in v6:
time: 75 us; the launch traced here: 74.7 us
  blocking collectives  62 us (83%)
  Pallas kernels  8.65 us (12%)
  starting transfers between devices  1.92 us (3%)
  waiting for transfers between devices  1.5 us (2%)
    all_to_all x1, blocking collectives, per_device(): parts = lax.all_to_all(parts, TILE, 0, 0, tiled=True)  21.6 us
    all_to_all x1, blocking collectives, per_device(): got = lax.all_to_all(pay, MEM, 0, 0, tiled=True)  16.6 us
    all_to_all x1, blocking collectives, per_device(): back = lax.all_to_all(back, MEM, 0, 0, tiled=True)  13.2 us
    all_gather x1, blocking collectives, per_device(): lax.all_gather(latents, 'c')  8.68 us
    pallas_call x1, Pallas kernels, per_device(): kernel_call(denoise_kernel, shaped((PEERS, 32, 128)), [pltpu.VMEM((14, 2,...  3.96 us
    pallas_call x1, Pallas kernels, per_device(): pl.pallas_call(inner_kernel, out_shape=(shaped((2, 8, PAIRS, 256)), shape...  3.2 us
    ppermute x1, starting transfers between devices, per_device(): five = lax.ppermute(five, TILE, across)  1.92 us
    all_gather x1, blocking collectives, per_device(): lax.all_gather(lax.dynamic_slice_in_dim(five, 4 * (1 - c), 1, axis=0), 'c...  1.84 us
  transfers between devices with their start and end apart: 1, of which 1 were waited for; matrix products, arithmetic and copies ran while one was open for 0% of the time, Pallas kernels for 4%

profile of v6, /device:TPU:1, one launch (start us, length us, event | category | flops | bytes accessed | tf_op | source)
XLA Modules:
  0.0 74.7 jit_solution(18299667163383702207)
XLA Ops:
  0.6 8.7 %all-gather = bf16[4,4,8192]{2,1,0:T(4,128)(2,1)S(1)} all-gather(bf16[2,4,8192]{2,1,0:T(4,128)(2,1)} %param.7), channel_id=2, replica_groups=mesh['y'=8,'x'=4,'z'=8,'c'=2] {'c'}, dimensions={0}, use_global_device_ids=true | all-gather | bytes 393216 | tf_op jit(solution)/shard_map/all_gather | solution.py:346
  9.3 0.1 shard_map.86
  9.4 1.9 %collective-permute-start = (bf16[5,2,64,128]{3,2,1,0:T(8,128)(2,1)S(1)}, bf16[5,2,64,128]{3,2,1,0:T(8,128)(2,1)S(1)}, u32[]{:S(2)}, u32[]{:S(2)}) collective-permute-start(bf16[5,2,64,128]{3,2,1,0:T(8,128)(2,1)S(1)} %get-tuple-element.17), channel_id=1, source_target_pairs={{1,2},{2,1},{3,4},{4,3},{5,6},{6,5},{7,8},{8,7},{9,10},{10,9},{11,... | collective-permute-start | bytes 491528 | tf_op jit(solution)/shard_map/ppermute | solution.py:347
  11.3 3.2 %shard_map.87 = (bf16[2,8,64,256]{3,2,1,0:T(8,128)(2,1)S(1)}, bf16[2,6,64,512]{3,2,1,0:T(8,128)(2,1)S(1)}, bf16[4,2,64,128]{3,2,1,0:T(8,128)(2,1)S(1)}, bf16[2,4...) custom-call(bf16[8,2,64,128]{3,2,1,0:T(8,128)(2,1)S(1)} %get-tuple-e, ...), custom_call_target="tpu_custom_call" | custom-call | flops 2000000000 | bytes 6000000 | tf_op jit(solution)/shard_map/pallas_call | solution.py:348
  14.6 1.5 %collective-permute-done.five_ref = bf16[5,2,64,128]{3,2,1,0:T(8,128)(2,1)S(1)} collective-permute-done((bf16[5,2,64,128]{3,2,1,0:T(8,128)(2,1)S(1)}, bf16[5,2,64,128]{3,2,1,0:T(8,128)(2,1)S(1)}, u32[]{:S(2)}, u32[]{:S(2)}) %collective-permute-start) | collective-permute-done | bytes 163872 | tf_op jit(solution)/shard_map/ppermute | solution.py:347
  16.1 1.8 %all_gather.11.one_ref = bf16[2,2,64,128]{3,2,1,0:T(8,128)(2,1)S(1)} all-gather(bf16[1,2,64,128]{3,2,1,0:T(8,128)(2,1)S(1)} %constant_dynamic-slice_fusion), channel_id=1, replica_groups=mesh['y'=8,'x'=4,'z'=8,'c'=2] {'c'}, dimensions={0}, use_global_device_ids=true | all-gather | bytes 98304 | tf_op jit(solution)/shard_map/all_gather | solution.py:367
  17.9 4.0 %shard_map.88 = bf16[32,32,128]{2,1,0:T(8,128)(2,1)S(1)} custom-call(bf16[8,2,64,128]{3,2,1,0:T(8,128)(2,1)S(1)} %get-tuple-element.16.chip_ref, bf16[5,2,64,128]{3,2,1,0:T(8,128)(2,1)S(1)} %collective-permute-done.five_ref, bf16[2,2,64,128]{3,2,1,0:T(8,128)(2,1)S(1)} %all_gather.11.one_ref, bf16[2,8,64,256]{3,2,1,0:T(8,128)(2,1)S(1)} %get-tuple-element.18.a_part, ...), custom_call_target="tpu_custom_call" | custom-call | flops 3000000000 | bytes 4300000 | tf_op jit(solution)/shard_map/pallas_call | solution.py:368
  21.9 16.6 %all_to_all.15.got_ref = bf16[32,32,128]{2,1,0:T(8,128)(2,1)S(1)} all-to-all(bf16[32,32,128]{2,1,0:T(8,128)(2,1)S(1)} %shard_map.88), channel_id=1, replica_groups=mesh['y'=8,'x'=4,'z'=8,'c'=2] {'y','x'}, dimensions={0} | all-to-all | bytes 524288 | tf_op jit(solution)/shard_map/all_to_all | solution.py:383
  38.5 0.3 shard_map.89
  38.8 21.6 %all_to_all.16.parts_ref = bf16[16,32,128]{2,1,0:T(8,128)(2,1)S(1)} all-to-all(bf16[16,32,128]{2,1,0:T(8,128)(2,1)S(1)} %shard_map.89), channel_id=1, replica_groups=mesh['y'=8,'x'=4,'z'=8,'c'=2] {'z','c'}, dimensions={0} | all-to-all | bytes 262144 | tf_op jit(solution)/shard_map/all_to_all | solution.py:388
  60.4 0.4 shard_map.90
  60.7 13.2 %all_to_all.17.got_ref = bf16[32,16,128]{2,1,0:T(8,128)(2,1)S(1)} all-to-all(bf16[32,16,128]{2,1,0:T(8,128)(2,1)S(1)} %get-tuple-element.28), channel_id=1, replica_groups=mesh['y'=8,'x'=4,'z'=8,'c'=2] {'y','x'}, dimensions={0} | all-to-all | bytes 262144 | tf_op jit(solution)/shard_map/all_to_all | solution.py:393
  74.0 0.7 shard_map.91
  (1 shorter events, 0.0 us)
Async XLA Ops:
  9.4 6.6 %collective-permute-start = (bf16[5,2,64,128]{3,2,1,0:T(8,128)(2,1)S(1)}, bf16[5,2,64,128]{3,2,1,0:T(8,128)(2,1)S(1)}, u32[]{:S(2)}, u32[]{:S(2)}) collective-permute-start(bf16[5,2,64,128]{3,2,1,0:T(8,128)(2,1)S(1)} %get-tuple-element.17), channel_id=1, source_target_pairs={{1,2},{2,1},{3,4},{4,3},{5,6},{6,5},{7,8},{8,7},{9,10},{10,9},{11,... | collective-permute-start | bytes 491528 | tf_op jit(solution)/shard_map/ppermute | solution.py:347

commit v7 on v6

--- a/solution.py
+++ b/solution.py
@@ -201,18 +201,16 @@
         h2_ref[m] = hidden_of(taps_of(a2_ref, m, 0, 2), w1_ref[1]).astype(BF16).reshape(2, PAIRS, 512)
 
 
-def denoise_kernel(chip_ref, five_ref, one_ref, a_part, h_part, x1_part, a2_part, h2_part, w1_ref, w2_ref, obs_ref,
-                   pick_ref, sides_ref, pay_ref, x_ref, a_ref, h_ref, x1_ref, a2_ref, h2_ref, x2_ref, flat):
+def denoise_kernel(chip_ref, five_ref, a_part, h_part, x1_part, a2_part, h2_part, w1_ref, w2_ref, obs_ref,
+                   edge_ref, own_ref, seen_ref, x_ref, a_ref, h_ref, x1_ref, a2_ref, h2_ref, x2_ref, flat):
     c = lax.axis_index("c")
     tile = 2 * lax.axis_index("z") + c
     first = jnp.where(tile == 0, 0.0, 1.0).astype(F32)
     last = jnp.where(tile == 15, 0.0, 1.0).astype(F32)
     start = 5 - 4 * c
-    one = one_ref[1 - c]
     norm = mean_over_channels()
     for m in range(2):
         patches(a_ref, m, 9 * c, five_ref[:, m], norm)
-        patches(a_ref, m, 13 - 13 * c, one[m : m + 1], norm)
         for k in (0, 6):
             a_ref[m, pl.ds(start + k, 2)] = a_part[m, k : k + 2]
         for k in (0, 4):
@@ -230,53 +228,59 @@
                 group[q] = jnp.where(c == 1, last if q >= high else 1.0, first if q < low else 1.0)
         return group
 
-    def split(values, factors):
-        width = values.shape[1]
-        rows = values.reshape(6, PAIRS, width)
-        return scaled_rows(rows[0:5], factors).astype(BF16), rows[5].astype(BF16)
-
-    products = []
-    for m in range(2):
-        left = jnp.concatenate([taps_of(a_ref, m, 7 * c, 5), taps_of(a_ref, m, 11 - 11 * c, 1)], axis=0)
-        products.append(first_of(left, w1_ref[0]))
-    for m in range(2):
-        h_ref[m, pl.ds(7 * c, 5)], h_ref[m, 11 - 11 * c] = split(silu(products[m]), edges(4, 1))
-    products = []
-    for m in range(2):
-        left = jnp.concatenate([taps_of(h_ref, m, 5 * c, 5), taps_of(h_ref, m, 9 - 9 * c, 1)], axis=0)
-        products.append(second(left, w2_ref[0]))
-    for m in range(2):
-        current = jnp.concatenate([x_ref[pl.ds(5 * c + 2, 5), m], x_ref[pl.ds(11 - 9 * c, 1), m]], axis=0)
-        group, single = split(updated(products[m], current).reshape(6 * PAIRS, 128), edges(3, 2))
-        x1_ref[pl.ds(5 * c, 5), m] = group
-        x1_ref[9 - 9 * c, m] = single
-        patches(a2_ref, m, 5 * c, group, norm)
-        patches(a2_ref, m, 9 - 9 * c, single[None], norm)
-    products = []
-    for m in range(2):
-        left = jnp.concatenate([taps_of(a2_ref, m, 3 * c, 5), taps_of(a2_ref, m, 7 - 7 * c, 1)], axis=0)
-        products.append(first_of(left, w1_ref[1]))
-    for m in range(2):
-        h2_ref[m, pl.ds(3 * c, 5)], h2_ref[m, 7 - 7 * c] = split(silu(products[m]), edges(2, 3))
-    products = [second(taps_of(h2_ref, m, 0, 6), w2_ref[1]) for m in range(2)]
-    seen = []
-    for m in range(2):
-        x2_ref[:, m] = scaled_rows(updated(products[m], x1_ref[2:8, m]), {0: first, 5: last}).astype(BF16)
-        patches(a_ref, m, 0, x2_ref[:, m], None)
-        y = lax.dot_general(obs_ref[...], a_ref[m, 0:6].reshape(384, 256), NT, preferred_element_type=F32)
+    products = [first_of(taps_of(a_ref, m, 7 * c, 5), w1_ref[0]) for m in range(2)]
+    for m in range(2):
+        hidden = silu(products[m]).reshape(5, PAIRS, 512)
+        h_ref[m, pl.ds(7 * c, 5)] = scaled_rows(hidden, edges(4, 1)).astype(BF16)
+    products = [second(taps_of(h_ref, m, 5 * c, 5), w2_ref[0]) for m in range(2)]
+    for m in range(2):
+        rows = scaled_rows(updated(products[m], x_ref[pl.ds(5 * c + 2, 5), m]), edges(3, 2)).astype(BF16)
+        x1_ref[pl.ds(5 * c, 5), m] = rows
+        patches(a2_ref, m, 5 * c, rows, norm)
+    products = [first_of(taps_of(a2_ref, m, 3 * c, 5), w1_ref[1]) for m in range(2)]
+    for m in range(2):
+        hidden = silu(products[m]).reshape(5, PAIRS, 512)
+        h2_ref[m, pl.ds(3 * c, 5)] = scaled_rows(hidden, edges(2, 3)).astype(BF16)
+    products = [second(taps_of(h2_ref, m, c, 5), w2_ref[1]) for m in range(2)]
+    for m in range(2):
+        rows = scaled_rows(updated(products[m], x1_ref[pl.ds(2 + c, 5), m]), edges(1, 4)).astype(BF16)
+        x2_ref[:, m] = rows
+        patches(a2_ref, m, 0, rows, None)
+    edge_ref[...] = x2_ref[4 - 4 * c]
+    for m in range(2):
+        seen_ref[m] = lax.dot_general(
+            obs_ref[...], a2_ref[m, 0:5].reshape(320, 256), NT, preferred_element_type=F32
+        )
+    for m in range(2):
+        for r in range(4):
+            flat[pl.ds(256 * m + r, PAIRS, stride=4), :] = x2_ref[1 - c + r, m].astype(F32)
+    for p in range(PEERS):
+        both = jnp.concatenate([flat[8 * p : 8 * p + 8], flat[256 + 8 * p : 256 + 8 * p + 8]], axis=0)
+        own_ref[p] = both.astype(BF16)
+
+
+def observe_kernel(edge_ref, own_ref, seen_ref, obs_ref, pick_ref, sides_ref, pay_ref, a_ref):
+    c = lax.axis_index("c")
+    edge = edge_ref[1 - c]
+    for m in range(2):
+        patches(a_ref, m, 0, edge[m : m + 1], None)
+    both = []
+    for m in range(2):
+        other = lax.dot_general(obs_ref[...], a_ref[m, 0], NT, preferred_element_type=F32)
+        own = seen_ref[m]
+        y = jnp.where(c == 1, jnp.concatenate([other, own], axis=1), jnp.concatenate([own, other], axis=1))
         whole = jnp.concatenate([y[16 * dr : 16 * dr + 16] for dr in range(3)], axis=1)
         high = whole.astype(BF16).astype(F32)
-        both = jnp.concatenate([high, whole - high], axis=0).astype(BF16)
-        picked = jnp.dot(both, pick_ref[...], preferred_element_type=F32)
-        seen.append(picked[0:16] + picked[16:32])
+        both += [high, whole - high]
+    picked = jnp.dot(jnp.concatenate(both, axis=0).astype(BF16), pick_ref[...], preferred_element_type=F32)
     odd = sides_ref[16:24] > 0.5
-    got = jnp.concatenate([jnp.where(odd, y[8:16], y[0:8]) for y in seen], axis=0).astype(BF16)
-    for m in range(2):
-        for r in range(4):
-            flat[pl.ds(256 * m + r, PAIRS, stride=4), :] = x2_ref[1 + r, m].astype(F32)
+    got = []
+    for m in range(2):
+        y = picked[32 * m : 32 * m + 16] + picked[32 * m + 16 : 32 * m + 32]
+        got.append(jnp.where(odd, y[8:16], y[0:8]))
+    got = jnp.concatenate(got, axis=0).astype(BF16)
     for p in range(PEERS):
-        both = jnp.concatenate([flat[8 * p : 8 * p + 8], flat[256 + 8 * p : 256 + 8 * p + 8]], axis=0)
-        pay_ref[p, 0:16] = both.astype(BF16)
+        pay_ref[p, 0:16] = own_ref[p]
         pay_ref[p, 16:32] = got
 
 
@@ -325,14 +329,21 @@
         back_ref[p] = flat[16 * p : 16 * p + 16].astype(BF16)
 
 
-def final_kernel(got_ref, covariance_in, out_ref, covariance_ref):
-    covariance_ref[...] = covariance_in[...]
-    for p in range(PEERS):
-        values = got_ref[p].astype(F32)
+def final_kernel(got_ref, covariance_in, out_hbm, covariance_hbm, out_ref, sems):
+    copies = [pltpu.make_async_copy(covariance_in, covariance_hbm, sems.at[8])]
+    copies[0].start()
+    for part in range(4):
         for m in range(2):
-            for t in range(2):
-                at = 128 * (2 * p + t)
-                out_ref[m, :, at : at + 128] = values[8 * m + 4 * t : 8 * m + 4 * t + 4]
+            for p in range(8 * part, 8 * part + 8):
+                values = got_ref[p, 8 * m : 8 * m + 8].astype(F32)
+                for t in range(2):
+                    at = 128 * (2 * p + t)
+                    out_ref[m, :, at : at + 128] = values[4 * t : 4 * t + 4]
+            span = pl.ds(2048 * part, 2048)
+            copies.append(pltpu.make_async_copy(out_ref.at[m, :, span], out_hbm.at[m, :, span], sems.at[2 * part + m]))
+            copies[-1].start()
+    for copy in copies:
+        copy.wait()
 
 
 def per_device(latents, in_weight, out_weight, observe_weight, obs_cells, obs_values, obs_precision):
@@ -364,10 +375,10 @@
         in_weight, jnp.transpose(out_weight, (0, 2, 1)), jnp.transpose(observe_weight), obs_cells, obs_values,
         obs_precision,
     )))
-    one = lax.all_gather(lax.dynamic_slice_in_dim(five, 4 * (1 - c), 1, axis=0), "c", axis=0, tiled=True)
-    pay = kernel_call(
+    *parts, obs, pick = parts
+    edge, own, seen = kernel_call(
         denoise_kernel,
-        shaped((PEERS, 32, 128)),
+        (shaped((2, PAIRS, 128)), shaped((PEERS, 16, 128)), shaped((2, 48, 320), F32)),
         [
             pltpu.VMEM((14, 2, PAIRS, 128), BF16),
             pltpu.VMEM((2, 14, PAIRS, 256), BF16),
@@ -375,11 +386,14 @@
             pltpu.VMEM((10, 2, PAIRS, 128), BF16),
             pltpu.VMEM((2, 10, PAIRS, 256), BF16),
             pltpu.VMEM((2, 8, PAIRS, 512), BF16),
-            pltpu.VMEM((6, 2, PAIRS, 128), BF16),
+            pltpu.VMEM((5, 2, PAIRS, 128), BF16),
             pltpu.VMEM((512, 128), F32),
         ],
         flops=3_000_000_000, moved=4_300_000,
-    )(chip, five, one, *parts, sides)
+    )(chip, five, *parts, obs)
+    pay = kernel_call(
+        observe_kernel, shaped((PEERS, 32, 128)), [pltpu.VMEM((2, 1, PAIRS, 256), BF16)], moved=800_000,
+    )(lax.all_gather(edge, "c"), own, seen, obs, pick, sides)
     got = lax.all_to_all(pay, MEM, 0, 0, tiled=True)
 
     parts = kernel_call(
@@ -391,7 +405,15 @@
         moved=700_000,
     )(got, parts)
     back = lax.all_to_all(back, MEM, 0, 0, tiled=True)
-    return kernel_call(final_kernel, (shaped((2, 4, 8192), F32), shaped((64, 64), F32)), moved=400_000)(back, covariance)
+    return pl.pallas_call(
+        final_kernel,
+        out_shape=(shaped((2, 4, 8192), F32), shaped((64, 64), F32)),
+        in_specs=[vmem, vmem],
+        out_specs=(hbm, hbm),
+        scratch_shapes=[pltpu.VMEM((2, 4, 8192), F32), pltpu.SemaphoreType.DMA((9,))],
+        cost_estimate=pl.CostEstimate(flops=0, bytes_accessed=400_000, transcendentals=0),
+        compiler_params=pltpu.CompilerParams(vmem_limit_bytes=LIMIT),
+    )(back, covariance)
 
 
 def solution(mesh):

time: 75 us -> 74.7 us (level)
    pallas_call x2 -> x3, Pallas kernels: 4.71 us -> 4.37 us  [the longest x1 3.2 us: per_device(): kernel_call(denoise_kernel, (shaped((2, PAIRS, 128)), shaped((PEERS, 16,...]
where the time goes in v7:
time: 74.7 us; the launch traced here: 74.4 us
  blocking collectives  62 us (83%)
  Pallas kernels  8.3 us (11%)
  starting transfers between devices  1.92 us (3%)
  waiting for transfers between devices  1.51 us (2%)
    all_to_all x1, blocking collectives, per_device(): parts = lax.all_to_all(parts, TILE, 0, 0, tiled=True)  21.6 us
    all_to_all x1, blocking collectives, per_device(): got = lax.all_to_all(pay, MEM, 0, 0, tiled=True)  16.6 us
    all_to_all x1, blocking collectives, per_device(): back = lax.all_to_all(back, MEM, 0, 0, tiled=True)  13.2 us
    all_gather x1, blocking collectives, per_device(): lax.all_gather(latents, 'c')  8.68 us
    pallas_call x1, Pallas kernels, per_device(): kernel_call(denoise_kernel, (shaped((2, PAIRS, 128)), shaped((PEERS, 16,...  3.2 us
    pallas_call x1, Pallas kernels, per_device(): pl.pallas_call(inner_kernel, out_shape=(shaped((2, 8, PAIRS, 256)), shape...  3.19 us
    ppermute x1, starting transfers between devices, per_device(): five = lax.ppermute(five, TILE, across)  1.92 us
    all_gather x1, blocking collectives, per_device(): lax.all_gather(edge, 'c')  1.86 us
  transfers between devices with their start and end apart: 1, of which 1 were waited for; matrix products, arithmetic and copies ran while one was open for 0% of the time, Pallas kernels for 4%

profile of v7, /device:TPU:1, one launch (start us, length us, event | category | flops | bytes accessed | tf_op | source)
XLA Modules:
  0.0 74.4 jit_solution(10340956883127502850)
XLA Ops:
  0.6 8.7 %all-gather = bf16[4,4,8192]{2,1,0:T(4,128)(2,1)S(1)} all-gather(bf16[2,4,8192]{2,1,0:T(4,128)(2,1)} %param.7), channel_id=2, replica_groups=mesh['y'=8,'x'=4,'z'=8,'c'=2] {'c'}, dimensions={0}, use_global_device_ids=true | all-gather | bytes 393216 | tf_op jit(solution)/shard_map/all_gather | solution.py:357
  9.3 0.1 shard_map.86
  9.4 1.9 %collective-permute-start = (bf16[5,2,64,128]{3,2,1,0:T(8,128)(2,1)S(1)}, bf16[5,2,64,128]{3,2,1,0:T(8,128)(2,1)S(1)}, u32[]{:S(2)}, u32[]{:S(2)}) collective-permute-start(bf16[5,2,64,128]{3,2,1,0:T(8,128)(2,1)S(1)} %get-tuple-element.20), channel_id=1, source_target_pairs={{1,2},{2,1},{3,4},{4,3},{5,6},{6,5},{7,8},{8,7},{9,10},{10,9},{11,... | collective-permute-start | bytes 491528 | tf_op jit(solution)/shard_map/ppermute | solution.py:358
  11.3 3.2 %shard_map.87 = (bf16[2,8,64,256]{3,2,1,0:T(8,128)(2,1)S(1)}, bf16[2,6,64,512]{3,2,1,0:T(8,128)(2,1)S(1)}, bf16[4,2,64,128]{3,2,1,0:T(8,128)(2,1)S(1)}, bf16[2,4...) custom-call(bf16[8,2,64,128]{3,2,1,0:T(8,128)(2,1)S(1)} %get-tuple-e, ...), custom_call_target="tpu_custom_call" | custom-call | flops 2000000000 | bytes 6000000 | tf_op jit(solution)/shard_map/pallas_call | solution.py:359
  14.5 1.5 %collective-permute-done.five_ref = bf16[5,2,64,128]{3,2,1,0:T(8,128)(2,1)S(1)} collective-permute-done((bf16[5,2,64,128]{3,2,1,0:T(8,128)(2,1)S(1)}, bf16[5,2,64,128]{3,2,1,0:T(8,128)(2,1)S(1)}, u32[]{:S(2)}, u32[]{:S(2)}) %collective-permute-start) | collective-permute-done | bytes 163872 | tf_op jit(solution)/shard_map/ppermute | solution.py:358
  16.1 3.2 %shard_map.88 = (bf16[2,64,128]{2,1,0:T(8,128)(2,1)S(1)}, bf16[32,16,128]{2,1,0:T(8,128)(2,1)S(1)}, f32[2,48,320]{2,1,0:T(8,128)S(1)}) custom-call(bf16[8,2,64,128]{3,2,1,0:T(8,128)(2,1)S(1)} %get-tuple-element.19.chip_ref, bf16[5,2,64,128]{3,2,1,0:T(8,128)(2,1)S(1)} %collective-permute-done.five_ref, bf16[2,8,64,256]{3,2,1,0:T(8,128)(2,1)S(1)} %get-tuple-element.21.a_part, ...), custom_call_target="tpu_custom_call" | custom-call | flops 3000000000 | bytes 4300000 | tf_op jit(solution)/shard_map/pallas_call | solution.py:379
  19.3 1.9 %all-gather.1 = bf16[4,64,128]{2,1,0:T(8,128)(2,1)S(1)} all-gather(bf16[2,64,128]{2,1,0:T(8,128)(2,1)S(1)} %get-tuple-element.29), channel_id=3, replica_groups=mesh['y'=8,'x'=4,'z'=8,'c'=2] {'c'}, dimensions={0}, use_global_device_ids=true | all-gather | bytes 98304 | tf_op jit(solution)/shard_map/all_gather | solution.py:396
  21.1 0.4 shard_map.89
  21.5 16.6 %all_to_all.15.got_ref = bf16[32,32,128]{2,1,0:T(8,128)(2,1)S(1)} all-to-all(bf16[32,32,128]{2,1,0:T(8,128)(2,1)S(1)} %shard_map.89), channel_id=1, replica_groups=mesh['y'=8,'x'=4,'z'=8,'c'=2] {'y','x'}, dimensions={0} | all-to-all | bytes 524288 | tf_op jit(solution)/shard_map/all_to_all | solution.py:397
  38.1 0.3 shard_map.90
  38.4 21.6 %all_to_all.16.parts_ref = bf16[16,32,128]{2,1,0:T(8,128)(2,1)S(1)} all-to-all(bf16[16,32,128]{2,1,0:T(8,128)(2,1)S(1)} %shard_map.90), channel_id=1, replica_groups=mesh['y'=8,'x'=4,'z'=8,'c'=2] {'z','c'}, dimensions={0} | all-to-all | bytes 262144 | tf_op jit(solution)/shard_map/all_to_all | solution.py:402
  60.0 0.4 shard_map.91
  60.4 13.2 %all_to_all.17.got_ref = bf16[32,16,128]{2,1,0:T(8,128)(2,1)S(1)} all-to-all(bf16[32,16,128]{2,1,0:T(8,128)(2,1)S(1)} %get-tuple-element.34), channel_id=1, replica_groups=mesh['y'=8,'x'=4,'z'=8,'c'=2] {'y','x'}, dimensions={0} | all-to-all | bytes 262144 | tf_op jit(solution)/shard_map/all_to_all | solution.py:407
  73.6 0.8 %shard_map.92 = (f32[2,4,8192]{2,1,0:T(4,128)}, f32[64,64]{1,0:T(8,128)}) custom-call(bf16[32,16,128]{2,1,0:T(8,128)(2,1)S(1)} %all_to_all.17.got_ref, f32[64,64]{1,0:T(8,128)S(1)} %get-tuple-element.35.covariance_in), custom_call_target="tpu_custom_call" | custom-call | bytes 400000 | tf_op jit(solution)/shard_map/pallas_call | solution.py:408
Async XLA Ops:
  9.4 6.6 %collective-permute-start = (bf16[5,2,64,128]{3,2,1,0:T(8,128)(2,1)S(1)}, bf16[5,2,64,128]{3,2,1,0:T(8,128)(2,1)S(1)}, u32[]{:S(2)}, u32[]{:S(2)}) collective-permute-start(bf16[5,2,64,128]{3,2,1,0:T(8,128)(2,1)S(1)} %get-tuple-element.20), channel_id=1, source_target_pairs={{1,2},{2,1},{3,4},{4,3},{5,6},{6,5},{7,8},{8,7},{9,10},{10,9},{11,... | collective-permute-start | bytes 491528 | tf_op jit(solution)/shard_map/ppermute | solution.py:358

commit v8 on v7

--- a/solution.py
+++ b/solution.py
@@ -49,25 +49,25 @@
     five_ref[...] = chip_ref[pl.ds(3 * c, 5)]
 
 
-def spread_weights(in_ref, out_ref, seen_ref, first_ref, second_ref, obs_ref):
-    first_ref[...] = jnp.zeros_like(first_ref)
-    second_ref[...] = jnp.zeros_like(second_ref)
-    for layer in range(2):
-        for dr in range(3):
-            for b, j in enumerate(BLOCKS):
-                for h in range(2):
-                    dc = j - h + 1
-                    if 0 <= dc <= 2:
-                        at = 64 * (3 * dr + dc)
-                        first_ref[layer, 256 * dr + 64 * b : 256 * dr + 64 * b + 64, 256 * h : 256 * h + 256] = (
-                            in_ref[layer, at : at + 64, :] * jnp.asarray(0.5, BF16)
-                        )
-                    dc = h - j + 1
-                    if 0 <= dc <= 2:
-                        at = 256 * (3 * dr + dc)
-                        second_ref[layer, 64 * b : 64 * b + 64, 512 * dr + 256 * h : 512 * dr + 256 * h + 256] = (
-                            out_ref[layer, :, at : at + 256]
-                        )
+def spread_weights(layer, in_ref, out_ref, first_ref, second_ref):
+    for dr in range(3):
+        for b, j in enumerate(BLOCKS):
+            for h in range(2):
+                dc, at = j - h + 1, (slice(256 * dr + 64 * b, 256 * dr + 64 * b + 64), slice(256 * h, 256 * h + 256))
+                tap = 64 * (3 * dr + dc)
+                if 0 <= dc <= 2:
+                    first_ref[(layer, *at)] = in_ref[layer, tap : tap + 64, :] * jnp.asarray(0.5, BF16)
+                else:
+                    first_ref[(layer, *at)] = jnp.zeros((64, 256), BF16)
+                dc, at = h - j + 1, (slice(64 * b, 64 * b + 64), slice(512 * dr + 256 * h, 512 * dr + 256 * h + 256))
+                tap = 256 * (3 * dr + dc)
+                if 0 <= dc <= 2:
+                    second_ref[(layer, *at)] = out_ref[layer, :, tap : tap + 256]
+                else:
+                    second_ref[(layer, *at)] = jnp.zeros((64, 256), BF16)
+
+
+def spread_observed(seen_ref, obs_ref):
     taps = seen_ref[...].astype(F32)
     none = jnp.zeros((8, 64), F32)
     rows = []
@@ -120,10 +120,6 @@
 
 def silu(v):
     return v + v * jnp.tanh(v)
-
-
-def hidden_of(left, weight):
-    return silu(first_of(left, weight))
 
 
 def scaled_rows(values, factors):
@@ -176,9 +172,12 @@
     for m in range(2):
         for row in (0, 4):
             patches(a_ref, m, row, chip_ref[row : row + 4, m], norm)
-    for fetch in fetches[:3]:
+    for fetch in fetches:
         fetch.wait()
+    spread_weights(0, in_ref, out_ref, w1_ref, w2_ref)
+    products = [first_of(taps_of(a_ref, m, 0, 6), w1_ref[0]) for m in range(2)]
     by_channel(values_ref, precision_ref, sides_ref)
+    spread_observed(seen_ref, obs_ref)
     cell = jnp.concatenate([cells_ref[r : r + 1, :] for r in range(4)], axis=1)
     pair = lax.shift_right_logical(cell, 1)
     lane_row = lax.broadcasted_iota(jnp.int32, (1, 128), 1) // 32
@@ -186,19 +185,16 @@
     for dr in range(3):
         pick_ref[384 * dr : 384 * dr + 384, :] = jnp.where(index == (lane_row + dr) * PAIRS + pair, 1.0, 0.0).astype(BF16)
     sides_ref[16:24] = jnp.broadcast_to((cell & 1).astype(F32), (8, 128))
-    for fetch in fetches[3:]:
-        fetch.wait()
-    spread_weights(in_ref, out_ref, seen_ref, w1_ref, w2_ref, obs_ref)
-    for m in range(2):
-        for row in (0, 3):
-            hidden = hidden_of(taps_of(a_ref, m, row, 3), w1_ref[0])
-            h_ref[m, row : row + 3] = hidden.astype(BF16).reshape(3, PAIRS, 512)
+    spread_weights(1, in_ref, out_ref, w1_ref, w2_ref)
+    for m in range(2):
+        h_ref[m] = silu(products[m]).astype(BF16).reshape(6, PAIRS, 512)
     products = [second(taps_of(h_ref, m, 0, 4), w2_ref[0]) for m in range(2)]
     for m in range(2):
         x1_ref[:, m] = updated(products[m], chip_ref[2:6, m]).astype(BF16)
         patches(a2_ref, m, 0, x1_ref[:, m], norm)
-    for m in range(2):
-        h2_ref[m] = hidden_of(taps_of(a2_ref, m, 0, 2), w1_ref[1]).astype(BF16).reshape(2, PAIRS, 512)
+    products = [first_of(taps_of(a2_ref, m, 0, 2), w1_ref[1]) for m in range(2)]
+    for m in range(2):
+        h2_ref[m] = silu(products[m]).astype(BF16).reshape(2, PAIRS, 512)
 
 
 def denoise_kernel(chip_ref, five_ref, a_part, h_part, x1_part, a2_part, h2_part, w1_ref, w2_ref, obs_ref,
@@ -329,21 +325,14 @@
         back_ref[p] = flat[16 * p : 16 * p + 16].astype(BF16)
 
 
-def final_kernel(got_ref, covariance_in, out_hbm, covariance_hbm, out_ref, sems):
-    copies = [pltpu.make_async_copy(covariance_in, covariance_hbm, sems.at[8])]
-    copies[0].start()
-    for part in range(4):
+def final_kernel(got_ref, covariance_in, out_ref, covariance_ref):
+    covariance_ref[...] = covariance_in[...]
+    for p in range(PEERS):
+        values = got_ref[p].astype(F32)
         for m in range(2):
-            for p in range(8 * part, 8 * part + 8):
-                values = got_ref[p, 8 * m : 8 * m + 8].astype(F32)
-                for t in range(2):
-                    at = 128 * (2 * p + t)
-                    out_ref[m, :, at : at + 128] = values[4 * t : 4 * t + 4]
-            span = pl.ds(2048 * part, 2048)
-            copies.append(pltpu.make_async_copy(out_ref.at[m, :, span], out_hbm.at[m, :, span], sems.at[2 * part + m]))
-            copies[-1].start()
-    for copy in copies:
-        copy.wait()
+            for t in range(2):
+                at = 128 * (2 * p + t)
+                out_ref[m, :, at : at + 128] = values[8 * m + 4 * t : 8 * m + 4 * t + 4]
 
 
 def per_device(latents, in_weight, out_weight, observe_weight, obs_cells, obs_values, obs_precision):
@@ -405,15 +394,7 @@
         moved=700_000,
     )(got, parts)
     back = lax.all_to_all(back, MEM, 0, 0, tiled=True)
-    return pl.pallas_call(
-        final_kernel,
-        out_shape=(shaped((2, 4, 8192), F32), shaped((64, 64), F32)),
-        in_specs=[vmem, vmem],
-        out_specs=(hbm, hbm),
-        scratch_shapes=[pltpu.VMEM((2, 4, 8192), F32), pltpu.SemaphoreType.DMA((9,))],
-        cost_estimate=pl.CostEstimate(flops=0, bytes_accessed=400_000, transcendentals=0),
-        compiler_params=pltpu.CompilerParams(vmem_limit_bytes=LIMIT),
-    )(back, covariance)
+    return kernel_call(final_kernel, (shaped((2, 4, 8192), F32), shaped((64, 64), F32)), moved=400_000)(back, covariance)
 
 
 def solution(mesh):

time: 74.7 us -> 74.6 us (level)
  transfers between devices with their start and end apart: 1 -> 1, of which waited for: 1 -> 1; matrix products, arithmetic and copies ran while one was open for 0% -> 0% of each run, Pallas kernels for 4% -> 5%
where the time goes in v8:
time: 74.6 us; the launch traced here: 74.3 us
  blocking collectives  62 us (83%)
  Pallas kernels  8.42 us (11%)
  starting transfers between devices  1.92 us (3%)
  waiting for transfers between devices  1.35 us (2%)
    all_to_all x1, blocking collectives, per_device(): parts = lax.all_to_all(parts, TILE, 0, 0, tiled=True)  21.5 us
    all_to_all x1, blocking collectives, per_device(): got = lax.all_to_all(pay, MEM, 0, 0, tiled=True)  16.8 us
    all_to_all x1, blocking collectives, per_device(): back = lax.all_to_all(back, MEM, 0, 0, tiled=True)  13.2 us
    all_gather x1, blocking collectives, per_device(): lax.all_gather(latents, 'c')  8.68 us
    pallas_call x1, Pallas kernels, per_device(): pl.pallas_call(inner_kernel, out_shape=(shaped((2, 8, PAIRS, 256)), shape...  3.35 us
    pallas_call x1, Pallas kernels, per_device(): kernel_call(denoise_kernel, (shaped((2, PAIRS, 128)), shaped((PEERS, 16,...  3.2 us
    ppermute x1, starting transfers between devices, per_device(): five = lax.ppermute(five, TILE, across)  1.92 us
    all_gather x1, blocking collectives, per_device(): lax.all_gather(edge, 'c')  1.86 us
  transfers between devices with their start and end apart: 1, of which 1 were waited for; matrix products, arithmetic and copies ran while one was open for 0% of the time, Pallas kernels for 5%

profile of v8, /device:TPU:1, one launch (start us, length us, event | category | flops | bytes accessed | tf_op | source)
XLA Modules:
  0.0 74.3 jit_solution(12454168706036078071)
XLA Ops:
  0.6 8.7 %all-gather = bf16[4,4,8192]{2,1,0:T(4,128)(2,1)S(1)} all-gather(bf16[2,4,8192]{2,1,0:T(4,128)(2,1)} %param.7), channel_id=2, replica_groups=mesh['y'=8,'x'=4,'z'=8,'c'=2] {'c'}, dimensions={0}, use_global_device_ids=true | all-gather | bytes 393216 | tf_op jit(solution)/shard_map/all_gather | solution.py:346
  9.3 0.1 shard_map.86
  9.4 1.9 %collective-permute-start = (bf16[5,2,64,128]{3,2,1,0:T(8,128)(2,1)S(1)}, bf16[5,2,64,128]{3,2,1,0:T(8,128)(2,1)S(1)}, u32[]{:S(2)}, u32[]{:S(2)}) collective-permute-start(bf16[5,2,64,128]{3,2,1,0:T(8,128)(2,1)S(1)} %get-tuple-element.20), channel_id=1, source_target_pairs={{1,2},{2,1},{3,4},{4,3},{5,6},{6,5},{7,8},{8,7},{9,10},{10,9},{11,... | collective-permute-start | bytes 491528 | tf_op jit(solution)/shard_map/ppermute | solution.py:347
  11.3 3.3 %shard_map.87 = (bf16[2,8,64,256]{3,2,1,0:T(8,128)(2,1)S(1)}, bf16[2,6,64,512]{3,2,1,0:T(8,128)(2,1)S(1)}, bf16[4,2,64,128]{3,2,1,0:T(8,128)(2,1)S(1)}, bf16[2,4...) custom-call(bf16[8,2,64,128]{3,2,1,0:T(8,128)(2,1)S(1)} %get-tuple-e, ...), custom_call_target="tpu_custom_call" | custom-call | flops 2000000000 | bytes 6000000 | tf_op jit(solution)/shard_map/pallas_call | solution.py:348
  14.7 1.4 %collective-permute-done.five_ref = bf16[5,2,64,128]{3,2,1,0:T(8,128)(2,1)S(1)} collective-permute-done((bf16[5,2,64,128]{3,2,1,0:T(8,128)(2,1)S(1)}, bf16[5,2,64,128]{3,2,1,0:T(8,128)(2,1)S(1)}, u32[]{:S(2)}, u32[]{:S(2)}) %collective-permute-start) | collective-permute-done | bytes 163872 | tf_op jit(solution)/shard_map/ppermute | solution.py:347
  16.1 3.2 %shard_map.88 = (bf16[2,64,128]{2,1,0:T(8,128)(2,1)S(1)}, bf16[32,16,128]{2,1,0:T(8,128)(2,1)S(1)}, f32[2,48,320]{2,1,0:T(8,128)S(1)}) custom-call(bf16[8,2,64,128]{3,2,1,0:T(8,128)(2,1)S(1)} %get-tuple-element.19.chip_ref, bf16[5,2,64,128]{3,2,1,0:T(8,128)(2,1)S(1)} %collective-permute-done.five_ref, bf16[2,8,64,256]{3,2,1,0:T(8,128)(2,1)S(1)} %get-tuple-element.21.a_part, ...), custom_call_target="tpu_custom_call" | custom-call | flops 3000000000 | bytes 4300000 | tf_op jit(solution)/shard_map/pallas_call | solution.py:368
  19.3 1.9 %all-gather.1 = bf16[4,64,128]{2,1,0:T(8,128)(2,1)S(1)} all-gather(bf16[2,64,128]{2,1,0:T(8,128)(2,1)S(1)} %get-tuple-element.29), channel_id=3, replica_groups=mesh['y'=8,'x'=4,'z'=8,'c'=2] {'c'}, dimensions={0}, use_global_device_ids=true | all-gather | bytes 98304 | tf_op jit(solution)/shard_map/all_gather | solution.py:385
  21.1 0.4 shard_map.89
  21.5 16.8 %all_to_all.15.got_ref = bf16[32,32,128]{2,1,0:T(8,128)(2,1)S(1)} all-to-all(bf16[32,32,128]{2,1,0:T(8,128)(2,1)S(1)} %shard_map.89), channel_id=1, replica_groups=mesh['y'=8,'x'=4,'z'=8,'c'=2] {'y','x'}, dimensions={0} | all-to-all | bytes 524288 | tf_op jit(solution)/shard_map/all_to_all | solution.py:386
  38.3 0.3 shard_map.90
  38.6 21.5 %all_to_all.16.parts_ref = bf16[16,32,128]{2,1,0:T(8,128)(2,1)S(1)} all-to-all(bf16[16,32,128]{2,1,0:T(8,128)(2,1)S(1)} %shard_map.90), channel_id=1, replica_groups=mesh['y'=8,'x'=4,'z'=8,'c'=2] {'z','c'}, dimensions={0} | all-to-all | bytes 262144 | tf_op jit(solution)/shard_map/all_to_all | solution.py:391
  60.0 0.4 shard_map.91
  60.4 13.2 %all_to_all.17.got_ref = bf16[32,16,128]{2,1,0:T(8,128)(2,1)S(1)} all-to-all(bf16[32,16,128]{2,1,0:T(8,128)(2,1)S(1)} %get-tuple-element.34), channel_id=1, replica_groups=mesh['y'=8,'x'=4,'z'=8,'c'=2] {'y','x'}, dimensions={0} | all-to-all | bytes 262144 | tf_op jit(solution)/shard_map/all_to_all | solution.py:396
  73.6 0.7 shard_map.92
Async XLA Ops:
  9.4 6.6 %collective-permute-start = (bf16[5,2,64,128]{3,2,1,0:T(8,128)(2,1)S(1)}, bf16[5,2,64,128]{3,2,1,0:T(8,128)(2,1)S(1)}, u32[]{:S(2)}, u32[]{:S(2)}) collective-permute-start(bf16[5,2,64,128]{3,2,1,0:T(8,128)(2,1)S(1)} %get-tuple-element.20), channel_id=1, source_target_pairs={{1,2},{2,1},{3,4},{4,3},{5,6},{6,5},{7,8},{8,7},{9,10},{10,9},{11,... | collective-permute-start | bytes 491528 | tf_op jit(solution)/shard_map/ppermute | solution.py:347

commit v9 on v7

--- a/solution.py
+++ b/solution.py
@@ -329,21 +329,14 @@
         back_ref[p] = flat[16 * p : 16 * p + 16].astype(BF16)
 
 
-def final_kernel(got_ref, covariance_in, out_hbm, covariance_hbm, out_ref, sems):
-    copies = [pltpu.make_async_copy(covariance_in, covariance_hbm, sems.at[8])]
-    copies[0].start()
-    for part in range(4):
+def final_kernel(got_ref, covariance_in, out_ref, covariance_ref):
+    covariance_ref[...] = covariance_in[...]
+    for p in range(PEERS):
+        values = got_ref[p].astype(F32)
         for m in range(2):
-            for p in range(8 * part, 8 * part + 8):
-                values = got_ref[p, 8 * m : 8 * m + 8].astype(F32)
-                for t in range(2):
-                    at = 128 * (2 * p + t)
-                    out_ref[m, :, at : at + 128] = values[4 * t : 4 * t + 4]
-            span = pl.ds(2048 * part, 2048)
-            copies.append(pltpu.make_async_copy(out_ref.at[m, :, span], out_hbm.at[m, :, span], sems.at[2 * part + m]))
-            copies[-1].start()
-    for copy in copies:
-        copy.wait()
+            for t in range(2):
+                at = 128 * (2 * p + t)
+                out_ref[m, :, at : at + 128] = values[8 * m + 4 * t : 8 * m + 4 * t + 4]
 
 
 def per_device(latents, in_weight, out_weight, observe_weight, obs_cells, obs_values, obs_precision):
@@ -405,15 +398,7 @@
         moved=700_000,
     )(got, parts)
     back = lax.all_to_all(back, MEM, 0, 0, tiled=True)
-    return pl.pallas_call(
-        final_kernel,
-        out_shape=(shaped((2, 4, 8192), F32), shaped((64, 64), F32)),
-        in_specs=[vmem, vmem],
-        out_specs=(hbm, hbm),
-        scratch_shapes=[pltpu.VMEM((2, 4, 8192), F32), pltpu.SemaphoreType.DMA((9,))],
-        cost_estimate=pl.CostEstimate(flops=0, bytes_accessed=400_000, transcendentals=0),
-        compiler_params=pltpu.CompilerParams(vmem_limit_bytes=LIMIT),
-    )(back, covariance)
+    return kernel_call(final_kernel, (shaped((2, 4, 8192), F32), shaped((64, 64), F32)), moved=400_000)(back, covariance)
 
 
 def solution(mesh):

time: 74.7 us -> 74.6 us (level)
  no operation moved by 1% of the time
where the time goes in v9:
time: 74.6 us; the launch traced here: 74.3 us
  blocking collectives  62 us (83%)
  Pallas kernels  8.26 us (11%)
  starting transfers between devices  1.92 us (3%)
  waiting for transfers between devices  1.51 us (2%)
    all_to_all x1, blocking collectives, per_device(): parts = lax.all_to_all(parts, TILE, 0, 0, tiled=True)  21.6 us
    all_to_all x1, blocking collectives, per_device(): got = lax.all_to_all(pay, MEM, 0, 0, tiled=True)  16.6 us
    all_to_all x1, blocking collectives, per_device(): back = lax.all_to_all(back, MEM, 0, 0, tiled=True)  13.2 us
    all_gather x1, blocking collectives, per_device(): lax.all_gather(latents, 'c')  8.68 us
    pallas_call x1, Pallas kernels, per_device(): kernel_call(denoise_kernel, (shaped((2, PAIRS, 128)), shaped((PEERS, 16,...  3.2 us
    pallas_call x1, Pallas kernels, per_device(): pl.pallas_call(inner_kernel, out_shape=(shaped((2, 8, PAIRS, 256)), shape...  3.19 us
    ppermute x1, starting transfers between devices, per_device(): five = lax.ppermute(five, TILE, across)  1.92 us
    all_gather x1, blocking collectives, per_device(): lax.all_gather(edge, 'c')  1.86 us
  transfers between devices with their start and end apart: 1, of which 1 were waited for; matrix products, arithmetic and copies ran while one was open for 0% of the time, Pallas kernels for 4%

profile of v9, /device:TPU:1, one launch (start us, length us, event | category | flops | bytes accessed | tf_op | source)
XLA Modules:
  0.0 74.3 jit_solution(10235093351510941929)
XLA Ops:
  0.6 8.7 %all-gather = bf16[4,4,8192]{2,1,0:T(4,128)(2,1)S(1)} all-gather(bf16[2,4,8192]{2,1,0:T(4,128)(2,1)} %param.7), channel_id=2, replica_groups=mesh['y'=8,'x'=4,'z'=8,'c'=2] {'c'}, dimensions={0}, use_global_device_ids=true | all-gather | bytes 393216 | tf_op jit(solution)/shard_map/all_gather | solution.py:350
  9.3 0.1 shard_map.86
  9.4 1.9 %collective-permute-start = (bf16[5,2,64,128]{3,2,1,0:T(8,128)(2,1)S(1)}, bf16[5,2,64,128]{3,2,1,0:T(8,128)(2,1)S(1)}, u32[]{:S(2)}, u32[]{:S(2)}) collective-permute-start(bf16[5,2,64,128]{3,2,1,0:T(8,128)(2,1)S(1)} %get-tuple-element.20), channel_id=1, source_target_pairs={{1,2},{2,1},{3,4},{4,3},{5,6},{6,5},{7,8},{8,7},{9,10},{10,9},{11,... | collective-permute-start | bytes 491528 | tf_op jit(solution)/shard_map/ppermute | solution.py:351
  11.3 3.2 %shard_map.87 = (bf16[2,8,64,256]{3,2,1,0:T(8,128)(2,1)S(1)}, bf16[2,6,64,512]{3,2,1,0:T(8,128)(2,1)S(1)}, bf16[4,2,64,128]{3,2,1,0:T(8,128)(2,1)S(1)}, bf16[2,4...) custom-call(bf16[8,2,64,128]{3,2,1,0:T(8,128)(2,1)S(1)} %get-tuple-e, ...), custom_call_target="tpu_custom_call" | custom-call | flops 2000000000 | bytes 6000000 | tf_op jit(solution)/shard_map/pallas_call | solution.py:352
  14.5 1.5 %collective-permute-done.five_ref = bf16[5,2,64,128]{3,2,1,0:T(8,128)(2,1)S(1)} collective-permute-done((bf16[5,2,64,128]{3,2,1,0:T(8,128)(2,1)S(1)}, bf16[5,2,64,128]{3,2,1,0:T(8,128)(2,1)S(1)}, u32[]{:S(2)}, u32[]{:S(2)}) %collective-permute-start) | collective-permute-done | bytes 163872 | tf_op jit(solution)/shard_map/ppermute | solution.py:351
  16.1 3.2 %shard_map.88 = (bf16[2,64,128]{2,1,0:T(8,128)(2,1)S(1)}, bf16[32,16,128]{2,1,0:T(8,128)(2,1)S(1)}, f32[2,48,320]{2,1,0:T(8,128)S(1)}) custom-call(bf16[8,2,64,128]{3,2,1,0:T(8,128)(2,1)S(1)} %get-tuple-element.19.chip_ref, bf16[5,2,64,128]{3,2,1,0:T(8,128)(2,1)S(1)} %collective-permute-done.five_ref, bf16[2,8,64,256]{3,2,1,0:T(8,128)(2,1)S(1)} %get-tuple-element.21.a_part, ...), custom_call_target="tpu_custom_call" | custom-call | flops 3000000000 | bytes 4300000 | tf_op jit(solution)/shard_map/pallas_call | solution.py:372
  19.3 1.9 %all-gather.1 = bf16[4,64,128]{2,1,0:T(8,128)(2,1)S(1)} all-gather(bf16[2,64,128]{2,1,0:T(8,128)(2,1)S(1)} %get-tuple-element.29), channel_id=3, replica_groups=mesh['y'=8,'x'=4,'z'=8,'c'=2] {'c'}, dimensions={0}, use_global_device_ids=true | all-gather | bytes 98304 | tf_op jit(solution)/shard_map/all_gather | solution.py:389
  21.1 0.4 shard_map.89
  21.5 16.6 %all_to_all.15.got_ref = bf16[32,32,128]{2,1,0:T(8,128)(2,1)S(1)} all-to-all(bf16[32,32,128]{2,1,0:T(8,128)(2,1)S(1)} %shard_map.89), channel_id=1, replica_groups=mesh['y'=8,'x'=4,'z'=8,'c'=2] {'y','x'}, dimensions={0} | all-to-all | bytes 524288 | tf_op jit(solution)/shard_map/all_to_all | solution.py:390
  38.1 0.3 shard_map.90
  38.4 21.6 %all_to_all.16.parts_ref = bf16[16,32,128]{2,1,0:T(8,128)(2,1)S(1)} all-to-all(bf16[16,32,128]{2,1,0:T(8,128)(2,1)S(1)} %shard_map.90), channel_id=1, replica_groups=mesh['y'=8,'x'=4,'z'=8,'c'=2] {'z','c'}, dimensions={0} | all-to-all | bytes 262144 | tf_op jit(solution)/shard_map/all_to_all | solution.py:395
  60.0 0.4 shard_map.91
  60.4 13.2 %all_to_all.17.got_ref = bf16[32,16,128]{2,1,0:T(8,128)(2,1)S(1)} all-to-all(bf16[32,16,128]{2,1,0:T(8,128)(2,1)S(1)} %get-tuple-element.34), channel_id=1, replica_groups=mesh['y'=8,'x'=4,'z'=8,'c'=2] {'y','x'}, dimensions={0} | all-to-all | bytes 262144 | tf_op jit(solution)/shard_map/all_to_all | solution.py:400
  73.6 0.7 shard_map.92
Async XLA Ops:
  9.4 6.6 %collective-permute-start = (bf16[5,2,64,128]{3,2,1,0:T(8,128)(2,1)S(1)}, bf16[5,2,64,128]{3,2,1,0:T(8,128)(2,1)S(1)}, u32[]{:S(2)}, u32[]{:S(2)}) collective-permute-start(bf16[5,2,64,128]{3,2,1,0:T(8,128)(2,1)S(1)} %get-tuple-element.20), channel_id=1, source_target_pairs={{1,2},{2,1},{3,4},{4,3},{5,6},{6,5},{7,8},{8,7},{9,10},{10,9},{11,... | collective-permute-start | bytes 491528 | tf_op jit(solution)/shard_map/ppermute | solution.py:351

commit v10 on v8

--- a/solution.py
+++ b/solution.py
@@ -172,11 +172,13 @@
     for m in range(2):
         for row in (0, 4):
             patches(a_ref, m, row, chip_ref[row : row + 4, m], norm)
-    for fetch in fetches:
+    for fetch in fetches[:3]:
+        fetch.wait()
+    by_channel(values_ref, precision_ref, sides_ref)
+    for fetch in fetches[3:]:
         fetch.wait()
     spread_weights(0, in_ref, out_ref, w1_ref, w2_ref)
     products = [first_of(taps_of(a_ref, m, 0, 6), w1_ref[0]) for m in range(2)]
-    by_channel(values_ref, precision_ref, sides_ref)
     spread_observed(seen_ref, obs_ref)
     cell = jnp.concatenate([cells_ref[r : r + 1, :] for r in range(4)], axis=1)
     pair = lax.shift_right_logical(cell, 1)

time: 74.6 us -> 74.6 us (level)
  transfers between devices with their start and end apart: 1 -> 1, of which waited for: 1 -> 1; matrix products, arithmetic and copies ran while one was open for 0% -> 0% of each run, Pallas kernels for 5% -> 4%
where the time goes in v10:
time: 74.6 us; the launch traced here: 74.3 us
  blocking collectives  62 us (83%)
  Pallas kernels  8.27 us (11%)
  starting transfers between devices  1.92 us (3%)
  waiting for transfers between devices  1.5 us (2%)
    all_to_all x1, blocking collectives, per_device(): parts = lax.all_to_all(parts, TILE, 0, 0, tiled=True)  21.6 us
    all_to_all x1, blocking collectives, per_device(): got = lax.all_to_all(pay, MEM, 0, 0, tiled=True)  16.6 us
    all_to_all x1, blocking collectives, per_device(): back = lax.all_to_all(back, MEM, 0, 0, tiled=True)  13.2 us
    all_gather x1, blocking collectives, per_device(): lax.all_gather(latents, 'c')  8.68 us
    pallas_call x1, Pallas kernels, per_device(): pl.pallas_call(inner_kernel, out_shape=(shaped((2, 8, PAIRS, 256)), shape...  3.2 us
    pallas_call x1, Pallas kernels, per_device(): kernel_call(denoise_kernel, (shaped((2, PAIRS, 128)), shaped((PEERS, 16,...  3.2 us
    ppermute x1, starting transfers between devices, per_device(): five = lax.ppermute(five, TILE, across)  1.92 us
    all_gather x1, blocking collectives, per_device(): lax.all_gather(edge, 'c')  1.86 us
  transfers between devices with their start and end apart: 1, of which 1 were waited for; matrix products, arithmetic and copies ran while one was open for 0% of the time, Pallas kernels for 4%

profile of v10, /device:TPU:1, one launch (start us, length us, event | category | flops | bytes accessed | tf_op | source)
XLA Modules:
  0.0 74.3 jit_solution(12312569540930297840)
XLA Ops:
  0.6 8.7 %all-gather = bf16[4,4,8192]{2,1,0:T(4,128)(2,1)S(1)} all-gather(bf16[2,4,8192]{2,1,0:T(4,128)(2,1)} %param.7), channel_id=2, replica_groups=mesh['y'=8,'x'=4,'z'=8,'c'=2] {'c'}, dimensions={0}, use_global_device_ids=true | all-gather | bytes 393216 | tf_op jit(solution)/shard_map/all_gather | solution.py:348
  9.3 0.1 shard_map.86
  9.4 1.9 %collective-permute-start = (bf16[5,2,64,128]{3,2,1,0:T(8,128)(2,1)S(1)}, bf16[5,2,64,128]{3,2,1,0:T(8,128)(2,1)S(1)}, u32[]{:S(2)}, u32[]{:S(2)}) collective-permute-start(bf16[5,2,64,128]{3,2,1,0:T(8,128)(2,1)S(1)} %get-tuple-element.20), channel_id=1, source_target_pairs={{1,2},{2,1},{3,4},{4,3},{5,6},{6,5},{7,8},{8,7},{9,10},{10,9},{11,... | collective-permute-start | bytes 491528 | tf_op jit(solution)/shard_map/ppermute | solution.py:349
  11.3 3.2 %shard_map.87 = (bf16[2,8,64,256]{3,2,1,0:T(8,128)(2,1)S(1)}, bf16[2,6,64,512]{3,2,1,0:T(8,128)(2,1)S(1)}, bf16[4,2,64,128]{3,2,1,0:T(8,128)(2,1)S(1)}, bf16[2,4...) custom-call(bf16[8,2,64,128]{3,2,1,0:T(8,128)(2,1)S(1)} %get-tuple-e, ...), custom_call_target="tpu_custom_call" | custom-call | flops 2000000000 | bytes 6000000 | tf_op jit(solution)/shard_map/pallas_call | solution.py:350
  14.6 1.5 %collective-permute-done.five_ref = bf16[5,2,64,128]{3,2,1,0:T(8,128)(2,1)S(1)} collective-permute-done((bf16[5,2,64,128]{3,2,1,0:T(8,128)(2,1)S(1)}, bf16[5,2,64,128]{3,2,1,0:T(8,128)(2,1)S(1)}, u32[]{:S(2)}, u32[]{:S(2)}) %collective-permute-start) | collective-permute-done | bytes 163872 | tf_op jit(solution)/shard_map/ppermute | solution.py:349
  16.1 3.2 %shard_map.88 = (bf16[2,64,128]{2,1,0:T(8,128)(2,1)S(1)}, bf16[32,16,128]{2,1,0:T(8,128)(2,1)S(1)}, f32[2,48,320]{2,1,0:T(8,128)S(1)}) custom-call(bf16[8,2,64,128]{3,2,1,0:T(8,128)(2,1)S(1)} %get-tuple-element.19.chip_ref, bf16[5,2,64,128]{3,2,1,0:T(8,128)(2,1)S(1)} %collective-permute-done.five_ref, bf16[2,8,64,256]{3,2,1,0:T(8,128)(2,1)S(1)} %get-tuple-element.21.a_part, ...), custom_call_target="tpu_custom_call" | custom-call | flops 3000000000 | bytes 4300000 | tf_op jit(solution)/shard_map/pallas_call | solution.py:370
  19.3 1.9 %all-gather.1 = bf16[4,64,128]{2,1,0:T(8,128)(2,1)S(1)} all-gather(bf16[2,64,128]{2,1,0:T(8,128)(2,1)S(1)} %get-tuple-element.29), channel_id=3, replica_groups=mesh['y'=8,'x'=4,'z'=8,'c'=2] {'c'}, dimensions={0}, use_global_device_ids=true | all-gather | bytes 98304 | tf_op jit(solution)/shard_map/all_gather | solution.py:387
  21.1 0.4 shard_map.89
  21.5 16.6 %all_to_all.15.got_ref = bf16[32,32,128]{2,1,0:T(8,128)(2,1)S(1)} all-to-all(bf16[32,32,128]{2,1,0:T(8,128)(2,1)S(1)} %shard_map.89), channel_id=1, replica_groups=mesh['y'=8,'x'=4,'z'=8,'c'=2] {'y','x'}, dimensions={0} | all-to-all | bytes 524288 | tf_op jit(solution)/shard_map/all_to_all | solution.py:388
  38.1 0.3 shard_map.90
  38.4 21.6 %all_to_all.16.parts_ref = bf16[16,32,128]{2,1,0:T(8,128)(2,1)S(1)} all-to-all(bf16[16,32,128]{2,1,0:T(8,128)(2,1)S(1)} %shard_map.90), channel_id=1, replica_groups=mesh['y'=8,'x'=4,'z'=8,'c'=2] {'z','c'}, dimensions={0} | all-to-all | bytes 262144 | tf_op jit(solution)/shard_map/all_to_all | solution.py:393
  60.0 0.4 shard_map.91
  60.4 13.2 %all_to_all.17.got_ref = bf16[32,16,128]{2,1,0:T(8,128)(2,1)S(1)} all-to-all(bf16[32,16,128]{2,1,0:T(8,128)(2,1)S(1)} %get-tuple-element.34), channel_id=1, replica_groups=mesh['y'=8,'x'=4,'z'=8,'c'=2] {'y','x'}, dimensions={0} | all-to-all | bytes 262144 | tf_op jit(solution)/shard_map/all_to_all | solution.py:398
  73.6 0.7 shard_map.92
Async XLA Ops:
  9.4 6.6 %collective-permute-start = (bf16[5,2,64,128]{3,2,1,0:T(8,128)(2,1)S(1)}, bf16[5,2,64,128]{3,2,1,0:T(8,128)(2,1)S(1)}, u32[]{:S(2)}, u32[]{:S(2)}) collective-permute-start(bf16[5,2,64,128]{3,2,1,0:T(8,128)(2,1)S(1)} %get-tuple-element.20), channel_id=1, source_target_pairs={{1,2},{2,1},{3,4},{4,3},{5,6},{6,5},{7,8},{8,7},{9,10},{10,9},{11,... | collective-permute-start | bytes 491528 | tf_op jit(solution)/shard_map/ppermute | solution.py:349

commit v11 on v10

--- a/solution.py
+++ b/solution.py
@@ -163,8 +163,8 @@
 def inner_kernel(chip_ref, in_hbm, out_hbm, seen_hbm, cells_hbm, values_hbm, precision_hbm,
                  a_ref, h_ref, x1_ref, a2_ref, h2_ref, w1_ref, w2_ref, obs_ref, pick_ref, sides_ref,
                  in_ref, out_ref, seen_ref, cells_ref, values_ref, precision_ref, sems):
-    sources = (cells_hbm, values_hbm, precision_hbm, seen_hbm, in_hbm, out_hbm)
-    targets = (cells_ref, values_ref, precision_ref, seen_ref, in_ref, out_ref)
+    sources = (in_hbm, out_hbm, cells_hbm, values_hbm, precision_hbm, seen_hbm)
+    targets = (in_ref, out_ref, cells_ref, values_ref, precision_ref, seen_ref)
     fetches = [pltpu.make_async_copy(a, b, sems.at[i]) for i, (a, b) in enumerate(zip(sources, targets))]
     for fetch in fetches:
         fetch.start()
@@ -172,10 +172,10 @@
     for m in range(2):
         for row in (0, 4):
             patches(a_ref, m, row, chip_ref[row : row + 4, m], norm)
-    for fetch in fetches[:3]:
+    for fetch in fetches[2:5]:
         fetch.wait()
     by_channel(values_ref, precision_ref, sides_ref)
-    for fetch in fetches[3:]:
+    for fetch in fetches[:2] + fetches[5:]:
         fetch.wait()
     spread_weights(0, in_ref, out_ref, w1_ref, w2_ref)
     products = [first_of(taps_of(a_ref, m, 0, 6), w1_ref[0]) for m in range(2)]

time: 74.6 us -> 74.6 us (level)
  no operation moved by 1% of the time
where the time goes in v11:
time: 74.6 us; the launch traced here: 74.3 us
  blocking collectives  62 us (83%)
  Pallas kernels  8.23 us (11%)
  starting transfers between devices  1.92 us (3%)
  waiting for transfers between devices  1.55 us (2%)
    all_to_all x1, blocking collectives, per_device(): parts = lax.all_to_all(parts, TILE, 0, 0, tiled=True)  21.7 us
    all_to_all x1, blocking collectives, per_device(): got = lax.all_to_all(pay, MEM, 0, 0, tiled=True)  16.6 us
    all_to_all x1, blocking collectives, per_device(): back = lax.all_to_all(back, MEM, 0, 0, tiled=True)  13.2 us
    all_gather x1, blocking collectives, per_device(): lax.all_gather(latents, 'c')  8.68 us
    pallas_call x1, Pallas kernels, per_device(): kernel_call(denoise_kernel, (shaped((2, PAIRS, 128)), shaped((PEERS, 16,...  3.2 us
    pallas_call x1, Pallas kernels, per_device(): pl.pallas_call(inner_kernel, out_shape=(shaped((2, 8, PAIRS, 256)), shape...  3.15 us
    ppermute x1, starting transfers between devices, per_device(): five = lax.ppermute(five, TILE, across)  1.92 us
    all_gather x1, blocking collectives, per_device(): lax.all_gather(edge, 'c')  1.86 us
  transfers between devices with their start and end apart: 1, of which 1 were waited for; matrix products, arithmetic and copies ran while one was open for 0% of the time, Pallas kernels for 4%

profile of v11, /device:TPU:1, one launch (start us, length us, event | category | flops | bytes accessed | tf_op | source)
XLA Modules:
  0.0 74.3 jit_solution(565498399957223541)
XLA Ops:
  0.6 8.7 %all-gather = bf16[4,4,8192]{2,1,0:T(4,128)(2,1)S(1)} all-gather(bf16[2,4,8192]{2,1,0:T(4,128)(2,1)} %param.7), channel_id=2, replica_groups=mesh['y'=8,'x'=4,'z'=8,'c'=2] {'c'}, dimensions={0}, use_global_device_ids=true | all-gather | bytes 393216 | tf_op jit(solution)/shard_map/all_gather | solution.py:348
  9.3 0.1 shard_map.86
  9.4 1.9 %collective-permute-start = (bf16[5,2,64,128]{3,2,1,0:T(8,128)(2,1)S(1)}, bf16[5,2,64,128]{3,2,1,0:T(8,128)(2,1)S(1)}, u32[]{:S(2)}, u32[]{:S(2)}) collective-permute-start(bf16[5,2,64,128]{3,2,1,0:T(8,128)(2,1)S(1)} %get-tuple-element.20), channel_id=1, source_target_pairs={{1,2},{2,1},{3,4},{4,3},{5,6},{6,5},{7,8},{8,7},{9,10},{10,9},{11,... | collective-permute-start | bytes 491528 | tf_op jit(solution)/shard_map/ppermute | solution.py:349
  11.3 3.2 %shard_map.87 = (bf16[2,8,64,256]{3,2,1,0:T(8,128)(2,1)S(1)}, bf16[2,6,64,512]{3,2,1,0:T(8,128)(2,1)S(1)}, bf16[4,2,64,128]{3,2,1,0:T(8,128)(2,1)S(1)}, bf16[2,4...) custom-call(bf16[8,2,64,128]{3,2,1,0:T(8,128)(2,1)S(1)} %get-tuple-e, ...), custom_call_target="tpu_custom_call" | custom-call | flops 2000000000 | bytes 6000000 | tf_op jit(solution)/shard_map/pallas_call | solution.py:350
  14.5 1.5 %collective-permute-done.five_ref = bf16[5,2,64,128]{3,2,1,0:T(8,128)(2,1)S(1)} collective-permute-done((bf16[5,2,64,128]{3,2,1,0:T(8,128)(2,1)S(1)}, bf16[5,2,64,128]{3,2,1,0:T(8,128)(2,1)S(1)}, u32[]{:S(2)}, u32[]{:S(2)}) %collective-permute-start) | collective-permute-done | bytes 163872 | tf_op jit(solution)/shard_map/ppermute | solution.py:349
  16.1 3.2 %shard_map.88 = (bf16[2,64,128]{2,1,0:T(8,128)(2,1)S(1)}, bf16[32,16,128]{2,1,0:T(8,128)(2,1)S(1)}, f32[2,48,320]{2,1,0:T(8,128)S(1)}) custom-call(bf16[8,2,64,128]{3,2,1,0:T(8,128)(2,1)S(1)} %get-tuple-element.19.chip_ref, bf16[5,2,64,128]{3,2,1,0:T(8,128)(2,1)S(1)} %collective-permute-done.five_ref, bf16[2,8,64,256]{3,2,1,0:T(8,128)(2,1)S(1)} %get-tuple-element.21.a_part, ...), custom_call_target="tpu_custom_call" | custom-call | flops 3000000000 | bytes 4300000 | tf_op jit(solution)/shard_map/pallas_call | solution.py:370
  19.3 1.9 %all-gather.1 = bf16[4,64,128]{2,1,0:T(8,128)(2,1)S(1)} all-gather(bf16[2,64,128]{2,1,0:T(8,128)(2,1)S(1)} %get-tuple-element.29), channel_id=3, replica_groups=mesh['y'=8,'x'=4,'z'=8,'c'=2] {'c'}, dimensions={0}, use_global_device_ids=true | all-gather | bytes 98304 | tf_op jit(solution)/shard_map/all_gather | solution.py:387
  21.1 0.4 shard_map.89
  21.5 16.6 %all_to_all.15.got_ref = bf16[32,32,128]{2,1,0:T(8,128)(2,1)S(1)} all-to-all(bf16[32,32,128]{2,1,0:T(8,128)(2,1)S(1)} %shard_map.89), channel_id=1, replica_groups=mesh['y'=8,'x'=4,'z'=8,'c'=2] {'y','x'}, dimensions={0} | all-to-all | bytes 524288 | tf_op jit(solution)/shard_map/all_to_all | solution.py:388
  38.1 0.3 shard_map.90
  38.4 21.7 %all_to_all.16.parts_ref = bf16[16,32,128]{2,1,0:T(8,128)(2,1)S(1)} all-to-all(bf16[16,32,128]{2,1,0:T(8,128)(2,1)S(1)} %shard_map.90), channel_id=1, replica_groups=mesh['y'=8,'x'=4,'z'=8,'c'=2] {'z','c'}, dimensions={0} | all-to-all | bytes 262144 | tf_op jit(solution)/shard_map/all_to_all | solution.py:393
  60.0 0.4 shard_map.91
  60.4 13.2 %all_to_all.17.got_ref = bf16[32,16,128]{2,1,0:T(8,128)(2,1)S(1)} all-to-all(bf16[32,16,128]{2,1,0:T(8,128)(2,1)S(1)} %get-tuple-element.34), channel_id=1, replica_groups=mesh['y'=8,'x'=4,'z'=8,'c'=2] {'y','x'}, dimensions={0} | all-to-all | bytes 262144 | tf_op jit(solution)/shard_map/all_to_all | solution.py:398
  73.6 0.7 shard_map.92
Async XLA Ops:
  9.4 6.6 %collective-permute-start = (bf16[5,2,64,128]{3,2,1,0:T(8,128)(2,1)S(1)}, bf16[5,2,64,128]{3,2,1,0:T(8,128)(2,1)S(1)}, u32[]{:S(2)}, u32[]{:S(2)}) collective-permute-start(bf16[5,2,64,128]{3,2,1,0:T(8,128)(2,1)S(1)} %get-tuple-element.20), channel_id=1, source_target_pairs={{1,2},{2,1},{3,4},{4,3},{5,6},{6,5},{7,8},{8,7},{9,10},{10,9},{11,... | collective-permute-start | bytes 491528 | tf_op jit(solution)/shard_map/ppermute | solution.py:349
